TPU v7x, 32 devices: a whole 2x2x4 slice. The times are simulated.
32 devices in a mesh: dp: 2 (over x), seq: 4 (over y, core), mp: 4 (over z).
Axes of the slice: x: 2, y: 2, z: 4, core: 2. Of those that a mesh axis runs over, the one named last changes fastest.
Arguments:
- incoming_embeddings: bfloat16 [4, 4, 1024, 512], P(None, 'seq', 'dp'), may hold values from -6 to 6
- output_sensitivity: bfloat16 [4, 4, 1024, 512], P(None, 'seq', 'dp'), may hold values from -6 to 6
- sequence_extents: int32 [4], replicated, may hold values from 512 to 4096, as said below
- asking_projector: bfloat16 [512, 512], P(('dp', 'seq'), 'mp'), may hold values from -0.375 to 0.375
- lookup_projector: bfloat16 [512, 512], P(('dp', 'seq'), 'mp'), may hold values from -0.375 to 0.375
- content_projector: bfloat16 [512, 512], P(('dp', 'seq'), 'mp'), may hold values from -0.25 to 0.25
- attention_combiner: bfloat16 [512, 512], P('mp', ('dp', 'seq')), may hold values from -1.5 to 1.5
- feedforward_expand: bfloat16 [512, 2048], P(('dp', 'seq'), 'mp'), may hold values from -0.25 to 0.25
- feedforward_contract: bfloat16 [2048, 512], P('mp', ('dp', 'seq')), may hold values from -0.125 to 0.125
- attention_norm_scale: bfloat16 [512], P(('dp', 'seq')), may hold values from 0.5 to 1.5
- attention_norm_bias: bfloat16 [512], P(('dp', 'seq')), may hold values from -1.5 to 1.5
- feedforward_norm_scale: bfloat16 [512], P(('dp', 'seq')), may hold values from 0.5 to 1.5
- feedforward_norm_bias: bfloat16 [512], P(('dp', 'seq')), may hold values from -1.5 to 1.5
Outputs:
- output: bfloat16 [4, 4, 1024, 512], P(None, 'seq', ('dp', 'mp'))
- token_grad: bfloat16 [4, 4, 1024, 512], P(None, 'seq', ('dp', 'mp'))
- query_grad: float32 [512, 512], P(('dp', 'seq'), 'mp')
- key_grad: float32 [512, 512], P(('dp', 'seq'), 'mp')
- value_grad: float32 [512, 512], P(('dp', 'seq'), 'mp')
- merge_grad: float32 [512, 512], P('mp', ('dp', 'seq'))
- up_grad: float32 [512, 2048], P(('dp', 'seq'), 'mp')
- down_grad: float32 [2048, 512], P('mp', ('dp', 'seq'))
- pregain_grad: float32 [512], P(('dp', 'seq'))
- preshift_grad: float32 [512], P(('dp', 'seq'))
- midgain_grad: float32 [512], P(('dp', 'seq'))
- midshift_grad: float32 [512], P(('dp', 'seq'))
Inputs may be any that keep to these rules, and one draw needn't show every extreme that they name: `sequence_extents`: valid tokens of each sequence in input order; one sequence has exactly 4096 and one exactly 512.
All inputs are finite; a program needn't handle non-finite values.
Results may differ from a plain program's by a relative error of at most 0.015.
Values may be sent and summed in bfloat16 or wider, within the bound.
A program may use at most 256 MiB of HBM per device.

v0:
```python
import jax
import jax.numpy as jnp
from jax import lax
from jax.sharding import PartitionSpec as P

HD = 64
NR = 16


def cut_along(x, dim, count):
    before, after = (x.shape[:dim], x.shape[dim + 1 :])
    return jnp.moveaxis(x.reshape(*before, count, -1, *after), dim, 0)


def summed_on_arrival(x, axis, dim):
    count = lax.axis_size(axis)
    blocks = lax.all_to_all(cut_along(x, dim, count), axis, 0, 0, tiled=True)
    return jnp.sum(blocks.astype(jnp.float32), axis=0)


def sent_together(arrays, axis, dim, along):
    ends, at = ([], 0)
    for a in arrays[:-1]:
        at += a.shape[along]
        ends.append(at)
    both = jnp.concatenate(arrays, axis=along)
    return tuple(jnp.split(summed_on_arrival(both, axis, dim), ends, axis=along))


def norm_rows(values, gain_row, shift_row):
    center = values - jnp.mean(values, axis=-1, keepdims=True)
    spread = jnp.mean(center * center, axis=-1, keepdims=True)
    return center * lax.rsqrt(spread + 1e-05) * gain_row + shift_row


def norm_gain_parts(values, grad_rows):
    center = values - jnp.mean(values, axis=-1, keepdims=True)
    spread = jnp.mean(center * center, axis=-1, keepdims=True)
    scaled = center * lax.rsqrt(spread + 1e-05)
    return (jnp.sum(grad_rows * scaled, axis=0), jnp.sum(grad_rows, axis=0))


def gelu_exact(values):
    return jax.nn.gelu(values, approximate=False)


def dot_plain(left_mat, right_mat):
    return jnp.dot(left_mat, right_mat, preferred_element_type=jnp.float32)


def dot_inner(left_mat, right_mat):
    return lax.dot_general(
        left_mat, right_mat, (((0,), (0,)), ((), ())), preferred_element_type=jnp.float32
    )


def dot_outer(left_mat, right_mat):
    return lax.dot_general(
        left_mat, right_mat, (((1,), (1,)), ((), ())), preferred_element_type=jnp.float32
    )


def group_sum(values, group_width):
    return jnp.sum(
        values.reshape((values.shape[0] // group_width, group_width) + values.shape[1:]), axis=1
    )


def block_shape(coarse_rows):
    query_len = min(coarse_rows, 512)
    span_len = query_len + 2 * NR
    window_len = -(-span_len // 128) * 128
    return (query_len, span_len, window_len)


def window_mask(level_at, first_row, query_len, window_len, span_len):
    rows_at = first_row + jnp.arange(query_len, dtype=jnp.int32)[:, None]
    keys_at = first_row + jnp.arange(window_len, dtype=jnp.int32)[None, :]
    inside = keys_at - first_row < span_len
    allowed = jnp.abs(rows_at // NR + 1 - keys_at // NR) <= 1
    if level_at > 0:
        half_block = NR // 2
        allowed = allowed & (jnp.abs(rows_at // half_block + 2 - keys_at // half_block) >= 2)
    return (allowed & inside).astype(jnp.float32)


def level_forward(query_rows, pair_wide, count_wide, level_at):
    coarse_rows = query_rows.shape[0]
    columns = query_rows.shape[1]
    heads_here = columns // HD
    query_len, span_len, window_len = block_shape(coarse_rows)
    tail_pad = window_len - span_len
    pair_padded = jnp.pad(pair_wide, ((0, tail_pad), (0, 0)))
    count_padded = jnp.pad(count_wide, (0, tail_pad))
    weight_list = []
    total_parts = []
    numer_parts = []
    for block_at in range(coarse_rows // query_len):
        first_row = block_at * query_len
        query_block = query_rows[first_row : first_row + query_len]
        pair_block = pair_padded[first_row : first_row + window_len]
        count_block = count_padded[first_row : first_row + window_len]
        keep_mask = (
            window_mask(level_at, first_row, query_len, window_len, span_len) * count_block[None, :]
        )
        head_weights = []
        head_totals = []
        head_numers = []
        for head_at in range(heads_here):
            head_cols = slice(head_at * HD, (head_at + 1) * HD)
            value_cols = slice(columns + head_at * HD, columns + (head_at + 1) * HD)
            scores = dot_outer(query_block[:, head_cols], pair_block[:, head_cols]) * HD ** (-0.5)
            weight = jnp.exp(scores) * keep_mask
            head_weights.append(weight)
            head_totals.append(jnp.sum(weight, axis=-1))
            head_numers.append(dot_plain(weight.astype(jnp.bfloat16), pair_block[:, value_cols]))
        weight_list.append(head_weights)
        total_parts.append(jnp.stack(head_totals, axis=1))
        numer_parts.append(jnp.concatenate(head_numers, axis=1))
    totals = jnp.concatenate(total_parts, axis=0)
    numer_part = jnp.concatenate(numer_parts, axis=0).reshape(coarse_rows, heads_here, HD)
    return ((query_rows, pair_padded, weight_list), totals, numer_part)


def level_backward(level_kept, numer_rows, total_rows):
    query_rows, pair_padded, weight_list = level_kept
    coarse_rows = query_rows.shape[0]
    columns = query_rows.shape[1]
    heads_here = columns // HD
    query_len, span_len, window_len = block_shape(coarse_rows)
    numer_flat = numer_rows.reshape(coarse_rows, columns)
    pair_grad = jnp.zeros(pair_padded.shape, jnp.float32)
    query_parts = []
    for block_at in range(coarse_rows // query_len):
        first_row = block_at * query_len
        query_block = query_rows[first_row : first_row + query_len]
        pair_block = pair_padded[first_row : first_row + window_len]
        numer_block = numer_flat[first_row : first_row + query_len]
        total_block = total_rows[first_row : first_row + query_len]
        query_heads = []
        key_heads = []
        value_heads = []
        for head_at in range(heads_here):
            head_cols = slice(head_at * HD, (head_at + 1) * HD)
            value_cols = slice(columns + head_at * HD, columns + (head_at + 1) * HD)
            weight = head_weights = weight_list[block_at][head_at]
            grad_here = numer_block[:, head_cols]
            score_grad = (
                (dot_outer(grad_here, pair_block[:, value_cols]) + total_block[:, head_at][:, None])
                * weight
            ).astype(jnp.bfloat16)
            query_heads.append(dot_plain(score_grad, pair_block[:, head_cols]) * HD ** (-0.5))
            key_heads.append(dot_inner(score_grad, query_block[:, head_cols]) * HD ** (-0.5))
            value_heads.append(dot_inner(head_weights.astype(jnp.bfloat16), grad_here))
        query_parts.append(jnp.concatenate(query_heads, axis=1))
        block_grad = jnp.concatenate(key_heads + value_heads, axis=1)
        pair_grad = pair_grad + jnp.pad(
            block_grad, ((first_row, pair_padded.shape[0] - first_row - window_len), (0, 0))
        )
    query_grad = jnp.concatenate(query_parts, axis=0)
    return (query_grad, pair_grad[: coarse_rows + 2 * NR])


def body(
    incoming_embeddings,
    output_sensitivity,
    sequence_extents,
    asking_projector,
    lookup_projector,
    content_projector,
    attention_combiner,
    feedforward_expand,
    feedforward_contract,
    attention_norm_scale,
    attention_norm_bias,
    feedforward_norm_scale,
    feedforward_norm_bias,
):
    groups = lax.axis_size("dp")
    slices = lax.axis_size("seq")
    models = lax.axis_size("mp")
    group_id = lax.axis_index("dp")
    slice_id = lax.axis_index("seq")
    model_id = lax.axis_index("mp")
    seq_count = incoming_embeddings.shape[0]
    piece_len = incoming_embeddings.shape[2]
    model_width = incoming_embeddings.shape[3]
    part_len = piece_len * groups
    batches = seq_count // groups
    share_len = piece_len // models
    share_rows = groups * share_len
    local_top = (part_len // NR).bit_length() - 1
    upper_start = local_top + 1
    level_top = (part_len * slices // (2 * NR)).bit_length() - 1
    upper_rows = NR // 2
    upper_whole = upper_rows * slices
    seq_ids = jnp.arange(seq_count, dtype=jnp.int32)
    inverse = jnp.sum(jnp.where(seq_ids[:, None] == seq_ids[None, :], seq_ids[:, None], 0), axis=0)
    send_tok = jnp.take(incoming_embeddings, seq_ids, axis=0).reshape(
        groups, batches, piece_len, model_width
    )
    send_cot = jnp.take(output_sensitivity, seq_ids, axis=0).reshape(
        groups, batches, piece_len, model_width
    )
    dealt_tok, dealt_cot = (
        lax.all_to_all(send_tok, "dp", split_axis=0, concat_axis=2, tiled=True),
        lax.all_to_all(send_cot, "dp", split_axis=0, concat_axis=2, tiled=True),
    )
    dealt_tok = dealt_tok.reshape(batches, part_len, model_width)
    dealt_cot = dealt_cot.reshape(batches, part_len, model_width)
    my_lengths = jnp.take(
        sequence_extents, lax.dynamic_slice_in_dim(seq_ids, group_id * batches, batches, 0)
    )

    def split_rows(rows):
        return rows.reshape((groups, models, share_len) + rows.shape[1:])

    def take_share(rows):
        return lax.dynamic_slice_in_dim(split_rows(rows), model_id, 1, 1).reshape(
            (share_rows,) + rows.shape[1:]
        )

    def neighbour_rims(gathered):
        padded = jnp.pad(gathered, ((2 * NR, 2 * NR), (0, 0)))
        from_left = lax.dynamic_slice_in_dim(padded, slice_id * 2 * NR + NR, NR, 0)
        from_right = lax.dynamic_slice_in_dim(padded, (slice_id + 2) * 2 * NR, NR, 0)
        return (from_left, from_right)

    def one_batch(batch_index, learnable_collection):
        full_query, full_key, full_value, full_merge, full_up, full_down = learnable_collection[:6]
        gain_pre, shift_pre, gain_mid, shift_mid = (
            learnable_tensor.astype(jnp.float32) for learnable_tensor in learnable_collection[6:]
        )
        columns = full_query.shape[1]
        heads_here = columns // HD
        length_now = my_lengths[batch_index]

        def level_counts(level_at, first_id, id_total):
            coarse_ids = first_id + jnp.arange(id_total, dtype=jnp.int32)
            group_len = 2**level_at
            return jnp.where(
                coarse_ids >= 0, jnp.clip(length_now - group_len * coarse_ids, 0, group_len), 0
            ).astype(jnp.float32)

        positions = slice_id * part_len + jnp.arange(part_len, dtype=jnp.int32)
        valid_rows = (positions < length_now).astype(jnp.float32)
        inputs = dealt_tok[batch_index].astype(jnp.float32)
        grad_in = dealt_cot[batch_index].astype(jnp.float32) * valid_rows[:, None]
        valid_share = take_share(valid_rows)
        normed, pull_pre = jax.vjp(norm_rows, inputs, gain_pre, shift_pre)
        normed_low = normed.astype(jnp.bfloat16)
        queries = dot_plain(normed_low, full_query).astype(jnp.bfloat16)
        keys_own = dot_plain(normed_low, full_key).astype(jnp.bfloat16)
        values_own = dot_plain(normed_low, full_value).astype(jnp.bfloat16)
        pair_own = jnp.concatenate([keys_own, values_own], axis=1)
        fine_all = (
            jnp.concatenate([queries, pair_own], axis=1).astype(jnp.float32) * valid_rows[:, None]
        )
        level_sums = [fine_all]
        for level_at in range(1, upper_start + 1):
            level_sums.append(group_sum(level_sums[-1], 2))
        query_levels = [queries]
        pair_levels = [pair_own]
        own_counts = [valid_rows]
        for level_at in range(1, local_top + 1):
            coarse_rows = part_len >> level_at
            counts_here = level_counts(level_at, slice_id * coarse_rows, coarse_rows)
            coarse_means = (level_sums[level_at] / jnp.maximum(counts_here, 1.0)[:, None]).astype(
                jnp.bfloat16
            )
            query_levels.append(coarse_means[:, :columns])
            pair_levels.append(coarse_means[:, columns:])
            own_counts.append(counts_here)
        edge_rows = jnp.concatenate(
            [
                jnp.concatenate([pair_rows[:NR], pair_rows[-NR:]], axis=0)
                for pair_rows in pair_levels
            ],
            axis=1,
        )
        edges_all, upper_all = (
            lax.all_gather(
                edge_rows.astype(jnp.float32).astype(jnp.bfloat16), "seq", axis=0, tiled=True
            ).astype(jnp.float32),
            lax.all_gather(
                level_sums[upper_start].astype(jnp.bfloat16), "seq", axis=0, tiled=True
            ).astype(jnp.float32),
        )
        left_edge, right_edge = neighbour_rims(edges_all)
        left_edge = left_edge.astype(jnp.bfloat16)
        right_edge = right_edge.astype(jnp.bfloat16)
        kept_levels = []
        total_all = jnp.zeros((part_len, heads_here), jnp.float32)
        numer_all = jnp.zeros((part_len, heads_here, HD), jnp.float32)
        for level_at in range(local_top + 1):
            coarse_rows = part_len >> level_at
            col_range = slice(level_at * 2 * columns, (level_at + 1) * 2 * columns)
            pair_wide = jnp.concatenate(
                [left_edge[:, col_range], pair_levels[level_at], right_edge[:, col_range]], axis=0
            )
            count_wide = level_counts(level_at, slice_id * coarse_rows - NR, coarse_rows + 2 * NR)
            level_kept, totals, numer_part = level_forward(
                query_levels[level_at], pair_wide, count_wide, level_at
            )
            kept_levels.append(level_kept)
            total_all = total_all + jnp.repeat(totals, 2**level_at, axis=0)
            numer_all = numer_all + jnp.repeat(numer_part, 2**level_at, axis=0)
        level_at = 7
        repeat_by = 2 ** (level_at - upper_start)
        coarse_rows = upper_whole // repeat_by
        counts_here = level_counts(level_at, 0, coarse_rows)
        coarse_means = (
            group_sum(upper_all, repeat_by) / jnp.maximum(counts_here, 1.0)[:, None]
        ).astype(jnp.bfloat16)
        pair_wide = jnp.pad(coarse_means[:, columns:], ((NR, NR), (0, 0)))
        count_wide = level_counts(level_at, -NR, coarse_rows + 2 * NR)
        level_kept, totals, numer_part = level_forward(
            coarse_means[:, :columns], pair_wide, count_wide, level_at
        )
        upper_kept = [level_kept]
        upper_counts = [counts_here]
        upper_total = jnp.repeat(totals, repeat_by, axis=0)
        upper_numer = jnp.repeat(numer_part, repeat_by, axis=0)
        total_all = total_all + jnp.repeat(
            lax.dynamic_slice_in_dim(upper_total, slice_id * upper_rows, upper_rows, 0),
            2**upper_start,
            axis=0,
        )
        numer_all = numer_all + jnp.repeat(
            lax.dynamic_slice_in_dim(upper_numer, slice_id * upper_rows, upper_rows, 0),
            2**upper_start,
            axis=0,
        )
        attended = (
            (numer_all / total_all[:, :, None]).reshape(part_len, columns).astype(jnp.bfloat16)
        )
        merged_part = dot_plain(attended, full_merge)
        branch_attn = lax.psum(merged_part, "mp")
        after_attn = inputs + branch_attn
        mid_normed, pull_mid = jax.vjp(norm_rows, after_attn, gain_mid, shift_mid)
        mid_low = mid_normed.astype(jnp.bfloat16)
        after_share = take_share(after_attn)
        up_proj = dot_plain(mid_low, full_up)
        activated, pull_gelu = jax.vjp(gelu_exact, up_proj)
        act_low = activated.astype(jnp.bfloat16)
        ffn_share = (
            lax.psum_scatter(
                split_rows(dot_plain(act_low, full_down)).astype(jnp.bfloat16),
                "mp",
                scatter_dimension=1,
                tiled=True,
            )
            .astype(jnp.float32)
            .reshape(share_rows, model_width)
        )
        result_share = (valid_share[:, None] * (after_share + ffn_share)).astype(jnp.bfloat16)
        grad_low = grad_in.astype(jnp.bfloat16)
        act_grad = dot_outer(grad_low, full_down)
        down_acc = dot_inner(act_low, grad_low)
        hidden_grad = pull_gelu(act_grad)[0].astype(jnp.bfloat16)
        up_acc = dot_inner(mid_low, hidden_grad)
        mid_part = dot_outer(hidden_grad, full_up)
        mid_grad = lax.psum(mid_part, "mp")
        back_mid = pull_mid(mid_grad)[0]
        residual_grad = grad_in + back_mid
        branch_grad = residual_grad.astype(jnp.bfloat16)
        residual_share = take_share(residual_grad)
        gain_mid_part, shift_mid_part = norm_gain_parts(after_share, take_share(mid_grad))
        merge_acc = dot_inner(attended, branch_grad)
        attended_grad = dot_outer(branch_grad, full_merge).reshape(part_len, heads_here, HD)
        numer_grad = (attended_grad / total_all[:, :, None]).astype(jnp.bfloat16)
        total_grad = -jnp.sum(attended_grad * numer_all, axis=-1) / (total_all * total_all)
        numer_wide = numer_grad.astype(jnp.float32)
        rim_parts = []
        own_pair_grads = []
        query_coarse = []
        for level_at in range(local_top + 1):
            coarse_rows = part_len >> level_at
            if level_at == 0:
                numer_sum = numer_grad
                total_sum = total_grad
            else:
                numer_sum = group_sum(numer_wide, 2**level_at).astype(jnp.bfloat16)
                total_sum = group_sum(total_grad, 2**level_at)
            query_grad, pair_grad = level_backward(kept_levels[level_at], numer_sum, total_sum)
            rim_parts.append(
                jnp.concatenate([pair_grad[:NR], pair_grad[NR + coarse_rows :]], axis=0)
            )
            own_pair_grads.append(pair_grad[NR : NR + coarse_rows])
            query_coarse.append(query_grad)
        rim_grads = jnp.concatenate(rim_parts, axis=1)
        upper_numer_grad = group_sum(numer_wide, 2**upper_start).reshape(upper_rows, columns)
        upper_total_grad = group_sum(total_grad, 2**upper_start)
        rims_all, numer_sums, total_sums = (
            lax.all_gather(rim_grads.astype(jnp.bfloat16), "seq", axis=0, tiled=True).astype(
                rim_grads.dtype
            ),
            lax.all_gather(upper_numer_grad.astype(jnp.bfloat16), "seq", axis=0, tiled=True).astype(
                upper_numer_grad.dtype
            ),
            lax.all_gather(upper_total_grad.astype(jnp.bfloat16), "seq", axis=0, tiled=True).astype(
                upper_total_grad.dtype
            ),
        )
        from_left, from_right = neighbour_rims(rims_all)
        fine_grad = jnp.zeros((part_len, 3 * columns), jnp.float32)
        for level_at in range(local_top + 1):
            coarse_rows = part_len >> level_at
            col_range = slice(level_at * 2 * columns, (level_at + 1) * 2 * columns)
            pair_here = (
                own_pair_grads[level_at]
                + jnp.pad(from_left[:, col_range], ((0, coarse_rows - NR), (0, 0)))
                + jnp.pad(from_right[:, col_range], ((coarse_rows - NR, 0), (0, 0)))
            )
            coarse_grad = jnp.concatenate([query_coarse[level_at], pair_here], axis=1)
            if level_at == 0:
                fine_grad = coarse_grad
            else:
                coarse_grad = coarse_grad / jnp.maximum(own_counts[level_at], 1.0)[:, None]
                fine_grad = (
                    fine_grad + jnp.repeat(coarse_grad, 2**level_at, axis=0) * valid_rows[:, None]
                )
        upper_grad = jnp.zeros((upper_whole, 3 * columns), jnp.float32)
        for index_at, level_at in enumerate(range(upper_start, level_top + 1)):
            repeat_by = 2 ** (level_at - upper_start)
            coarse_rows = upper_whole // repeat_by
            numer_sum = (
                group_sum(numer_sums, repeat_by)
                .reshape(coarse_rows, heads_here, HD)
                .astype(jnp.bfloat16)
            )
            total_sum = group_sum(total_sums, repeat_by)
            query_grad, pair_grad = level_backward(upper_kept[index_at], numer_sum, total_sum)
            coarse_grad = (
                jnp.concatenate([query_grad, pair_grad[NR : NR + coarse_rows]], axis=1)
                / jnp.maximum(upper_counts[index_at], 1.0)[:, None]
            )
            upper_grad = jnp.repeat(coarse_grad, repeat_by, axis=0)
        own_upper = lax.dynamic_slice_in_dim(upper_grad, slice_id * upper_rows, upper_rows, 0)
        fine_grad = fine_grad + jnp.repeat(own_upper, 2**upper_start, axis=0) * valid_rows[:, None]
        rows_grad = fine_grad.astype(jnp.bfloat16)
        query_rows_grad = rows_grad[:, :columns]
        key_rows_grad = rows_grad[:, columns : 2 * columns]
        value_rows_grad = rows_grad[:, 2 * columns :]
        query_acc = dot_inner(normed_low, query_rows_grad)
        key_acc = dot_inner(normed_low, key_rows_grad)
        value_acc = dot_inner(normed_low, value_rows_grad)
        normed_part = (
            dot_outer(query_rows_grad, full_query)
            + dot_outer(key_rows_grad, full_key)
            + dot_outer(value_rows_grad, full_value)
        )
        normed_grad, gain_mid_sum, shift_mid_sum = (
            lax.psum(normed_part.astype(jnp.bfloat16), "mp").astype(jnp.float32),
            lax.psum(gain_mid_part.astype(jnp.bfloat16), "mp").astype(jnp.float32),
            lax.psum(shift_mid_part.astype(jnp.bfloat16), "mp").astype(jnp.float32),
        )
        back_pre, gain_pre_acc, shift_pre_acc = pull_pre(normed_grad)
        input_share = (residual_share + take_share(back_pre)).astype(jnp.bfloat16)
        grad_terms = (
            query_acc,
            key_acc,
            value_acc,
            merge_acc,
            up_acc,
            down_acc,
            gain_pre_acc,
            shift_pre_acc,
            gain_mid_sum,
            shift_mid_sum,
        )
        return (result_share, input_share, grad_terms)

    result_list = []
    grad_list = []
    running_sum = None
    for batch_index in range(batches):
        learnable_collection = (
            lax.all_gather(asking_projector, ("dp", "seq"), axis=0, tiled=True),
            lax.all_gather(lookup_projector, ("dp", "seq"), axis=0, tiled=True),
            lax.all_gather(content_projector, ("dp", "seq"), axis=0, tiled=True),
            lax.all_gather(attention_combiner, ("dp", "seq"), axis=1, tiled=True),
            lax.all_gather(feedforward_expand, ("dp", "seq"), axis=0, tiled=True),
            lax.all_gather(feedforward_contract, ("dp", "seq"), axis=1, tiled=True),
            lax.all_gather(attention_norm_scale, ("dp", "seq"), axis=0, tiled=True),
            lax.all_gather(attention_norm_bias, ("dp", "seq"), axis=0, tiled=True),
            lax.all_gather(feedforward_norm_scale, ("dp", "seq"), axis=0, tiled=True),
            lax.all_gather(feedforward_norm_bias, ("dp", "seq"), axis=0, tiled=True),
        )
        result_share, input_share, grad_terms = one_batch(batch_index, learnable_collection)
        result_list.append(result_share)
        grad_list.append(input_share)
        if running_sum is None:
            running_sum = grad_terms
        else:
            running_sum = tuple(
                (older_sum + newer_sum for older_sum, newer_sum in zip(running_sum, grad_terms))
            )
    owned_grads = (
        *sent_together(
            (
                running_sum[0].astype(jnp.bfloat16),
                running_sum[1].astype(jnp.bfloat16),
                running_sum[2].astype(jnp.bfloat16),
            ),
            ("dp", "seq"),
            0,
            1,
        ),
        summed_on_arrival(running_sum[3].astype(jnp.bfloat16), ("dp", "seq"), 1),
        summed_on_arrival(running_sum[4].astype(jnp.bfloat16), ("dp", "seq"), 0),
        summed_on_arrival(running_sum[5].astype(jnp.bfloat16), ("dp", "seq"), 1),
        summed_on_arrival(running_sum[6].astype(jnp.bfloat16), ("dp", "seq"), 0),
        summed_on_arrival(running_sum[7].astype(jnp.bfloat16), ("dp", "seq"), 0),
        summed_on_arrival(running_sum[8].astype(jnp.bfloat16), ("dp", "seq"), 0),
        summed_on_arrival(running_sum[9].astype(jnp.bfloat16), ("dp", "seq"), 0),
    )
    result_all = jnp.stack(result_list, axis=0).reshape(batches, groups, share_len, model_width)
    grad_all = jnp.stack(grad_list, axis=0).reshape(batches, groups, share_len, model_width)
    back_out, back_grad = (
        lax.all_to_all(result_all, "dp", split_axis=1, concat_axis=0, tiled=True),
        lax.all_to_all(grad_all, "dp", split_axis=1, concat_axis=0, tiled=True),
    )
    back_out = jnp.take(back_out, inverse, axis=0)
    back_grad = jnp.take(back_grad, inverse, axis=0)
    return (
        back_out,
        back_grad,
        owned_grads[0],
        owned_grads[1],
        owned_grads[2],
        owned_grads[3],
        owned_grads[4],
        owned_grads[5],
        owned_grads[6],
        owned_grads[7],
        owned_grads[8],
        owned_grads[9],
    )


def solution(mesh):
    in_specs = (
        P(None, "seq", "dp", None),
        P(None, "seq", "dp", None),
        P(),
        P(("dp", "seq"), "mp"),
        P(("dp", "seq"), "mp"),
        P(("dp", "seq"), "mp"),
        P("mp", ("dp", "seq")),
        P(("dp", "seq"), "mp"),
        P("mp", ("dp", "seq")),
        P(("dp", "seq")),
        P(("dp", "seq")),
        P(("dp", "seq")),
        P(("dp", "seq")),
    )
    out_specs = (
        P(None, "seq", ("dp", "mp"), None),
        P(None, "seq", ("dp", "mp"), None),
        P(("dp", "seq"), "mp"),
        P(("dp", "seq"), "mp"),
        P(("dp", "seq"), "mp"),
        P("mp", ("dp", "seq")),
        P(("dp", "seq"), "mp"),
        P("mp", ("dp", "seq")),
        P(("dp", "seq")),
        P(("dp", "seq")),
        P(("dp", "seq")),
        P(("dp", "seq")),
    )
    return jax.shard_map(body, mesh=mesh, in_specs=in_specs, out_specs=out_specs, check_vma=False)
```

profile of v0, /device:TPU:0, one launch (start us, length us, event | category | flops | bytes accessed | tf_op | source)
XLA Modules:
  0.0 1504.0 jit_solution(3274863624410577909)
XLA Ops:
  10.8 3.7 gather_fusion.3
  14.6 4.0 bitcast_select_fusion.1
  18.7 4.3 all-to-all-start
  47.3 10.3 all_gather.72
  57.6 9.7 all_gather.73
  76.4 8.0 all_gather.74
  86.7 13.8 all-reduce.72
  110.0 10.5 all_gather.77
  154.9 7.4 all_gather.75
  196.3 5.5 all_gather.76
  231.4 5.1 multiply_reduce_fusion.4
  285.2 20.6 %all_gather.82 = bf16[128,1792]{1,0:T(8,128)(2,1)} all-gather(bf16[32,1792]{1,0:T(8,128)(2,1)} %constant_dynamic-update-slice_fusion.7), channel_id=1, replica_groups=mesh['dp'=2,'seq'=4,'mp'=4] {'seq'}, dimensions={0}, use_global_device_ids=true | all-gather | bytes 573440 | tf_op jit(solution)/shard_map/all_gather | solution.py:282
  340.7 5.2 all_gather.83
  492.7 4.8 all-to-all-start.2
  501.9 27.2 %all_gather.80 = bf16[512,512]{1,0:T(8,128)(2,1)} all-gather(bf16[64,512]{1,0:T(8,128)(2,1)} %param.24), channel_id=1, replica_groups=mesh['dp'=2,'seq'=4,'mp'=4] {'dp','seq'}, dimensions={0}, use_global_device_ids=true | all-gather | bytes 589824 | tf_op jit(solution)/shard_map/all_gather | solution.py:483
  529.1 10.8 all_gather.81
  545.1 103.4 %all-reduce.81.cloned.1.call-done = (f32[1024,512]{1,0:T(8,128)}, f32[1024,512]{1,0:T(8,128)}) async-done(((f32[1024,512]{1,0:T(8,128)}, f32[1024,512]{1,0:T(8,128)}), (f32[1024,512]{1,0:T(8,128)}, f32[1024,512]{1,0:T(8,128)})) %all-reduce.81.cloned.1.call-update) | async-done | bytes 4194320 | tf_op jit(solution)/shard_map/psum | solution.py:338
  656.7 5.8 add_convert_fusion.3
  666.0 7.7 add_convert_fusion.1
  787.1 4.3 all-to-all-start.7
  800.2 4.1 all-to-all-start.6
  809.5 67.3 %all-reduce.79.cloned.1.call-done = (f32[1024,512]{1,0:T(8,128)}, f32[1024,512]{1,0:T(8,128)}) async-done(((f32[1024,512]{1,0:T(8,128)}, f32[1024,512]{1,0:T(8,128)}), (f32[1024,512]{1,0:T(8,128)}, f32[1024,512]{1,0:T(8,128)})) %all-reduce.79.cloned.1.call-update) | async-done | bytes 4194320 | tf_op jit(solution)/shard_map/psum | solution.py:363
  876.9 3.9 multiply_reduce_fusion.1
  893.2 3.8 fusion.251
  897.0 4.9 copy.1223
  903.5 4.7 fusion.255
  970.5 3.9 fusion.257
  1008.7 5.4 all_gather.85
  1015.8 5.0 all-gather
  1034.2 7.3 all_gather.84
  1105.1 4.6 fusion.41
  1121.6 4.2 fusion.252
  1125.8 4.9 copy.1275
  1132.4 4.7 fusion.256
  1181.2 3.8 fusion.260
  1198.0 3.9 fusion.258
  1244.2 5.2 all_gather.88
  1252.5 5.0 all-gather.1
  1279.9 7.3 all_gather.87
  1355.3 4.6 fusion.39
  1371.1 10.4 all-reduce.73
  1387.4 4.6 all-to-all-start.1
  1393.3 5.5 all-to-all-done.1
  1402.9 3.8 all-to-all-done.11
  1418.9 4.1 all-to-all-done.5
  1433.9 23.5 %all-reduce.83.cloned.1.call-done = (bf16[1024,512]{1,0:T(8,128)(2,1)}, bf16[1024,512]{1,0:T(8,128)(2,1)}) async-done(((bf16[1024,512]{1,0:T(8,128)(2,1)}, bf16[1024,512]{1,0:T(8,128)(2,1)}), (bf16[1024,512]{1,0:T(8,128)(2,1)}, bf16[1024,512]{1,0:T(8,128)(2,1)})) %all-reduce.83.cloned.1.call-update) | async-done | bytes 2097168 | tf_op jit(solution)/shard_map/psum | solution.py:454
  1473.0 4.2 all-to-all-start.8
  1487.0 6.5 all-to-all-done.3
  (2494 shorter events, 987.8 us)
Async XLA Ops:
  18.6 28.7 %copy-start.498 = (bf16[64,128]{1,0:T(8,128)(2,1)S(1)}, bf16[64,128]{1,0:T(8,128)(2,1)}, u32[]{:S(2)}) copy-start(bf16[64,128]{1,0:T(8,128)(2,1)} %param.20) | copy-start | bytes 49156
  18.6 39.0 %copy-start.499 = (bf16[64,128]{1,0:T(8,128)(2,1)S(1)}, bf16[64,128]{1,0:T(8,128)(2,1)}, u32[]{:S(2)}) copy-start(bf16[64,128]{1,0:T(8,128)(2,1)} %param.21) | copy-start | bytes 49156
  18.6 57.8 %copy-start.500 = (bf16[64,128]{1,0:T(8,128)(2,1)S(1)}, bf16[64,128]{1,0:T(8,128)(2,1)}, u32[]{:S(2)}) copy-start(bf16[64,128]{1,0:T(8,128)(2,1)} %param.22) | copy-start | bytes 49156
  18.6 65.8 %copy-start.654 = (u32[32]{0:T(128)S(1)}, u32[32]{0:T(128)}, u32[]{:S(2)}) copy-start(u32[32]{0:T(128)} %constant.745) | copy-start | bytes 388
  18.6 67.1 %copy-start.648 = (bf16[64]{0:T(256)(128)(2,1)S(1)}, bf16[64]{0:T(256)(128)(2,1)}, u32[]{:S(2)}) copy-start(bf16[64]{0:T(256)(128)(2,1)} %param.26) | copy-start | bytes 388
  18.6 67.3 %copy-start.649 = (bf16[64]{0:T(256)(128)(2,1)S(1)}, bf16[64]{0:T(256)(128)(2,1)}, u32[]{:S(2)}) copy-start(bf16[64]{0:T(256)(128)(2,1)} %param.27) | copy-start | bytes 388
  18.7 67.5 %copy-start.650 = (bf16[64]{0:T(256)(128)(2,1)S(1)}, bf16[64]{0:T(256)(128)(2,1)}, u32[]{:S(2)}) copy-start(bf16[64]{0:T(256)(128)(2,1)} %param.28) | copy-start | bytes 388
  18.7 67.8 %copy-start.651 = (bf16[64]{0:T(256)(128)(2,1)S(1)}, bf16[64]{0:T(256)(128)(2,1)}, u32[]{:S(2)}) copy-start(bf16[64]{0:T(256)(128)(2,1)} %param.29) | copy-start | bytes 388
  18.7 91.3 %copy-start.501 = (bf16[128,64]{0,1:T(8,128)(2,1)S(1)}, bf16[128,64]{0,1:T(8,128)(2,1)}, u32[]{:S(2)}) copy-start(bf16[128,64]{0,1:T(8,128)(2,1)} %param.23) | copy-start | bytes 49156
  18.7 106.7 %all-to-all-start = ((bf16[2,2,512,512]{3,2,1,0:T(8,128)(2,1)}), bf16[2,2,512,512]{3,2,1,0:T(8,128)(2,1)S(1)}, u32[]{:S(2)}, u32[]{:S(2)}) async-start(bf16[2,2,512,512]{3,2,1,0:T(8,128)(2,1)} %bitcast.1000), calls=%async_computation | async-start | bytes 4194304 | tf_op jit(solution)/shard_map/all_to_all | solution.py:206
  23.0 625.4 %all-reduce.81.cloned.1.call-start = ((), (), s32[]{:S(2)}) async-start(), calls=%async_computation.17 | async-start | bytes 8388608 | tf_op jit(solution)/shard_map/psum | solution.py:338
  27.5 120.0 %copy-start.480 = (f32[512]{0:T(512)}, f32[512]{0:T(512)S(1)}, u32[]{:S(2)}) copy-start(f32[512]{0:T(512)S(1)} %get-tuple-element.454) | copy-start | bytes 6148
  29.4 118.5 %copy-start.519 = (f32[256]{0:T(256)}, f32[256]{0:T(256)S(1)}, u32[]{:S(2)}) copy-start(f32[256]{0:T(256)S(1)} %get-tuple-element.462) | copy-start | bytes 3076
  57.6 167.2 %copy-start.87 = (bf16[512,128]{1,0:T(8,128)(2,1)}, bf16[512,128]{1,0:T(8,128)(2,1)S(1)}, u32[]{:S(2)}) copy-start(bf16[512,128]{1,0:T(8,128)(2,1)S(1)} %all_gather.72) | copy-start | bytes 393220
  67.2 64.9 %copy-start.89 = (bf16[512,128]{1,0:T(8,128)(2,1)}, bf16[512,128]{1,0:T(8,128)(2,1)S(1)}, u32[]{:S(2)}) copy-start(bf16[512,128]{1,0:T(8,128)(2,1)S(1)} %all_gather.73) | copy-start | bytes 393220
  84.4 48.1 %copy-start.93 = (bf16[512,128]{1,0:T(8,128)(2,1)}, bf16[512,128]{1,0:T(8,128)(2,1)S(1)}, u32[]{:S(2)}) copy-start(bf16[512,128]{1,0:T(8,128)(2,1)S(1)} %all_gather.74) | copy-start | bytes 393220
  100.5 26.9 %copy-start.401 = (f32[512]{0:T(512)}, f32[512]{0:T(512)S(1)}, u32[]{:S(2)}) copy-start(f32[512]{0:T(512)S(1)} %convert_element_type.1074) | copy-start | bytes 6148
  125.4 523.1 %copy-start.3 = (bf16[2,2,512,512]{3,2,1,0:T(8,128)(2,1)}, bf16[2,2,512,512]{3,2,1,0:T(8,128)(2,1)S(1)}, u32[]{:S(2)}) copy-start(bf16[2,2,512,512]{3,2,1,0:T(8,128)(2,1)S(1)} %all-to-all-done) | copy-start | bytes 6291460
  166.6 201.2 %copy-start.37 = (f32[512,640]{1,0:T(8,128)}, f32[512,640]{1,0:T(8,128)S(1)}, u32[]{:S(2)}) copy-start(f32[512,640]{1,0:T(8,128)S(1)} %get-tuple-element.432) | copy-start | bytes 3932164
  264.4 59.4 %copy-start.168 = (bf16[128,384]{0,1:T(8,128)(2,1)}, bf16[128,384]{0,1:T(8,128)(2,1)S(1)}, u32[]{:S(2)}) copy-start(bf16[128,384]{0,1:T(8,128)(2,1)S(1)} %divide_convert_fusion.21) | copy-start | bytes 294916
  325.2 27.7 %copy-start.573 = (f32[640]{0:T(1024)S(1)}, f32[640]{0:T(1024)}, u32[]{:S(2)}) copy-start(f32[640]{0:T(1024)} %get-tuple-element.325) | copy-start | bytes 7684
  325.2 27.7 %copy-start.581 = (s32[640]{0:T(1024)S(1)}, s32[640]{0:T(1024)}, u32[]{:S(2)}) copy-start(s32[640]{0:T(1024)} %get-tuple-element.444) | copy-start | bytes 7684
  325.2 27.7 %copy-start.603 = (s32[512]{0:T(512)S(1)}, s32[512]{0:T(512)}, u32[]{:S(2)}) copy-start(s32[512]{0:T(512)} %get-tuple-element.449) | copy-start | bytes 6148
  325.2 27.7 %copy-start.659 = (pred[640]{0:T(1024)(128)(4,1)S(1)}, pred[640]{0:T(1024)(128)(4,1)}, u32[]{:S(2)}) copy-start(pred[640]{0:T(1024)(128)(4,1)} %iota_compare_fusion.11) | copy-start | bytes 1924
  346.6 108.8 %copy-start.277 = (bf16[32,256]{1,0:T(8,128)(2,1)}, bf16[32,256]{1,0:T(8,128)(2,1)S(1)}, u32[]{:S(2)}) copy-start(bf16[32,256]{1,0:T(8,128)(2,1)S(1)} %slice.1842) | copy-start | bytes 49156
  492.7 47.2 %all-to-all-start.2 = ((bf16[2,2,512,512]{3,2,1,0:T(8,128)(2,1)}), bf16[2,2,512,512]{3,2,1,0:T(8,128)(2,1)}, u32[]{:S(2)}, u32[]{:S(2)}) async-start(bf16[2,2,512,512]{3,2,1,0:T(8,128)(2,1)} %bitcast.999), calls=%async_computation.4 | async-start | bytes 4194304 | tf_op jit(solution)/shard_map/all_to_all | solution.py:207
  497.5 308.8 %reduce-scatter.3.cloned.1.call-start = ((), (), s32[]{:S(2)}) async-start(), calls=%async_computation.14 | async-start | bytes 1310720 | tf_op jit(solution)/shard_map/reduce_scatter | solution.py:347
  666.0 141.4 %reduce-scatter.5.cloned.1.call-start = ((), (), s32[]{:S(2)}) async-start(), calls=%async_computation.15 | async-start | bytes 1310720 | tf_op jit(solution)/shard_map/reduce_scatter | solution.py:347
  677.2 199.6 %all-reduce.79.cloned.1.call-start = ((), (), s32[]{:S(2)}) async-start(), calls=%async_computation.16 | async-start | bytes 8388608 | tf_op jit(solution)/shard_map/psum | solution.py:363
  787.1 13.1 all-to-all-start.7
  800.2 587.2 %all-to-all-start.6 = ((bf16[8,64,512]{2,1,0:T(8,128)(2,1)}), bf16[8,64,512]{2,1,0:T(8,128)(2,1)}, u32[]{:S(2)}, u32[]{:S(2)}) async-start(bf16[8,64,512]{2,1,0:T(8,128)(2,1)} %bitcast.182), calls=%async_computation.8 | async-start | bytes 1048576 | tf_op jit(solution)/shard_map/all_to_all | solution.py:17
  804.4 72.5 %copy-start.352 = (f32[1024]{0:T(1024)S(1)}, f32[1024]{0:T(1024)}, u32[]{:S(2)}) copy-start(f32[1024]{0:T(1024)} %copy-done.351) | copy-start | bytes 12292
  804.4 653.0 %all-reduce.83.cloned.1.call-start = ((), (), s32[]{:S(2)}) async-start(), calls=%async_computation.18 | async-start | bytes 4194304 | tf_op jit(solution)/shard_map/psum | solution.py:454
  1243.6 25.9 %copy-start.236 = (bf16[384,256]{0,1:T(8,128)(2,1)S(1)}, bf16[384,256]{0,1:T(8,128)(2,1)}, u32[]{:S(2)}) copy-start(bf16[384,256]{0,1:T(8,128)(2,1)} %fusion.947) | copy-start | bytes 589828
  1387.4 11.5 all-to-all-start.1
  1392.0 25.9 %copy-start.272 = (bf16[512,128]{0,1:T(8,128)(2,1)S(1)}, bf16[512,128]{0,1:T(8,128)(2,1)}, u32[]{:S(2)}) copy-start(bf16[512,128]{0,1:T(8,128)(2,1)} %fusion.125) | copy-start | bytes 393220
  1398.9 7.8 all-to-all-start.11
  1406.7 7.8 all-to-all-start.10
  1414.5 8.5 all-to-all-start.5
  1417.9 39.5 %copy-start.4 = (bf16[2,2,512,512]{3,2,1,0:T(8,128)(2,1)S(1)}, bf16[2,2,512,512]{3,2,1,0:T(8,128)(2,1)}, u32[]{:S(2)}) copy-start(bf16[2,2,512,512]{3,2,1,0:T(8,128)(2,1)} %copy-done.3) | copy-start | bytes 6291460
  1417.9 39.5 %copy-start.348 = (f32[1,4,2,128]{3,1,2,0:T(4,128)S(1)}, f32[1,4,2,128]{3,1,2,0:T(4,128)}, u32[]{:S(2)}) copy-start(f32[1,4,2,128]{3,1,2,0:T(4,128)} %copy-done.347) | copy-start | bytes 12292
  1418.0 39.5 %copy-start.350 = (f32[1,4,2,128]{3,1,2,0:T(4,128)S(1)}, f32[1,4,2,128]{3,1,2,0:T(4,128)}, u32[]{:S(2)}) copy-start(f32[1,4,2,128]{3,1,2,0:T(4,128)} %copy-done.349) | copy-start | bytes 12292
  1418.0 39.4 %copy-start.402 = (f32[512]{0:T(512)S(1)}, f32[512]{0:T(512)}, u32[]{:S(2)}) copy-start(f32[512]{0:T(512)} %copy-done.401) | copy-start | bytes 6148
  1423.0 10.9 all-to-all-start.4
  1460.9 12.0 all-to-all-start.9
  1472.3 23.7 %copy-start.124 = (bf16[4,128,512]{2,1,0:T(8,128)(2,1)S(1)}, bf16[4,128,512]{2,1,0:T(8,128)(2,1)}, u32[]{:S(2)}) copy-start(bf16[4,128,512]{2,1,0:T(8,128)(2,1)} %gather_fusion.2) | copy-start | bytes 1572868
  1473.0 8.8 all-to-all-start.8
  1481.7 11.7 all-to-all-start.3
  (654 other events, 3271.9 us)
Sparse Core Ops, SparseCore 0:
  492.8 155.6 all-reduce.80
  666.1 26.1 reduce-scatter.2
  694.6 25.7 reduce-scatter.4
  722.8 154.0 all-reduce.78
  1371.2 86.1 all-reduce.82
where the time goes:
time: 1520 us; the launch traced here: 1500 us
  local copies, waits for them, and re-layouts  472 us (31%)
  other arithmetic  294 us (19%)
  matrix products  270 us (18%)
  waiting for transfers between devices  223 us (15%)
  blocking collectives  175 us (12%)
  starting transfers between devices  47.2 us (3%)
  between operations  22.6 us (1%)
    dot_general x84, matrix products, dot_outer(): lax.dot_general(left_mat, right_mat, (((1,), (1,)), ((), ())), preferred_...  125 us
    psum x1, waiting for transfers between devices, one_batch(): branch_attn = lax.psum(merged_part, 'mp')  103 us
    reduce_sum x40, other arithmetic, group_sum(): jnp.sum(values.reshape((values.shape[0] // group_width, group_width) + va...  88.7 us
    dot_general x84, matrix products, dot_inner(): lax.dot_general(left_mat, right_mat, (((0,), (0,)), ((), ())), preferred_...  73.6 us
    dot_general x84, matrix products, dot_plain(): return jnp.dot(left_mat, right_mat, preferred_element_type=jnp.float32)  71.9 us
    psum x1, waiting for transfers between devices, one_batch(): mid_grad = lax.psum(mid_part, 'mp')  67.3 us
    reshape x18, local copies, waits for them, and re-layouts, one_batch(): jnp.repeat(coarse_grad, 2 ** level_at, axis=0) * valid_rows[:, None]  52.7 us
    unnamed x1395, local copies, waits for them, and re-layouts  46.1 us
  transfers between devices with their start and end apart: 17, of which 11 were waited for; matrix products, arithmetic and copies ran while one was open for 44% of the time, Pallas kernels for 0%

commit v1 on v0

--- a/solution.py
+++ b/solution.py
@@ -1,6 +1,10 @@
+import functools
+
 import jax
 import jax.numpy as jnp
 from jax import lax
+from jax.experimental import pallas as pl
+from jax.experimental.pallas import tpu as pltpu
 from jax.sharding import PartitionSpec as P
 
 HD = 64
@@ -161,7 +165,7 @@
     return (query_grad, pair_grad[: coarse_rows + 2 * NR])
 
 
-def body(
+def general_body(
     incoming_embeddings,
     output_sensitivity,
     sequence_extents,
@@ -194,12 +198,10 @@
     level_top = (part_len * slices // (2 * NR)).bit_length() - 1
     upper_rows = NR // 2
     upper_whole = upper_rows * slices
-    seq_ids = jnp.arange(seq_count, dtype=jnp.int32)
-    inverse = jnp.sum(jnp.where(seq_ids[:, None] == seq_ids[None, :], seq_ids[:, None], 0), axis=0)
-    send_tok = jnp.take(incoming_embeddings, seq_ids, axis=0).reshape(
+    send_tok = incoming_embeddings.reshape(
         groups, batches, piece_len, model_width
     )
-    send_cot = jnp.take(output_sensitivity, seq_ids, axis=0).reshape(
+    send_cot = output_sensitivity.reshape(
         groups, batches, piece_len, model_width
     )
     dealt_tok, dealt_cot = (
@@ -208,9 +210,7 @@
     )
     dealt_tok = dealt_tok.reshape(batches, part_len, model_width)
     dealt_cot = dealt_cot.reshape(batches, part_len, model_width)
-    my_lengths = jnp.take(
-        sequence_extents, lax.dynamic_slice_in_dim(seq_ids, group_id * batches, batches, 0)
-    )
+    my_lengths = lax.dynamic_slice_in_dim(sequence_extents, group_id * batches, batches, 0)
 
     def split_rows(rows):
         return rows.reshape((groups, models, share_len) + rows.shape[1:])
@@ -521,8 +521,6 @@
         lax.all_to_all(result_all, "dp", split_axis=1, concat_axis=0, tiled=True),
         lax.all_to_all(grad_all, "dp", split_axis=1, concat_axis=0, tiled=True),
     )
-    back_out = jnp.take(back_out, inverse, axis=0)
-    back_grad = jnp.take(back_grad, inverse, axis=0)
     return (
         back_out,
         back_grad,
@@ -537,6 +535,710 @@
         owned_grads[8],
         owned_grads[9],
     )
+
+
+MESH = pl.DeviceIdType.MESH
+NEG = -1e30
+
+
+def nn(a, b):
+    return lax.dot_general(a, b, (((1,), (0,)), ((), ())), preferred_element_type=jnp.float32)
+
+
+def nt(a, b):
+    return lax.dot_general(a, b, (((1,), (1,)), ((), ())), preferred_element_type=jnp.float32)
+
+
+def tn(a, b):
+    return lax.dot_general(a, b, (((0,), (0,)), ((), ())), preferred_element_type=jnp.float32)
+
+
+def halves(values):
+    high = values.astype(jnp.bfloat16)
+    return high, (values - high.astype(jnp.float32)).astype(jnp.bfloat16)
+
+
+class Plan:
+    def __init__(self, part, spots):
+        self.part, self.spots = part, spots
+        self.levels = (part // NR).bit_length()
+        self.top = (part * spots // (2 * NR)).bit_length() - 1
+        self.own = [part >> level for level in range(self.levels)]
+        self.at, row = [], 0
+        for rows in self.own:
+            self.at.append(row)
+            row += rows + 2 * NR
+        self.upper = row
+        self.rows = row + spots * NR
+        self.pool_at, row = [None], 0
+        for rows in self.own[1:]:
+            self.pool_at.append(row)
+            row += rows
+        self.pool_upper = row
+        self.pooled = row + NR
+        self.slot, row = [], 0
+        for level in range(self.levels, self.top + 1):
+            self.slot.append((level, row, part >> level))
+            row += part >> level
+        assert row <= NR and spots * NR == 128 and self.pooled == part
+        self.segments = [(self.at[lv], self.own[lv] + 2 * NR, lv) for lv in range(self.levels)]
+        self.inner, self.outer = [], []
+        level = 0
+        while level < self.levels:
+            start, total = self.at[level], self.own[level] + 2 * NR
+            end = start + total
+            if total < 96:
+                self.outer.append((start, self.upper - start, self.upper - 128, None))
+                break
+            row = start
+            while row < end:
+                count = min(96, end - row)
+                window = max(start, min(row - NR, end - 128))
+                tile = (row, count, window, level if window + 128 <= end else None)
+                inside = window >= start + NR and window + 128 <= end - NR
+                (self.inner if inside else self.outer).append(tile)
+                row += count
+            level += 1
+        self.outer.append((self.upper, 128, self.upper, None))
+        self.tiles = self.inner + self.outer
+
+
+def row_places(plan, rows, low, high, spot):
+    level = jnp.full(rows.shape, -1, jnp.int32)
+    place = jnp.zeros(rows.shape, jnp.int32)
+    for start, count, lv in plan.segments:
+        if start < high and start + count > low:
+            inside = (rows >= start) & (rows < start + count)
+            level = jnp.where(inside, lv, level)
+            place = jnp.where(inside, spot * plan.own[lv] - NR + rows - start, place)
+    if high > plan.upper:
+        owner = lax.shift_right_arithmetic(rows - plan.upper, 4)
+        within = (rows - plan.upper) & (NR - 1)
+        for lv, first, count in plan.slot:
+            inside = (rows >= plan.upper) & (within >= first) & (within < first + count)
+            level = jnp.where(inside, lv, level)
+            place = jnp.where(inside, owner * count + within - first, place)
+    return level, place
+
+
+def log_counts(plan, tile, spot, length):
+    first, count, window, level = tile
+    row_at = first + lax.broadcasted_iota(jnp.int32, (count, 128), 0)
+    key_at = window + lax.broadcasted_iota(jnp.int32, (8, 128), 1)
+    row_level, row_place = row_places(plan, row_at, first, first + count, spot)
+    key_level, key_place = row_places(plan, key_at, window, window + 128, spot)
+    span = lax.shift_left(jnp.ones_like(key_level), jnp.maximum(key_level, 0))
+    counts = jnp.clip(length - span * key_place, 0, span)
+    usable = (counts > 0) & (key_place >= 0) & (key_level >= 0)
+    logs = jnp.where(usable, jnp.log(jnp.maximum(counts, 1).astype(jnp.float32)), NEG)
+    coarse = lambda level_at, place_at, by: level_at * 65536 + lax.shift_right_arithmetic(place_at, by)
+    key_block = coarse(key_level, key_place, 4)[:1]
+    key_half = coarse(key_level, key_place, 3)[:1]
+    allowed = jnp.abs(coarse(row_level, row_place, 4) - key_block) <= 1
+    if level != 0:
+        apart = jnp.abs(coarse(row_level, row_place, 3) - key_half) >= 2
+        allowed = allowed & (apart if level is not None else apart | (row_level == 0)) & (row_level >= 0)
+    return jnp.where(allowed, logs[:1], NEG)
+
+
+def pool_bounds(plan, shape, dim):
+    row = lax.broadcasted_iota(jnp.int32, shape, dim)
+    low = jnp.full(shape, -1, jnp.int32)
+    size = jnp.zeros(shape, jnp.int32)
+    level = jnp.zeros(shape, jnp.int32)
+    parts = [(plan.pool_at[lv], plan.own[lv], lv) for lv in range(1, plan.levels)]
+    parts += [(plan.pool_upper + first, count, lv) for lv, first, count in plan.slot]
+    for start, count, lv in parts:
+        inside = (row >= start) & (row < start + count)
+        low = jnp.where(inside, (row - start) << lv, low)
+        size = jnp.where(inside, 1 << lv, size)
+    return low, size
+
+
+def whole_layer(plan, dims, net_count, *refs):
+    (extents, own_weights, own_norms, tokens_in, cotangent_in,
+     out_rows, out_grads, weight_grads, norm_grads,
+     weights, norms, tokens, cotangent, ext, logs, pool, unpool, inverse, work,
+     attended, ratio, recip, normed, scaled, rstd, grad_ext, total_ext, residual, acc, acc2, totals, result, row_grads,
+     grads, got1, got2, got3, got4, norm_got,
+     load_sem, send_sem, recv_sem) = refs
+    part, width, pair, hidden = dims
+    f32, bf16 = jnp.float32, jnp.bfloat16
+    models = weights.shape[0]
+    ax, sq, az = lax.axis_index("dp"), lax.axis_index("seq"), lax.axis_index("mp")
+    ay, ac = sq // 2, sq % 2
+    spot = sq * 2 + ax
+    spots = plan.spots
+    length = extents[az]
+    qkv = 3 * pair
+
+    def device(x, y, c, z):
+        return (x, y * 2 + c, z)
+
+    def at_spot(place):
+        return (place % 2, place // 2, az)
+
+    barrier = pltpu.get_barrier_semaphore()
+    for step in range(1, spots):
+        pl.semaphore_signal(barrier, inc=1, device_id=at_spot((spot + step) % spots), device_id_type=MESH)
+    for step in range(1, models):
+        pl.semaphore_signal(barrier, inc=1, device_id=device(ax, ay, ac, (az + step) % models), device_id_type=MESH)
+    load_tokens = pltpu.make_async_copy(tokens_in.at[az, 0], tokens, load_sem.at[0])
+    load_cotangent = pltpu.make_async_copy(cotangent_in.at[az, 0], cotangent, load_sem.at[1])
+    load_tokens.start()
+    load_cotangent.start()
+    weights[az, ax, ay, ac] = own_weights[...]
+    norms[spot] = own_norms[...]
+    pl.semaphore_wait(barrier, spots - 1 + models - 1)
+
+    used = [0]
+    sent = []
+
+    def copy(src, dst, to):
+        i = used[0]
+        used[0] += 1
+        assert i < net_count
+        return pltpu.make_async_remote_copy(
+            src_ref=src, dst_ref=dst, send_sem=send_sem.at[i], recv_sem=recv_sem.at[i],
+            device_id=to, device_id_type=MESH)
+
+    def send(src, dst, to):
+        c = copy(src, dst, to)
+        c.start()
+        sent.append((c, None))
+        return c
+
+    x_peer = device(1 - ax, ay, ac, az)
+    y_peer = device(ax, 1 - ay, ac, az)
+    c_peer = device(ax, ay, 1 - ac, az)
+
+    chunks = [(0, 2 * pair, True), (2 * pair, 2 * pair, False),
+              (4 * pair, hidden, True), (4 * pair + hidden, hidden, False)]
+
+    def gather_z(chunk):
+        col, count, _ = chunk
+        cols = pl.ds(col, count)
+        place = weights.at[az, ax, ay, ac, :, cols]
+        return [send(own_weights.at[:, cols], place, device(ax, ay, ac, (az + step) % models))
+                for step in range(1, models)]
+
+    def gather_first(chunk):
+        col, count, x_first = chunk
+        block = weights.at[:, ax, ay, ac, :, pl.ds(col, count)]
+        return [send(block, block, x_peer if x_first else y_peer)]
+
+    def gather_second(chunk):
+        col, count, x_first = chunk
+        cols = pl.ds(col, count)
+        block = weights.at[:, :, ay, ac, :, cols] if x_first else weights.at[:, ax, :, ac, :, cols]
+        return [send(block, block, y_peer if x_first else x_peer)]
+
+    def gather_core(chunk):
+        col, count, _ = chunk
+        block = weights.at[:, :, :, ac, :, pl.ds(col, count)]
+        return [send(block, block, c_peer)]
+
+    def arrive(copies):
+        for c in copies:
+            c.wait_recv()
+
+    norm_copies = [send(own_norms, norms.at[spot], at_spot((spot + step) % spots)) for step in range(1, spots)]
+    flight = [gather_z(chunk) for chunk in chunks]
+
+    low, size = pool_bounds(plan, (part, 128), 0)
+    for block in range(part // 128):
+        token_at = block * 128 + lax.broadcasted_iota(jnp.int32, (part, 128), 1)
+        member = (token_at >= low) & (token_at < low + size) & (token_at + spot * part < length)
+        pool[:, block * 128:(block + 1) * 128] = jnp.where(member, 1.0, 0.0).astype(bf16)
+    first_token = spot * part + low
+    counts = jnp.clip(length - first_token, 0, size)
+    inverse[...] = 1.0 / jnp.maximum(counts, 1).astype(f32)
+    low, size = pool_bounds(plan, (8, part), 1)
+    token_at = lax.broadcasted_iota(jnp.int32, (part, part), 0)
+    member = (token_at >= low[:1]) & (token_at < (low + size)[:1])
+    unpool[...] = jnp.where(member, 1.0, 0.0).astype(bf16)
+    load_tokens.wait()
+
+    def statistics(values):
+        center = values - jnp.mean(values, axis=-1, keepdims=True)
+        spread = jnp.mean(center * center, axis=-1, keepdims=True)
+        scale = lax.rsqrt(spread + 1e-05)
+        return center * scale, scale
+
+    xhat, scale = statistics(tokens[...].astype(f32))
+    scaled[...] = xhat
+    rstd[...] = jnp.broadcast_to(scale, (part, 128))
+    arrive(flight[0])
+    flight[0] = gather_first(chunks[0])
+    arrive(flight[1])
+    flight[1] = gather_first(chunks[1])
+    for i, tile in enumerate(plan.tiles):
+        logs[i, 0:tile[1]] = log_counts(plan, tile, spot, length)
+    arrive(norm_copies)
+    gains = norms[0]
+    for i in range(1, spots):
+        gains = gains + norms[i]
+    pre_gain, pre_shift, mid_gain, mid_shift = (gains[i:i + 1] for i in range(4))
+    normed[...] = (scaled[...] * pre_gain + pre_shift).astype(bf16)
+    for i in (0, 1):
+        arrive(flight[i])
+        flight[i] = gather_second(chunks[i])
+    for i in (0, 1):
+        arrive(flight[i])
+        flight[i] = gather_core(chunks[i])
+    for i in (2, 3):
+        arrive(flight[i])
+        flight[i] = gather_first(chunks[i])
+
+    def weight_cols(m, col, count):
+        return weights[m, :, :, :, :, col:col + count].reshape(width, count)
+
+    arrive(flight[0])
+    arrive(flight[1])
+
+    def project(m, carry):
+        rows = nn(normed[...], weight_cols(m, 0, qkv)).astype(bf16)
+        ext[m, NR:NR + part, :] = rows
+        sums = nn(pool[...], rows)
+        means = (sums * jnp.concatenate([inverse[...]] * 3, axis=1)).astype(bf16)
+        for lv in range(1, plan.levels):
+            ext[m, plan.at[lv] + NR:plan.at[lv] + NR + plan.own[lv], :] = means[plan.pool_at[lv]:plan.pool_at[lv] + plan.own[lv]]
+        ext[m, pl.ds(plan.upper + spot * NR, NR), :] = means[plan.pool_upper:plan.pool_upper + NR]
+        return carry
+
+    lax.fori_loop(0, models, project, 0)
+
+    is_first, is_last = spot == 0, spot == spots - 1
+
+    def exchange(arrays):
+        pending = []
+        for ref in arrays:
+            lead = (slice(None),) * (len(ref.shape) - 2)
+            for lv in range(plan.levels):
+                start, rows = plan.at[lv], plan.own[lv]
+                to_right = copy(ref.at[lead + (pl.ds(start + rows, NR), slice(None))],
+                                ref.at[lead + (pl.ds(start, NR), slice(None))], at_spot((spot + 1) % spots))
+                to_left = copy(ref.at[lead + (pl.ds(start + NR, NR), slice(None))],
+                               ref.at[lead + (pl.ds(start + NR + rows, NR), slice(None))],
+                               at_spot((spot + spots - 1) % spots))
+                pending.append((to_right, to_left))
+        uppers = []
+        for ref in arrays:
+            lead = (slice(None),) * (len(ref.shape) - 2)
+            block = ref.at[lead + (pl.ds(plan.upper + spot * NR, NR), slice(None))]
+            for step in range(1, spots):
+                uppers.append(copy(block, block, at_spot((spot + step) % spots)))
+
+        @pl.when(jnp.logical_not(is_last))
+        def _():
+            for to_right, _ in pending:
+                to_right.start()
+
+        @pl.when(jnp.logical_not(is_first))
+        def _():
+            for _, to_left in pending:
+                to_left.start()
+
+        for c in uppers:
+            c.start()
+
+        @pl.when(is_first)
+        def _():
+            for ref in arrays:
+                lead = (slice(None),) * (len(ref.shape) - 2)
+                for lv in range(plan.levels):
+                    place = lead + (slice(plan.at[lv], plan.at[lv] + NR), slice(None))
+                    ref[place] = jnp.zeros(ref.shape[:-2] + (NR, ref.shape[-1]), ref.dtype)
+
+        @pl.when(is_last)
+        def _():
+            for ref in arrays:
+                lead = (slice(None),) * (len(ref.shape) - 2)
+                for lv in range(plan.levels):
+                    row = plan.at[lv] + NR + plan.own[lv]
+                    ref[lead + (slice(row, row + NR), slice(None))] = jnp.zeros(
+                        ref.shape[:-2] + (NR, ref.shape[-1]), ref.dtype)
+
+        def wait():
+            @pl.when(jnp.logical_not(is_first))
+            def _():
+                for to_right, _ in pending:
+                    to_right.wait_recv()
+
+            @pl.when(jnp.logical_not(is_last))
+            def _():
+                for _, to_left in pending:
+                    to_left.wait_recv()
+
+            for c in uppers:
+                c.wait_recv()
+
+        def done():
+            @pl.when(jnp.logical_not(is_last))
+            def _():
+                for to_right, _ in pending:
+                    to_right.wait_send()
+
+            @pl.when(jnp.logical_not(is_first))
+            def _():
+                for _, to_left in pending:
+                    to_left.wait_send()
+
+            for c in uppers:
+                c.wait_send()
+
+        return wait, done
+
+    rims_wait, rims_done = exchange([ext])
+
+    lane = lax.broadcasted_iota(jnp.int32, (1, pair), 1)
+    left_head = lane < HD
+
+    def both_heads(rows):
+        zero = jnp.zeros_like(rows)
+        return jnp.concatenate([jnp.where(left_head, rows, zero), jnp.where(left_head, zero, rows)], axis=0)
+
+    def joined(rows):
+        half = rows.shape[0] // 2
+        return jnp.where(left_head, rows[:half], rows[half:])
+
+    ones = jnp.ones((128, 128), bf16)
+    slot_row = pl.multiple_of(spot * NR, NR)
+
+    def tile_weights(m, index, rows_at, count, window, own_slot=False):
+        queries = both_heads(ext[m, rows_at, 0:pair])
+        keys = ext[m, window:window + 128, pair:2 * pair]
+        values = jnp.concatenate([ext[m, window:window + 128, 2 * pair:3 * pair], ones], axis=1)
+        mask = logs[index, pl.ds(slot_row, NR)] if own_slot else logs[index, 0:count]
+        weight = jnp.exp(nt(queries, keys) + jnp.concatenate([mask, mask], axis=0))
+        return queries, keys, values, weight
+
+    def attend(tiles):
+        def body(m, carry):
+            for tile in tiles:
+                first, count, window, _ = tile
+                own_slot = first == plan.upper
+                if own_slot:
+                    rows_at, count = pl.ds(pl.multiple_of(plan.upper + slot_row, NR), NR), NR
+                else:
+                    rows_at = slice(first, first + count)
+                _, _, values, weight = tile_weights(m, plan.tiles.index(tile), rows_at, count, window, own_slot)
+                both = nn(weight.astype(bf16), values)
+                work[m, first:first + count, 0:pair] = joined(both[:, :128])
+                work[m, first:first + count, pair:2 * pair] = joined(both[:, 128:])
+            return carry
+
+        lax.fori_loop(0, models, body, 0)
+
+    attend(plan.inner)
+    for i in (2, 3):
+        arrive(flight[i])
+        flight[i] = gather_second(chunks[i])
+    rims_wait()
+    attend(plan.outer)
+    for i in (2, 3):
+        arrive(flight[i])
+        flight[i] = gather_core(chunks[i])
+
+    def coarse_rows(m, cols, slot_at):
+        rows = [work[m, plan.at[lv] + NR:plan.at[lv] + NR + plan.own[lv], 0:cols] for lv in range(1, plan.levels)]
+        return jnp.concatenate(rows + [work[m, slot_at, 0:cols]], axis=0)
+
+    def spread_out(rows):
+        high, rest = halves(rows)
+        return nn(unpool[...], high) + nn(unpool[...], rest)
+
+    def normalise(m, carry):
+        both = spread_out(coarse_rows(m, 2 * pair, slice(plan.upper, plan.upper + NR)))
+        both = both + work[m, NR:NR + part, 0:2 * pair]
+        inv_total = 1.0 / both[:, pair:]
+        quotient = both[:, :pair] * inv_total
+        ratio[m] = quotient
+        recip[m] = inv_total
+        attended[m] = quotient.astype(bf16)
+        return carry
+
+    lax.fori_loop(0, models, normalise, 0)
+
+    residual[...] = tokens[...].astype(f32)
+
+    def merge(m, carry):
+        residual[...] += nt(attended[m], weight_cols(m, qkv, pair))
+        return carry
+
+    lax.fori_loop(0, models, merge, 0)
+    after = residual[...]
+    mid_hat, mid_scale = statistics(after)
+    mid = (mid_hat * mid_gain + mid_shift).astype(bf16)
+    mid_t = mid.T
+    load_cotangent.wait()
+    row_at = lax.broadcasted_iota(jnp.int32, (part, 1), 0) + spot * part
+    valid = row_at < length
+    out_grad = jnp.where(valid, cotangent[...], jnp.zeros((), bf16))
+    out_grad_t = out_grad.T
+    arrive(flight[2])
+    arrive(flight[3])
+    acc[...] = jnp.zeros(acc.shape, f32)
+    acc2[...] = jnp.zeros(acc.shape, f32)
+    block_shape = grads.shape[1:5] + (hidden,)
+
+    def feed(m, carry):
+        expand = weight_cols(m, 4 * pair, hidden)
+        contract_t = weight_cols(m, 4 * pair + hidden, hidden)
+        up = nn(mid, expand)
+        phi = 0.5 + 0.5 * lax.erf(up * (0.5 ** 0.5))
+        act = (up * phi).astype(bf16)
+        slope = phi + up * (jnp.exp(-0.5 * up * up) * 0.3989422804014327)
+        acc[...] += nt(act, contract_t)
+        hidden_grad = (nn(out_grad, contract_t) * slope).astype(bf16)
+        grads[m, :, :, :, :, 4 * pair:4 * pair + hidden] = nn(mid_t, hidden_grad).astype(bf16).reshape(block_shape)
+        grads[m, :, :, :, :, 4 * pair + hidden:4 * pair + 2 * hidden] = nn(out_grad_t, act).astype(bf16).reshape(block_shape)
+        acc2[...] += nt(hidden_grad, expand)
+        return carry
+
+    lax.fori_loop(0, models, feed, 0)
+    result[...] = jnp.where(valid, after + acc[...], 0.0).astype(bf16)
+    mid_grad = acc2[...]
+
+    def reduce_core(chunk):
+        col, count, _ = chunk
+        cols = pl.ds(col, count)
+        return [send(grads.at[:, :, :, 1 - ac, :, cols], got1.at[:, :, :, :, cols], c_peer)]
+
+    def reduce_first(chunk):
+        col, count, x_first = chunk
+        cols = pl.ds(col, count)
+        got1[:, :, :, :, cols] = got1[:, :, :, :, cols] + grads[:, :, :, ac, :, cols]
+        src = got1.at[:, 1 - ax, :, :, cols] if x_first else got1.at[:, :, 1 - ay, :, cols]
+        return [send(src, got2.at[:, :, :, cols], x_peer if x_first else y_peer)]
+
+    def reduce_second(chunk):
+        col, count, x_first = chunk
+        cols = pl.ds(col, count)
+        mine = got1[:, ax, :, :, cols] if x_first else got1[:, :, ay, :, cols]
+        got2[:, :, :, cols] = got2[:, :, :, cols] + mine
+        src = got2.at[:, 1 - ay if x_first else 1 - ax, :, cols]
+        return [send(src, got3.at[:, :, cols], y_peer if x_first else x_peer)]
+
+    def reduce_z(chunk):
+        col, count, x_first = chunk
+        cols = pl.ds(col, count)
+        got3[:, :, cols] = got3[:, :, cols] + got2[:, ay if x_first else ax, :, cols]
+        return [send(got3.at[(az + step) % models, :, cols], got4.at[step - 1, :, cols],
+                     device(ax, ay, ac, (az + step) % models)) for step in range(1, models)]
+
+    def reduce_end(chunk):
+        col, count, _ = chunk
+        cols = pl.ds(col, count)
+        total = got3[az, :, cols].astype(f32)
+        for step in range(1, models):
+            total = total + got4[step - 1, :, cols].astype(f32)
+        weight_grads[:, cols] = total
+
+    back = {i: reduce_core(chunks[i]) for i in (2, 3)}
+
+    def rows_home(source, target):
+        share = part // models
+        target[az] = source[pl.ds(pl.multiple_of(az * share, share), share), :]
+        return [send(source.at[pl.ds(pl.multiple_of(((az + step) % models) * share, share), share), :],
+                     target.at[az], device(ax, ay, ac, (az + step) % models)) for step in range(1, models)]
+
+    def norm_back(grad, hat, scale_row, gain):
+        scaled_grad = grad * gain
+        mean_grad = jnp.mean(scaled_grad, axis=-1, keepdims=True)
+        mean_along = jnp.mean(scaled_grad * hat, axis=-1, keepdims=True)
+        return scale_row * (scaled_grad - mean_grad - hat * mean_along)
+
+    through = out_grad.astype(f32) + norm_back(mid_grad, mid_hat, mid_scale, mid_gain)
+    residual[...] = through
+    branch = through.astype(bf16)
+    branch_t = branch.T
+    norm_sums = [jnp.sum(mid_grad * mid_hat, axis=0, keepdims=True), jnp.sum(mid_grad, axis=0, keepdims=True)]
+
+    merge_shape = grads.shape[1:5] + (pair,)
+    select_row = lax.broadcasted_iota(jnp.int32, (pair, 128), 0) // HD
+    select_col = lax.broadcasted_iota(jnp.int32, (pair, 128), 1) // 2
+
+    totals[...] = jnp.zeros(totals.shape, f32)
+
+    def unmerge(m, carry):
+        grads[m, :, :, :, :, qkv:qkv + pair] = nn(branch_t, attended[m]).astype(bf16).reshape(merge_shape)
+        attended_grad = nn(branch, weight_cols(m, qkv, pair)) * recip[m]
+        fine = attended_grad.astype(bf16)
+        grad_ext[m, NR:NR + part, :] = fine
+        sums = nn(pool[...], fine).astype(bf16)
+        for lv in range(1, plan.levels):
+            grad_ext[m, plan.at[lv] + NR:plan.at[lv] + NR + plan.own[lv], :] = sums[plan.pool_at[lv]:plan.pool_at[lv] + plan.own[lv]]
+        grad_ext[m, pl.ds(pl.multiple_of(plan.upper + slot_row, NR), NR), :] = sums[plan.pool_upper:plan.pool_upper + NR]
+        high, rest = halves(attended_grad * ratio[m])
+        chosen = jnp.where(select_row + 2 * m == select_col, -1.0, 0.0).astype(bf16)
+        totals[...] += nn(high, chosen) + nn(rest, chosen)
+        return carry
+
+    lax.fori_loop(0, models, unmerge, 0)
+    even = lax.broadcasted_iota(jnp.int32, (1, 128), 1) % 2 == 0
+
+    def high_rest(values):
+        high, rest = halves(values)
+        return jnp.where(even, high, rest)
+
+    high, rest = halves(totals[...])
+    total_ext[NR:NR + part, :] = jnp.where(even, high, rest)
+    sums = high_rest(nn(pool[...], high) + nn(pool[...], rest))
+    for lv in range(1, plan.levels):
+        total_ext[plan.at[lv] + NR:plan.at[lv] + NR + plan.own[lv], :] = sums[plan.pool_at[lv]:plan.pool_at[lv] + plan.own[lv]]
+    total_ext[pl.ds(pl.multiple_of(plan.upper + slot_row, NR), NR), :] = sums[plan.pool_upper:plan.pool_upper + NR]
+    back_wait, back_done = exchange([grad_ext, total_ext])
+    rows_out = rows_home(result, out_rows)
+
+    head_of_lane = lax.broadcasted_iota(jnp.int32, (1, 128), 1) // 2
+
+    def clear(m, carry):
+        work[m] = jnp.zeros(work.shape[1:], f32)
+        return carry
+
+    lax.fori_loop(0, models, clear, 0)
+
+    def attend_back(tiles):
+        def body(m, carry):
+            for tile in tiles:
+                first, count, window, _ = tile
+                rows_at = slice(first, first + count)
+                queries, keys, values, weight = tile_weights(m, plan.tiles.index(tile), rows_at, count, window)
+                numer = both_heads(grad_ext[m, rows_at, :])
+                tot = total_ext[rows_at, :]
+                zero = jnp.zeros_like(tot)
+                tots = jnp.concatenate([jnp.where(head_of_lane == 2 * m, tot, zero),
+                                        jnp.where(head_of_lane == 2 * m + 1, tot, zero)], axis=0)
+                score_grad = (weight * nt(jnp.concatenate([numer, tots], axis=1), values)).astype(bf16)
+                work[m, rows_at, 0:pair] = joined(nn(score_grad, keys))
+                key_rows = slice(window, window + 128)
+                work[m, key_rows, pair:2 * pair] += tn(score_grad, queries)
+                work[m, key_rows, 2 * pair:3 * pair] += tn(weight.astype(bf16), numer)
+            return carry
+
+        lax.fori_loop(0, models, body, 0)
+
+    attend_back(plan.inner)
+    for i in (2, 3):
+        arrive(back[i])
+        back[i] = reduce_first(chunks[i])
+    back_wait()
+    attend_back(plan.outer)
+    for i in (2, 3):
+        arrive(back[i])
+        back[i] = reduce_second(chunks[i])
+
+    normed_t = normed[...].T
+    qkv_shape = grads.shape[1:5] + (qkv,)
+    query_scale = jnp.where(lax.broadcasted_iota(jnp.int32, (1, qkv), 1) < pair, HD ** -0.5, 1.0)
+
+    acc[...] = jnp.zeros(acc.shape, f32)
+
+    def finish(m, carry):
+        coarse = coarse_rows(m, qkv, pl.ds(pl.multiple_of(plan.upper + slot_row, NR), NR))
+        spread = spread_out(coarse * jnp.concatenate([inverse[...]] * 3, axis=1))
+        rows = (work[m, NR:NR + part, :] + jnp.where(valid, spread, 0.0)).astype(bf16)
+        grads[m, :, :, :, :, 0:qkv] = (nn(normed_t, rows) * query_scale).astype(bf16).reshape(qkv_shape)
+        acc[...] += nt(rows, weight_cols(m, 0, qkv))
+        return carry
+
+    lax.fori_loop(0, models, finish, 0)
+    normed_grad = acc[...]
+    for i in (0, 1):
+        back[i] = reduce_core(chunks[i])
+    for i in (2, 3):
+        arrive(back[i])
+        back[i] = reduce_z(chunks[i])
+    hat = scaled[...]
+    row_grads[...] = (residual[...] + norm_back(normed_grad, hat, rstd[:, 0:1], pre_gain)).astype(bf16)
+    grads_out = rows_home(row_grads, out_grads)
+    norm_sums = [jnp.sum(normed_grad * hat, axis=0, keepdims=True), jnp.sum(normed_grad, axis=0, keepdims=True)] + norm_sums
+    norm_got[0] = jnp.concatenate(norm_sums + [jnp.zeros((4, width), f32)], axis=0)
+    norm_peers = [[c_peer], [y_peer], [x_peer], [device(ax, ay, ac, (az + step) % models) for step in range(1, models)]]
+
+    def norm_send(stage):
+        first = 1 + 2 * stage
+        return [send(norm_got.at[2 * stage], norm_got.at[first + i], to) for i, to in enumerate(norm_peers[stage])]
+
+    def norm_sum(stage):
+        total = norm_got[2 * stage]
+        for i in range(len(norm_peers[stage])):
+            total = total + norm_got[1 + 2 * stage + i]
+        return total
+
+    small = norm_send(0)
+    stages = [reduce_first, reduce_second, reduce_z]
+    for step, stage in enumerate(stages):
+        for i in (0, 1):
+            arrive(back[i])
+            back[i] = stage(chunks[i])
+        arrive(small)
+        norm_got[2 * step + 2] = norm_sum(step)
+        small = norm_send(step + 1)
+    for i in (2, 3, 0, 1):
+        arrive(back[i])
+        reduce_end(chunks[i])
+    arrive(small)
+    norm_grads[...] = norm_sum(3)
+    arrive(rows_out)
+    arrive(grads_out)
+    for c, _ in sent:
+        c.wait_send()
+    rims_done()
+    back_done()
+
+
+def fast_body(plan, incoming_embeddings, output_sensitivity, sequence_extents, asking_projector, lookup_projector,
+              content_projector, attention_combiner, feedforward_expand, feedforward_contract,
+              attention_norm_scale, attention_norm_bias, feedforward_norm_scale, feedforward_norm_bias):
+    bf16, f32 = jnp.bfloat16, jnp.float32
+    models = lax.axis_size("mp")
+    seqs, _, part, width = incoming_embeddings.shape
+    strip, pair = asking_projector.shape
+    hidden = feedforward_expand.shape[1]
+    owner = lax.axis_index("dp") * lax.axis_size("seq") + lax.axis_index("seq")
+    own_weights = jnp.concatenate(
+        [asking_projector * jnp.asarray(HD ** -0.5, bf16), lookup_projector, content_projector,
+         attention_combiner.T, feedforward_expand, feedforward_contract.T], axis=1)
+    columns = own_weights.shape[1]
+    norm_parts = jnp.stack([attention_norm_scale, attention_norm_bias, feedforward_norm_scale, feedforward_norm_bias])
+    own_norms = lax.dynamic_update_slice(
+        jnp.zeros((8, width), f32), norm_parts.astype(f32), (0, owner * strip))
+    share = part // models
+    spots, rows = plan.spots, plan.rows
+    deep = (2, 2, 2, strip, columns)
+    net_count = 128
+    vmem = pltpu.VMEM
+    scratch = [
+        vmem((models,) + deep, bf16), vmem((spots, 8, width), f32), vmem((part, width), bf16), vmem((part, width), bf16),
+        vmem((models, rows, 3 * pair), bf16), vmem((len(plan.tiles), 128, 128), f32),
+        vmem((part, part), bf16), vmem((part, part), bf16), vmem((part, 128), f32), vmem((models, rows, 3 * pair), f32),
+        vmem((models, part, pair), bf16), vmem((models, part, pair), f32), vmem((models, part, pair), f32),
+        vmem((part, width), bf16), vmem((part, width), f32), vmem((part, 128), f32),
+        vmem((models, rows, pair), bf16), vmem((rows, 128), bf16), vmem((part, width), f32), vmem((part, width), f32),
+        vmem((part, width), f32), vmem((part, 128), f32), vmem((part, width), bf16), vmem((part, width), bf16),
+        vmem((models,) + deep, bf16), vmem((models, 2, 2, strip, columns), bf16), vmem((models, 2, strip, columns), bf16),
+        vmem((models, strip, columns), bf16), vmem((models - 1, strip, columns), bf16), vmem((10, 8, width), f32),
+        pltpu.SemaphoreType.DMA((2,)), pltpu.SemaphoreType.DMA((net_count,)), pltpu.SemaphoreType.DMA((net_count,)),
+    ]
+    any_space, in_vmem = pl.BlockSpec(memory_space=pl.ANY), pl.BlockSpec(memory_space=pltpu.VMEM)
+    out_rows, out_grads, weight_grads, norm_grads = pl.pallas_call(
+        functools.partial(whole_layer, plan, (part, width, pair, hidden), net_count),
+        out_shape=(jax.ShapeDtypeStruct((seqs, share, width), bf16), jax.ShapeDtypeStruct((seqs, share, width), bf16),
+                   jax.ShapeDtypeStruct((strip, columns), f32), jax.ShapeDtypeStruct((8, width), f32)),
+        in_specs=[pl.BlockSpec(memory_space=pltpu.SMEM), in_vmem, in_vmem, any_space, any_space],
+        out_specs=(in_vmem,) * 4,
+        scratch_shapes=scratch,
+        compiler_params=pltpu.CompilerParams(collective_id=0, has_side_effects=True, vmem_limit_bytes=60 * 2 ** 20),
+        name="layer",
+    )(sequence_extents, own_weights, own_norms, incoming_embeddings, output_sensitivity)
+    ends = [0, pair, 2 * pair, 3 * pair, 4 * pair, 4 * pair + hidden, columns]
+    query_grad, key_grad, value_grad, merge_t, up_grad, down_t = (
+        weight_grads[:, low:high] for low, high in zip(ends, ends[1:]))
+    mine = lax.dynamic_slice(norm_grads, (0, owner * strip), (4, strip))
+    return (out_rows[:, None], out_grads[:, None], query_grad, key_grad, value_grad, merge_t.T, up_grad, down_t.T,
+            mine[0], mine[1], mine[2], mine[3])
 
 
 def solution(mesh):
@@ -569,4 +1271,12 @@
         P(("dp", "seq")),
         P(("dp", "seq")),
     )
-    return jax.shard_map(body, mesh=mesh, in_specs=in_specs, out_specs=out_specs, check_vma=False)
+    sizes = (mesh.shape["dp"], mesh.shape["seq"], mesh.shape["mp"])
+
+    def chosen(*arrays):
+        seqs, _, part, width = arrays[0].shape
+        if sizes == (2, 4, 4) and seqs == sizes[2] and part == width == 512 and arrays[3].shape[1] == 128:
+            return fast_body(Plan(part, sizes[0] * sizes[1]), *arrays)
+        return general_body(*arrays)
+
+    return jax.shard_map(chosen, mesh=mesh, in_specs=in_specs, out_specs=out_specs, check_vma=False)

time: 1520 us -> 153 us (0.10)
  local copies, waits for them, and re-layouts: 472 us -> 12.1 us
  other arithmetic: 294 us -> 1.44 us
  matrix products: 270 us -> 0 us
  waiting for transfers between devices: 223 us -> 0 us
  blocking collectives: 175 us -> 0 us
  Pallas kernels: 0 us -> 138 us
  starting transfers between devices: 47.2 us -> 0 us
  between operations: 22.6 us -> 0.7 us
    dot_general x252 -> x0, matrix products: 270 us -> none  [the longest x84 125 us: dot_outer(): lax.dot_general(left_mat, right_mat, (((1,), (1,)), ((), ())), preferred_...]
    psum x3 -> x0, waiting for transfers between devices: 194 us -> none  [the longest x1 103 us: one_batch(): branch_attn = lax.psum(merged_part, 'mp')]
    reshape x136 -> x0, local copies, waits for them, and re-layouts: 175 us -> none  [the longest x18 52.7 us: one_batch(): jnp.repeat(coarse_grad, 2 ** level_at, axis=0) * valid_rows[:, None]]
    all_gather x16 -> x0, blocking collectives: 150 us -> none  [the longest x2 28 us: one_batch(): lax.all_gather(edge_rows.astype(jnp.float32).astype(jnp.bfloat16), 'seq',...]
    pallas_call x0 -> x1, Pallas kernels: none -> 138 us  [fast_body(): pl.pallas_call(functools.partial(whole_layer, plan, (part, width, pair, h...]
    reduce_sum x66 -> x0, other arithmetic: 120 us -> none  [the longest x40 88.7 us: group_sum(): jnp.sum(values.reshape((values.shape[0] // group_width, group_width) + va...]
    broadcast_in_dim x126 -> x1, local copies, waits for them, and re-layouts: 72.5 us -> 0.01 us  [fast_body(): jnp.zeros((8, width), f32)]
    all_to_all x12 -> x0, starting transfers between devices: 47 us -> none  [the longest x8 29.7 us: summed_on_arrival(): blocks = lax.all_to_all(cut_along(x, dim, count), axis, 0, 0, tiled=True)]
  transfers between devices with their start and end apart: 17 -> 0, of which waited for: 11 -> 0; matrix products, arithmetic and copies ran while one was open for 44% -> 0% of each run, Pallas kernels for 0% -> 0%
where the time goes in v1:
time: 153 us; the launch traced here: 152 us
  Pallas kernels  138 us (90%)
  local copies, waits for them, and re-layouts  12.1 us (8%)
    pallas_call x1, Pallas kernels, fast_body(): pl.pallas_call(functools.partial(whole_layer, plan, (part, width, pair, h...  138 us
    unnamed x12, local copies, waits for them, and re-layouts  6.37 us
    transpose x2, local copies, waits for them, and re-layouts, fast_body(): return (out_rows[:, None], out_grads[:, None], query_grad, key_grad, valu...  3.14 us

profile of v1, /device:TPU:0, one launch (start us, length us, event | category | flops | bytes accessed | tf_op | source)
XLA Modules:
  0.0 152.0 jit_solution(11916429992634668179)
XLA Ops:
  0.7 0.7 maximum_convert_fusion
  1.4 0.4 dynamic_update_slice.3.refs_2_
  1.8 0.0 copy-start.2
  1.8 0.7 multiply_dynamic-update-slice_fusion
  2.5 0.7 constant_dynamic-update-slice_fusion.2
  3.2 0.7 constant_dynamic-update-slice_fusion.1
  4.0 0.7 bitcast_dynamic-update-slice_fusion.1
  4.7 0.8 constant_dynamic-update-slice_fusion
  5.5 0.8 bitcast_dynamic-update-slice_fusion.refs_1_
  6.4 0.0 copy-done.2
  6.4 0.0 copy-start.1
  6.4 0.7 copy-done.1
  7.0 137.8 %layer.1 = (bf16[4,128,512]{2,1,0:T(8,128)(2,1)}, bf16[4,128,512]{2,1,0:T(8,128)(2,1)}, f32[64,1536]{1,0:T(8,128)}, f32[8,512]{1,0:T(8,128)}) custom-call(s32[4]{0:T(128)} %refs_0_.1, bf16[64,1536]{1,0:T(8,128)(2,1)} %copy-done.1, f32[8,512]{1,0:T(8,128)} %copy-done.2, bf16[4,1,512,512]{3,2,1,0:T(8,128)(2,1)} %refs_3_.1, bf16[4,1,512,512]{3,2,1,0:T(8,128)(2,1)} %refs_4_.1), custom_call_target="tpu_custom_call" | custom-call | tf_op jit(solution)/shard_map/layer/pallas_call | solution.py:1226
  144.9 0.0 copy-start
  144.9 0.8 constant_dynamic-slice_fusion
  145.7 0.5 slice_bitcast_fusion.2
  146.2 1.5 slice_bitcast_fusion.1
  147.7 1.7 %slice_bitcast_fusion = (f32[512,64]{0,1:T(8,128)}, f32[64,512]{1,0:T(8,128)}) fusion(f32[64,1536]{1,0:T(8,128)} %get-tuple-element.18), kind=kLoop, calls=%fused_computation | loop fusion | bytes 524288 | tf_op jit(solution)/shard_map/transpose | solution.py:1240
  149.4 1.9 %copy.35 = bf16[4,1,128,512]{3,2,1,0:T(8,128)(2,1)} copy(bf16[4,1,128,512]{3,2,1,0:T(8,128)(2,1)} %bitcast.27) | data formatting | bytes 1048576
  151.2 0.0 copy-done
  151.2 0.8 copy.36
  (1 shorter events, 0.0 us)
Async XLA Ops:
  1.8 4.6 %copy-start.2 = (f32[8,512]{1,0:T(8,128)}, f32[8,512]{1,0:T(8,128)S(1)}, u32[]{:S(2)}) copy-start(f32[8,512]{1,0:T(8,128)S(1)} %dynamic_update_slice.3.refs_2_) | copy-start | bytes 49156
  6.4 0.7 copy-start.1
  144.9 6.4 %copy-start = (bf16[4,128,512]{2,1,0:T(8,128)(2,1)S(1)}, bf16[4,128,512]{2,1,0:T(8,128)(2,1)}, u32[]{:S(2)}) copy-start(bf16[4,128,512]{2,1,0:T(8,128)(2,1)} %get-tuple-element.17) | copy-start | bytes 1572868

commit v2 on v1

--- a/solution.py
+++ b/solution.py
@@ -602,6 +602,15 @@
         self.outer.append((self.upper, 128, self.upper, None))
         self.tiles = self.inner + self.outer
 
+    def own_pieces(self, tile):
+        first, count = tile[:2]
+        pieces = []
+        for start, rows in zip(self.at, self.own):
+            low, high = max(first, start + NR), min(first + count, start + NR + rows)
+            if low < high:
+                pieces.append((low, high - low))
+        return pieces
+
 
 def row_places(plan, rows, low, high, spot):
     level = jnp.full(rows.shape, -1, jnp.int32)
@@ -655,16 +664,45 @@
     return low, size
 
 
+def spread_columns(rows, place, count):
+    width = rows.shape[1]
+    source = lax.broadcasted_iota(jnp.int32, (width, width * count), 0)
+    target = lax.broadcasted_iota(jnp.int32, (width, width * count), 1)
+    return nn(rows, jnp.where(target == source + place * width, 1.0, 0.0).astype(rows.dtype))
+
+
+def flipped(rows):
+    size = rows.shape[1]
+    row = lax.broadcasted_iota(jnp.int32, (size, size), 0)
+    col = lax.broadcasted_iota(jnp.int32, (size, size), 1)
+    return nt(jnp.where(row == col, 1.0, 0.0).astype(rows.dtype), rows).astype(rows.dtype)
+
+
+def flip_bits(value, k):
+    low, high, k_low, k_high = value % 2, value // 2, k % 2, k // 2
+    return (high + k_high - 2 * high * k_high) * 2 + low + k_low - 2 * low * k_low
+
+
+class Marks:
+    def __init__(self):
+        self.used = 0
+
+    def take(self, count):
+        self.used += count
+        return self.used - count
+
+
 def whole_layer(plan, dims, net_count, *refs):
-    (extents, own_weights, own_norms, tokens_in, cotangent_in,
+    (extents, w_query, w_key, w_value, w_merge, w_expand, w_contract, norm_parts, tokens_in, cotangent_in,
      out_rows, out_grads, weight_grads, norm_grads,
      weights, norms, tokens, cotangent, ext, logs, pool, unpool, inverse, work,
      attended, ratio, recip, normed, scaled, rstd, grad_ext, total_ext, residual, acc, acc2, totals, result, row_grads,
-     grads, got1, got2, got3, got4, norm_got,
+     active, slope, grads, got1, got2, got3, got4, norm_got,
      load_sem, send_sem, recv_sem) = refs
     part, width, pair, hidden = dims
     f32, bf16 = jnp.float32, jnp.bfloat16
     models = weights.shape[0]
+    strip, columns = weights.shape[4:]
     ax, sq, az = lax.axis_index("dp"), lax.axis_index("seq"), lax.axis_index("mp")
     ay, ac = sq // 2, sq % 2
     spot = sq * 2 + ax
@@ -678,85 +716,106 @@
     def at_spot(place):
         return (place % 2, place // 2, az)
 
+    def plane(k):
+        return flip_bits(az, k)
+
+    x_peer, y_peer, c_peer = device(1 - ax, ay, ac, az), device(ax, 1 - ay, ac, az), device(ax, ay, 1 - ac, az)
+    z_peer = lambda k: device(ax, ay, ac, plane(k))
+
     barrier = pltpu.get_barrier_semaphore()
     for step in range(1, spots):
         pl.semaphore_signal(barrier, inc=1, device_id=at_spot((spot + step) % spots), device_id_type=MESH)
-    for step in range(1, models):
-        pl.semaphore_signal(barrier, inc=1, device_id=device(ax, ay, ac, (az + step) % models), device_id_type=MESH)
+    for k in range(1, models):
+        pl.semaphore_signal(barrier, inc=1, device_id=z_peer(k), device_id_type=MESH)
     load_tokens = pltpu.make_async_copy(tokens_in.at[az, 0], tokens, load_sem.at[0])
     load_cotangent = pltpu.make_async_copy(cotangent_in.at[az, 0], cotangent, load_sem.at[1])
     load_tokens.start()
     load_cotangent.start()
-    weights[az, ax, ay, ac] = own_weights[...]
-    norms[spot] = own_norms[...]
+    own = (az, ax, ay, ac)
+    weights[own + (slice(None), slice(0, pair))] = w_query[...] * jnp.asarray(HD ** -0.5, bf16)
+    weights[own + (slice(None), slice(pair, 2 * pair))] = w_key[...]
+    weights[own + (slice(None), slice(2 * pair, qkv))] = w_value[...]
+    weights[own + (slice(None), slice(qkv, qkv + pair))] = flipped(w_merge[...])
+    weights[own + (slice(None), slice(4 * pair, 4 * pair + hidden))] = w_expand[...]
+    weights[own + (slice(None), slice(4 * pair + hidden, columns))] = flipped(w_contract[...])
+    owner = ax * 4 + sq
+    norms[spot] = spread_columns(norm_parts[...], owner, width // strip)
     pl.semaphore_wait(barrier, spots - 1 + models - 1)
 
-    used = [0]
-    sent = []
-
-    def copy(src, dst, to):
-        i = used[0]
-        used[0] += 1
-        assert i < net_count
+    marks = Marks()
+
+    def copy(i, src, dst, to):
         return pltpu.make_async_remote_copy(
             src_ref=src, dst_ref=dst, send_sem=send_sem.at[i], recv_sem=recv_sem.at[i],
             device_id=to, device_id_type=MESH)
 
-    def send(src, dst, to):
-        c = copy(src, dst, to)
+    sent = []
+
+    def send(i, src, dst, to):
+        c = copy(i, src, dst, to)
         c.start()
-        sent.append((c, None))
+        sent.append(c)
         return c
-
-    x_peer = device(1 - ax, ay, ac, az)
-    y_peer = device(ax, 1 - ay, ac, az)
-    c_peer = device(ax, ay, 1 - ac, az)
-
-    chunks = [(0, 2 * pair, True), (2 * pair, 2 * pair, False),
-              (4 * pair, hidden, True), (4 * pair + hidden, hidden, False)]
-
-    def gather_z(chunk):
-        col, count, _ = chunk
-        cols = pl.ds(col, count)
-        place = weights.at[az, ax, ay, ac, :, cols]
-        return [send(own_weights.at[:, cols], place, device(ax, ay, ac, (az + step) % models))
-                for step in range(1, models)]
-
-    def gather_first(chunk):
-        col, count, x_first = chunk
-        block = weights.at[:, ax, ay, ac, :, pl.ds(col, count)]
-        return [send(block, block, x_peer if x_first else y_peer)]
-
-    def gather_second(chunk):
-        col, count, x_first = chunk
-        cols = pl.ds(col, count)
-        block = weights.at[:, :, ay, ac, :, cols] if x_first else weights.at[:, ax, :, ac, :, cols]
-        return [send(block, block, y_peer if x_first else x_peer)]
-
-    def gather_core(chunk):
-        col, count, _ = chunk
-        block = weights.at[:, :, :, ac, :, pl.ds(col, count)]
-        return [send(block, block, c_peer)]
 
     def arrive(copies):
         for c in copies:
             c.wait_recv()
 
-    norm_copies = [send(own_norms, norms.at[spot], at_spot((spot + step) % spots)) for step in range(1, spots)]
-    flight = [gather_z(chunk) for chunk in chunks]
+    class Gather:
+        def __init__(self, col, count, through_y):
+            self.cols, self.rows = pl.ds(col, count), through_y
+            self.flight = {}
+
+        def block(self, k, x, y, rows=slice(None)):
+            return weights.at[plane(k), x, y, ac, rows, self.cols]
+
+        def to_planes(self):
+            here = self.block(0, ax, ay)
+            for k in range(1, models):
+                self.flight["z", k] = [send(marks.take(1), here, here, z_peer(k))]
+
+        def to_sides(self, k):
+            if k:
+                arrive(self.flight["z", k])
+            here = self.block(k, ax, ay)
+            self.flight["side", k] = [send(marks.take(1), here, here, x_peer), send(marks.take(1), here, here, y_peer)]
+
+        def to_corner(self, k):
+            arrive(self.flight["side", k])
+            first = self.block(k, 1 - ax, ay, pl.ds(0, self.rows))
+            rest = self.block(k, ax, 1 - ay, pl.ds(self.rows, strip - self.rows))
+            self.flight["corner", k] = [send(marks.take(1), first, first, y_peer), send(marks.take(1), rest, rest, x_peer)]
+
+        def to_core(self, k):
+            arrive(self.flight["corner", k])
+            here = weights.at[plane(k), :, :, ac, :, self.cols]
+            self.flight["core", k] = [send(marks.take(1), here, here, c_peer)]
+
+        def here(self, k):
+            arrive(self.flight["core", k])
+
+    first_gather = Gather(0, qkv, 32)
+    merge_gather = Gather(qkv, pair + hidden, 48)
+    last_gather = Gather(4 * pair + hidden, hidden, 48)
+
+    first_gather.to_planes()
+    first_gather.to_sides(0)
+    norm_copies = [send(marks.take(1), norms.at[spot], norms.at[spot], at_spot((spot + step) % spots))
+                   for step in range(1, spots)]
 
     low, size = pool_bounds(plan, (part, 128), 0)
     for block in range(part // 128):
         token_at = block * 128 + lax.broadcasted_iota(jnp.int32, (part, 128), 1)
         member = (token_at >= low) & (token_at < low + size) & (token_at + spot * part < length)
         pool[:, block * 128:(block + 1) * 128] = jnp.where(member, 1.0, 0.0).astype(bf16)
-    first_token = spot * part + low
-    counts = jnp.clip(length - first_token, 0, size)
+    counts = jnp.clip(length - spot * part - low, 0, size)
     inverse[...] = 1.0 / jnp.maximum(counts, 1).astype(f32)
     low, size = pool_bounds(plan, (8, part), 1)
     token_at = lax.broadcasted_iota(jnp.int32, (part, part), 0)
     member = (token_at >= low[:1]) & (token_at < (low + size)[:1])
     unpool[...] = jnp.where(member, 1.0, 0.0).astype(bf16)
+    first_gather.to_corner(0)
+    first_gather.to_sides(1)
     load_tokens.wait()
 
     def statistics(values):
@@ -768,128 +827,110 @@
     xhat, scale = statistics(tokens[...].astype(f32))
     scaled[...] = xhat
     rstd[...] = jnp.broadcast_to(scale, (part, 128))
-    arrive(flight[0])
-    flight[0] = gather_first(chunks[0])
-    arrive(flight[1])
-    flight[1] = gather_first(chunks[1])
+    first_gather.to_sides(2)
+    first_gather.to_sides(3)
+    merge_gather.to_planes()
+    first_gather.to_core(0)
+    first_gather.to_corner(1)
     for i, tile in enumerate(plan.tiles):
         logs[i, 0:tile[1]] = log_counts(plan, tile, spot, length)
+    first_gather.to_corner(2)
+    first_gather.to_corner(3)
+    merge_gather.to_sides(0)
+    first_gather.to_core(1)
     arrive(norm_copies)
     gains = norms[0]
     for i in range(1, spots):
         gains = gains + norms[i]
     pre_gain, pre_shift, mid_gain, mid_shift = (gains[i:i + 1] for i in range(4))
     normed[...] = (scaled[...] * pre_gain + pre_shift).astype(bf16)
-    for i in (0, 1):
-        arrive(flight[i])
-        flight[i] = gather_second(chunks[i])
-    for i in (0, 1):
-        arrive(flight[i])
-        flight[i] = gather_core(chunks[i])
-    for i in (2, 3):
-        arrive(flight[i])
-        flight[i] = gather_first(chunks[i])
+    first_gather.to_core(2)
+    first_gather.to_core(3)
+    last_gather.to_planes()
+
+    is_first, is_last = spot == 0, spot == spots - 1
+
+    @pl.when(is_first)
+    def _():
+        for lv in range(plan.levels):
+            rows = slice(plan.at[lv], plan.at[lv] + NR)
+            ext[:, rows, :] = jnp.zeros((models, NR, qkv), bf16)
+            grad_ext[:, rows, :] = jnp.zeros((models, NR, pair), bf16)
+            total_ext[rows, :] = jnp.zeros((NR, 128), bf16)
+
+    @pl.when(is_last)
+    def _():
+        for lv in range(plan.levels):
+            end = plan.at[lv] + NR + plan.own[lv]
+            rows = slice(end, end + NR)
+            ext[:, rows, :] = jnp.zeros((models, NR, qkv), bf16)
+            grad_ext[:, rows, :] = jnp.zeros((models, NR, pair), bf16)
+            total_ext[rows, :] = jnp.zeros((NR, 128), bf16)
 
     def weight_cols(m, col, count):
         return weights[m, :, :, :, :, col:col + count].reshape(width, count)
 
-    arrive(flight[0])
-    arrive(flight[1])
-
-    def project(m, carry):
+    slot_row = pl.multiple_of(spot * NR, NR)
+    own_slot_rows = pl.ds(pl.multiple_of(plan.upper + slot_row, NR), NR)
+    per_rim = plan.levels * 2 + spots - 1
+
+    class Rims:
+        def __init__(self, view, base):
+            right, left = at_spot((spot + 1) % spots), at_spot((spot + spots - 1) % spots)
+            self.to_right, self.to_left, self.to_all = [], [], []
+            for lv in range(plan.levels):
+                start, rows = plan.at[lv], plan.own[lv]
+                self.to_right.append(copy(base + 2 * lv, view(pl.ds(start + rows, NR)), view(pl.ds(start, NR)), right))
+                self.to_left.append(copy(base + 2 * lv + 1, view(pl.ds(start + NR, NR)), view(pl.ds(start + NR + rows, NR)), left))
+            block = view(own_slot_rows)
+            for step in range(1, spots):
+                self.to_all.append(copy(base + 2 * plan.levels + step - 1, block, block, at_spot((spot + step) % spots)))
+
+        def each(self, verb, not_first, not_last):
+            @pl.when(jnp.logical_not(is_last))
+            def _():
+                for c in not_last:
+                    getattr(c, verb)()
+
+            @pl.when(jnp.logical_not(is_first))
+            def _():
+                for c in not_first:
+                    getattr(c, verb)()
+
+            for c in self.to_all:
+                getattr(c, verb)()
+
+        def start(self):
+            self.each("start", self.to_left, self.to_right)
+
+        def wait(self):
+            self.each("wait_recv", self.to_right, self.to_left)
+
+        def done(self):
+            self.each("wait_send", self.to_left, self.to_right)
+
+    pair_base = marks.take(models * per_rim)
+    query_base = marks.take(per_rim)
+    grad_base = marks.take(models * per_rim)
+    total_base = marks.take(per_rim)
+    pair_rims = lambda k: Rims(lambda rows: ext.at[plane(k), rows, pl.ds(pair, 2 * pair)], pair_base + k * per_rim)
+    query_rims = lambda: Rims(lambda rows: ext.at[:, rows, pl.ds(0, pair)], query_base)
+    grad_rims = lambda k: Rims(lambda rows: grad_ext.at[plane(k), rows, :], grad_base + k * per_rim)
+    total_rims = lambda: Rims(lambda rows: total_ext.at[rows, :], total_base)
+
+    for k in range(models):
+        first_gather.here(k)
+        m = plane(k)
         rows = nn(normed[...], weight_cols(m, 0, qkv)).astype(bf16)
         ext[m, NR:NR + part, :] = rows
-        sums = nn(pool[...], rows)
-        means = (sums * jnp.concatenate([inverse[...]] * 3, axis=1)).astype(bf16)
+        means = (nn(pool[...], rows) * jnp.concatenate([inverse[...]] * 3, axis=1)).astype(bf16)
         for lv in range(1, plan.levels):
             ext[m, plan.at[lv] + NR:plan.at[lv] + NR + plan.own[lv], :] = means[plan.pool_at[lv]:plan.pool_at[lv] + plan.own[lv]]
-        ext[m, pl.ds(plan.upper + spot * NR, NR), :] = means[plan.pool_upper:plan.pool_upper + NR]
-        return carry
-
-    lax.fori_loop(0, models, project, 0)
-
-    is_first, is_last = spot == 0, spot == spots - 1
-
-    def exchange(arrays):
-        pending = []
-        for ref in arrays:
-            lead = (slice(None),) * (len(ref.shape) - 2)
-            for lv in range(plan.levels):
-                start, rows = plan.at[lv], plan.own[lv]
-                to_right = copy(ref.at[lead + (pl.ds(start + rows, NR), slice(None))],
-                                ref.at[lead + (pl.ds(start, NR), slice(None))], at_spot((spot + 1) % spots))
-                to_left = copy(ref.at[lead + (pl.ds(start + NR, NR), slice(None))],
-                               ref.at[lead + (pl.ds(start + NR + rows, NR), slice(None))],
-                               at_spot((spot + spots - 1) % spots))
-                pending.append((to_right, to_left))
-        uppers = []
-        for ref in arrays:
-            lead = (slice(None),) * (len(ref.shape) - 2)
-            block = ref.at[lead + (pl.ds(plan.upper + spot * NR, NR), slice(None))]
-            for step in range(1, spots):
-                uppers.append(copy(block, block, at_spot((spot + step) % spots)))
-
-        @pl.when(jnp.logical_not(is_last))
-        def _():
-            for to_right, _ in pending:
-                to_right.start()
-
-        @pl.when(jnp.logical_not(is_first))
-        def _():
-            for _, to_left in pending:
-                to_left.start()
-
-        for c in uppers:
-            c.start()
-
-        @pl.when(is_first)
-        def _():
-            for ref in arrays:
-                lead = (slice(None),) * (len(ref.shape) - 2)
-                for lv in range(plan.levels):
-                    place = lead + (slice(plan.at[lv], plan.at[lv] + NR), slice(None))
-                    ref[place] = jnp.zeros(ref.shape[:-2] + (NR, ref.shape[-1]), ref.dtype)
-
-        @pl.when(is_last)
-        def _():
-            for ref in arrays:
-                lead = (slice(None),) * (len(ref.shape) - 2)
-                for lv in range(plan.levels):
-                    row = plan.at[lv] + NR + plan.own[lv]
-                    ref[lead + (slice(row, row + NR), slice(None))] = jnp.zeros(
-                        ref.shape[:-2] + (NR, ref.shape[-1]), ref.dtype)
-
-        def wait():
-            @pl.when(jnp.logical_not(is_first))
-            def _():
-                for to_right, _ in pending:
-                    to_right.wait_recv()
-
-            @pl.when(jnp.logical_not(is_last))
-            def _():
-                for _, to_left in pending:
-                    to_left.wait_recv()
-
-            for c in uppers:
-                c.wait_recv()
-
-        def done():
-            @pl.when(jnp.logical_not(is_last))
-            def _():
-                for to_right, _ in pending:
-                    to_right.wait_send()
-
-            @pl.when(jnp.logical_not(is_first))
-            def _():
-                for _, to_left in pending:
-                    to_left.wait_send()
-
-            for c in uppers:
-                c.wait_send()
-
-        return wait, done
-
-    rims_wait, rims_done = exchange([ext])
+        ext[m, own_slot_rows, :] = means[plan.pool_upper:plan.pool_upper + NR]
+        pair_rims(k).start()
+
+    for k in range(1, models):
+        merge_gather.to_sides(k)
 
     lane = lax.broadcasted_iota(jnp.int32, (1, pair), 1)
     left_head = lane < HD
@@ -903,42 +944,53 @@
         return jnp.where(left_head, rows[:half], rows[half:])
 
     ones = jnp.ones((128, 128), bf16)
-    slot_row = pl.multiple_of(spot * NR, NR)
-
-    def tile_weights(m, index, rows_at, count, window, own_slot=False):
-        queries = both_heads(ext[m, rows_at, 0:pair])
+
+    def stacked(parts):
+        return parts[0] if len(parts) == 1 else jnp.concatenate(parts, axis=0)
+
+    def tile_weights(m, rows, mask, window):
+        queries = both_heads(rows)
         keys = ext[m, window:window + 128, pair:2 * pair]
         values = jnp.concatenate([ext[m, window:window + 128, 2 * pair:3 * pair], ones], axis=1)
-        mask = logs[index, pl.ds(slot_row, NR)] if own_slot else logs[index, 0:count]
         weight = jnp.exp(nt(queries, keys) + jnp.concatenate([mask, mask], axis=0))
         return queries, keys, values, weight
 
-    def attend(tiles):
-        def body(m, carry):
+    def attend(tiles, first_k, last_k, wait_rims):
+        def body(k, carry):
+            m = plane(k)
+            if wait_rims:
+                pair_rims(k).wait()
             for tile in tiles:
-                first, count, window, _ = tile
-                own_slot = first == plan.upper
-                if own_slot:
-                    rows_at, count = pl.ds(pl.multiple_of(plan.upper + slot_row, NR), NR), NR
+                first, _, window, _ = tile
+                index = plan.tiles.index(tile)
+                if first == plan.upper:
+                    pieces = [(first, NR)]
+                    rows, mask = ext[m, own_slot_rows, 0:pair], logs[index, pl.ds(slot_row, NR)]
                 else:
-                    rows_at = slice(first, first + count)
-                _, _, values, weight = tile_weights(m, plan.tiles.index(tile), rows_at, count, window, own_slot)
+                    pieces = plan.own_pieces(tile)
+                    rows = stacked([ext[m, low:low + count, 0:pair] for low, count in pieces])
+                    mask = stacked([logs[index, low - first:low - first + count] for low, count in pieces])
+                _, _, values, weight = tile_weights(m, rows, mask, window)
                 both = nn(weight.astype(bf16), values)
-                work[m, first:first + count, 0:pair] = joined(both[:, :128])
-                work[m, first:first + count, pair:2 * pair] = joined(both[:, 128:])
+                numer, tot = joined(both[:, :128]), joined(both[:, 128:])
+                at = 0
+                for low, count in pieces:
+                    work[m, low:low + count, 0:pair] = numer[at:at + count]
+                    work[m, low:low + count, pair:2 * pair] = tot[at:at + count]
+                    at += count
             return carry
 
-        lax.fori_loop(0, models, body, 0)
-
-    attend(plan.inner)
-    for i in (2, 3):
-        arrive(flight[i])
-        flight[i] = gather_second(chunks[i])
-    rims_wait()
-    attend(plan.outer)
-    for i in (2, 3):
-        arrive(flight[i])
-        flight[i] = gather_core(chunks[i])
+        lax.fori_loop(first_k, last_k, body, 0)
+
+    attend(plan.inner, 0, models, False)
+    attend(plan.outer, 0, 2, True)
+    for k in range(models):
+        merge_gather.to_corner(k)
+    for k in range(models):
+        last_gather.to_sides(k)
+    attend(plan.outer, 2, models, True)
+    for k in range(models):
+        merge_gather.to_core(k)
 
     def coarse_rows(m, cols, slot_at):
         rows = [work[m, plan.at[lv] + NR:plan.at[lv] + NR + plan.own[lv], 0:cols] for lv in range(1, plan.levels)]
@@ -959,8 +1011,12 @@
         return carry
 
     lax.fori_loop(0, models, normalise, 0)
+    for k in range(models):
+        last_gather.to_corner(k)
 
     residual[...] = tokens[...].astype(f32)
+    for k in range(models):
+        merge_gather.here(k)
 
     def merge(m, carry):
         residual[...] += nt(attended[m], weight_cols(m, qkv, pair))
@@ -976,72 +1032,124 @@
     valid = row_at < length
     out_grad = jnp.where(valid, cotangent[...], jnp.zeros((), bf16))
     out_grad_t = out_grad.T
-    arrive(flight[2])
-    arrive(flight[3])
     acc[...] = jnp.zeros(acc.shape, f32)
     acc2[...] = jnp.zeros(acc.shape, f32)
     block_shape = grads.shape[1:5] + (hidden,)
 
-    def feed(m, carry):
-        expand = weight_cols(m, 4 * pair, hidden)
+    def feed_up(m, carry):
+        up = nn(mid, weight_cols(m, 4 * pair, hidden))
+        phi = 0.5 + 0.5 * lax.erf(up * (0.5 ** 0.5))
+        active[m] = (up * phi).astype(bf16)
+        slope[m] = phi + up * (jnp.exp(-0.5 * up * up) * 0.3989422804014327)
+        return carry
+
+    lax.fori_loop(0, models, feed_up, 0)
+    for k in range(models):
+        last_gather.to_core(k)
+    query_rims().start()
+
+    class Reduce:
+        def __init__(self, col, count):
+            self.cols = pl.ds(col, count)
+            self.core = marks.take(models)
+            self.side = marks.take(2 * models)
+            self.corner = marks.take(2 * models)
+            self.z = marks.take(models)
+
+        def core_copy(self, k):
+            m = plane(k)
+            return copy(self.core + k, grads.at[m, :, :, 1 - ac, :, self.cols], got1.at[m, :, :, :, self.cols], c_peer)
+
+        def side_copies(self, k):
+            m = plane(k)
+            return [copy(self.side + 2 * k, got1.at[m, 1 - ax, :, pl.ds(0, 32), self.cols],
+                         got2.at[m, :, pl.ds(0, 32), self.cols], x_peer),
+                    copy(self.side + 2 * k + 1, got1.at[m, :, 1 - ay, pl.ds(32, 32), self.cols],
+                         got2.at[m, :, pl.ds(32, 32), self.cols], y_peer)]
+
+        def corner_copies(self, k):
+            m = plane(k)
+            return [copy(self.corner + 2 * k, got2.at[m, 1 - ay, pl.ds(0, 32), self.cols],
+                         got3.at[m, pl.ds(0, 32), self.cols], y_peer),
+                    copy(self.corner + 2 * k + 1, got2.at[m, 1 - ax, pl.ds(32, 32), self.cols],
+                         got3.at[m, pl.ds(32, 32), self.cols], x_peer)]
+
+        def z_copy(self, k):
+            m = plane(k)
+            return copy(self.z + k, got3.at[m, :, self.cols], got4.at[k, :, self.cols], z_peer(k))
+
+        def start(self, k):
+            self.core_copy(k).start()
+
+        def to_sides(self, k):
+            m = plane(k)
+            self.core_copy(k).wait_recv()
+            got1[m, :, :, :, self.cols] = got1[m, :, :, :, self.cols] + grads[m, :, :, ac, :, self.cols]
+            for c in self.side_copies(k):
+                c.start()
+
+        def to_corner(self, k):
+            m = plane(k)
+            arrive(self.side_copies(k))
+            top, bottom = pl.ds(0, 32), pl.ds(32, 32)
+            got2[m, :, top, self.cols] = got2[m, :, top, self.cols] + got1[m, ax, :, top, self.cols]
+            got2[m, :, bottom, self.cols] = got2[m, :, bottom, self.cols] + got1[m, :, ay, bottom, self.cols]
+            for c in self.corner_copies(k):
+                c.start()
+
+        def to_planes(self, k):
+            m = plane(k)
+            arrive(self.corner_copies(k))
+            top, bottom = pl.ds(0, 32), pl.ds(32, 32)
+            got3[m, top, self.cols] = got3[m, top, self.cols] + got2[m, ay, top, self.cols]
+            got3[m, bottom, self.cols] = got3[m, bottom, self.cols] + got2[m, ax, bottom, self.cols]
+
+            @pl.when(k > 0)
+            def _():
+                self.z_copy(k).start()
+
+        def end(self):
+            total = got3[az, :, self.cols].astype(f32)
+            for k in range(1, models):
+                self.z_copy(k).wait_recv()
+                total = total + got4[k, :, self.cols].astype(f32)
+            weight_grads[:, self.cols] = total
+
+        def done(self, k):
+            self.core_copy(k).wait_send()
+            for c in self.side_copies(k) + self.corner_copies(k):
+                c.wait_send()
+
+            @pl.when(k > 0)
+            def _():
+                self.z_copy(k).wait_send()
+
+    feed_reduce = Reduce(4 * pair, 2 * hidden)
+    attention_reduce = Reduce(0, 4 * pair)
+    for k in range(models):
+        last_gather.here(k)
+
+    def feed_down(step, carry):
+        k = models - 1 - step
+        m = plane(k)
         contract_t = weight_cols(m, 4 * pair + hidden, hidden)
-        up = nn(mid, expand)
-        phi = 0.5 + 0.5 * lax.erf(up * (0.5 ** 0.5))
-        act = (up * phi).astype(bf16)
-        slope = phi + up * (jnp.exp(-0.5 * up * up) * 0.3989422804014327)
-        acc[...] += nt(act, contract_t)
-        hidden_grad = (nn(out_grad, contract_t) * slope).astype(bf16)
+        acc[...] += nt(active[m], contract_t)
+        hidden_grad = (nn(out_grad, contract_t) * slope[m]).astype(bf16)
         grads[m, :, :, :, :, 4 * pair:4 * pair + hidden] = nn(mid_t, hidden_grad).astype(bf16).reshape(block_shape)
-        grads[m, :, :, :, :, 4 * pair + hidden:4 * pair + 2 * hidden] = nn(out_grad_t, act).astype(bf16).reshape(block_shape)
-        acc2[...] += nt(hidden_grad, expand)
+        grads[m, :, :, :, :, 4 * pair + hidden:columns] = nn(out_grad_t, active[m]).astype(bf16).reshape(block_shape)
+        feed_reduce.start(k)
+        acc2[...] += nt(hidden_grad, weight_cols(m, 4 * pair, hidden))
         return carry
 
-    lax.fori_loop(0, models, feed, 0)
+    lax.fori_loop(0, models, feed_down, 0)
     result[...] = jnp.where(valid, after + acc[...], 0.0).astype(bf16)
     mid_grad = acc2[...]
-
-    def reduce_core(chunk):
-        col, count, _ = chunk
-        cols = pl.ds(col, count)
-        return [send(grads.at[:, :, :, 1 - ac, :, cols], got1.at[:, :, :, :, cols], c_peer)]
-
-    def reduce_first(chunk):
-        col, count, x_first = chunk
-        cols = pl.ds(col, count)
-        got1[:, :, :, :, cols] = got1[:, :, :, :, cols] + grads[:, :, :, ac, :, cols]
-        src = got1.at[:, 1 - ax, :, :, cols] if x_first else got1.at[:, :, 1 - ay, :, cols]
-        return [send(src, got2.at[:, :, :, cols], x_peer if x_first else y_peer)]
-
-    def reduce_second(chunk):
-        col, count, x_first = chunk
-        cols = pl.ds(col, count)
-        mine = got1[:, ax, :, :, cols] if x_first else got1[:, :, ay, :, cols]
-        got2[:, :, :, cols] = got2[:, :, :, cols] + mine
-        src = got2.at[:, 1 - ay if x_first else 1 - ax, :, cols]
-        return [send(src, got3.at[:, :, cols], y_peer if x_first else x_peer)]
-
-    def reduce_z(chunk):
-        col, count, x_first = chunk
-        cols = pl.ds(col, count)
-        got3[:, :, cols] = got3[:, :, cols] + got2[:, ay if x_first else ax, :, cols]
-        return [send(got3.at[(az + step) % models, :, cols], got4.at[step - 1, :, cols],
-                     device(ax, ay, ac, (az + step) % models)) for step in range(1, models)]
-
-    def reduce_end(chunk):
-        col, count, _ = chunk
-        cols = pl.ds(col, count)
-        total = got3[az, :, cols].astype(f32)
-        for step in range(1, models):
-            total = total + got4[step - 1, :, cols].astype(f32)
-        weight_grads[:, cols] = total
-
-    back = {i: reduce_core(chunks[i]) for i in (2, 3)}
 
     def rows_home(source, target):
         share = part // models
         target[az] = source[pl.ds(pl.multiple_of(az * share, share), share), :]
-        return [send(source.at[pl.ds(pl.multiple_of(((az + step) % models) * share, share), share), :],
-                     target.at[az], device(ax, ay, ac, (az + step) % models)) for step in range(1, models)]
+        return [send(marks.take(1), source.at[pl.ds(pl.multiple_of(plane(k) * share, share), share), :],
+                     target.at[az], z_peer(k)) for k in range(1, models)]
 
     def norm_back(grad, hat, scale_row, gain):
         scaled_grad = grad * gain
@@ -1058,38 +1166,42 @@
     merge_shape = grads.shape[1:5] + (pair,)
     select_row = lax.broadcasted_iota(jnp.int32, (pair, 128), 0) // HD
     select_col = lax.broadcasted_iota(jnp.int32, (pair, 128), 1) // 2
-
     totals[...] = jnp.zeros(totals.shape, f32)
 
-    def unmerge(m, carry):
-        grads[m, :, :, :, :, qkv:qkv + pair] = nn(branch_t, attended[m]).astype(bf16).reshape(merge_shape)
+    def unmerge(step, carry):
+        k = models - 1 - step
+        m = plane(k)
         attended_grad = nn(branch, weight_cols(m, qkv, pair)) * recip[m]
         fine = attended_grad.astype(bf16)
         grad_ext[m, NR:NR + part, :] = fine
         sums = nn(pool[...], fine).astype(bf16)
         for lv in range(1, plan.levels):
             grad_ext[m, plan.at[lv] + NR:plan.at[lv] + NR + plan.own[lv], :] = sums[plan.pool_at[lv]:plan.pool_at[lv] + plan.own[lv]]
-        grad_ext[m, pl.ds(pl.multiple_of(plan.upper + slot_row, NR), NR), :] = sums[plan.pool_upper:plan.pool_upper + NR]
+        grad_ext[m, own_slot_rows, :] = sums[plan.pool_upper:plan.pool_upper + NR]
+        grad_rims(k).start()
         high, rest = halves(attended_grad * ratio[m])
         chosen = jnp.where(select_row + 2 * m == select_col, -1.0, 0.0).astype(bf16)
         totals[...] += nn(high, chosen) + nn(rest, chosen)
+        grads[m, :, :, :, :, qkv:qkv + pair] = nn(branch_t, attended[m]).astype(bf16).reshape(merge_shape)
         return carry
 
     lax.fori_loop(0, models, unmerge, 0)
     even = lax.broadcasted_iota(jnp.int32, (1, 128), 1) % 2 == 0
-
-    def high_rest(values):
-        high, rest = halves(values)
-        return jnp.where(even, high, rest)
-
     high, rest = halves(totals[...])
     total_ext[NR:NR + part, :] = jnp.where(even, high, rest)
-    sums = high_rest(nn(pool[...], high) + nn(pool[...], rest))
+    pooled_high, pooled_rest = halves(nn(pool[...], high) + nn(pool[...], rest))
+    sums = jnp.where(even, pooled_high, pooled_rest)
     for lv in range(1, plan.levels):
         total_ext[plan.at[lv] + NR:plan.at[lv] + NR + plan.own[lv], :] = sums[plan.pool_at[lv]:plan.pool_at[lv] + plan.own[lv]]
-    total_ext[pl.ds(pl.multiple_of(plan.upper + slot_row, NR), NR), :] = sums[plan.pool_upper:plan.pool_upper + NR]
-    back_wait, back_done = exchange([grad_ext, total_ext])
+    total_ext[own_slot_rows, :] = sums[plan.pool_upper:plan.pool_upper + NR]
+    total_rims().start()
     rows_out = rows_home(result, out_rows)
+
+    def advance(step, carry):
+        feed_reduce.to_sides(models - 1 - step)
+        return carry
+
+    lax.fori_loop(0, models, advance, 0)
 
     head_of_lane = lax.broadcasted_iota(jnp.int32, (1, 128), 1) // 2
 
@@ -1098,95 +1210,124 @@
         return carry
 
     lax.fori_loop(0, models, clear, 0)
-
-    def attend_back(tiles):
-        def body(m, carry):
-            for tile in tiles:
-                first, count, window, _ = tile
-                rows_at = slice(first, first + count)
-                queries, keys, values, weight = tile_weights(m, plan.tiles.index(tile), rows_at, count, window)
-                numer = both_heads(grad_ext[m, rows_at, :])
-                tot = total_ext[rows_at, :]
-                zero = jnp.zeros_like(tot)
-                tots = jnp.concatenate([jnp.where(head_of_lane == 2 * m, tot, zero),
-                                        jnp.where(head_of_lane == 2 * m + 1, tot, zero)], axis=0)
-                score_grad = (weight * nt(jnp.concatenate([numer, tots], axis=1), values)).astype(bf16)
-                work[m, rows_at, 0:pair] = joined(nn(score_grad, keys))
-                key_rows = slice(window, window + 128)
-                work[m, key_rows, pair:2 * pair] += tn(score_grad, queries)
-                work[m, key_rows, 2 * pair:3 * pair] += tn(weight.astype(bf16), numer)
-            return carry
-
-        lax.fori_loop(0, models, body, 0)
-
-    attend_back(plan.inner)
-    for i in (2, 3):
-        arrive(back[i])
-        back[i] = reduce_first(chunks[i])
-    back_wait()
-    attend_back(plan.outer)
-    for i in (2, 3):
-        arrive(back[i])
-        back[i] = reduce_second(chunks[i])
-
     normed_t = normed[...].T
+    acc[...] = jnp.zeros(acc.shape, f32)
     qkv_shape = grads.shape[1:5] + (qkv,)
     query_scale = jnp.where(lax.broadcasted_iota(jnp.int32, (1, qkv), 1) < pair, HD ** -0.5, 1.0)
-
-    acc[...] = jnp.zeros(acc.shape, f32)
-
-    def finish(m, carry):
-        coarse = coarse_rows(m, qkv, pl.ds(pl.multiple_of(plan.upper + slot_row, NR), NR))
+    total_rims().wait()
+    query_rims().wait()
+
+    def back_tile(m, tile):
+        first, count, window, _ = tile
+        rows_at = slice(first, first + count)
+        mask = logs[plan.tiles.index(tile), 0:count]
+        queries, keys, values, weight = tile_weights(m, ext[m, rows_at, 0:pair], mask, window)
+        numer = both_heads(grad_ext[m, rows_at, :])
+        tot = total_ext[rows_at, :]
+        zero = jnp.zeros_like(tot)
+        tots = jnp.concatenate([jnp.where(head_of_lane == 2 * m, tot, zero),
+                                jnp.where(head_of_lane == 2 * m + 1, tot, zero)], axis=0)
+        score_grad = (weight * nt(jnp.concatenate([numer, tots], axis=1), values)).astype(bf16)
+        work[m, rows_at, 0:pair] = joined(nn(score_grad, keys))
+        key_rows = slice(window, window + 128)
+        work[m, key_rows, pair:2 * pair] += tn(score_grad, queries)
+        work[m, key_rows, 2 * pair:3 * pair] += tn(weight.astype(bf16), numer)
+
+    def back(step, carry):
+        k = models - 1 - step
+        m = plane(k)
+        grad_rims(k).wait()
+        for tile in plan.tiles:
+            back_tile(m, tile)
+        coarse = coarse_rows(m, qkv, own_slot_rows)
         spread = spread_out(coarse * jnp.concatenate([inverse[...]] * 3, axis=1))
         rows = (work[m, NR:NR + part, :] + jnp.where(valid, spread, 0.0)).astype(bf16)
         grads[m, :, :, :, :, 0:qkv] = (nn(normed_t, rows) * query_scale).astype(bf16).reshape(qkv_shape)
+        attention_reduce.start(k)
         acc[...] += nt(rows, weight_cols(m, 0, qkv))
+
+        @pl.when(step >= 1)
+        def _():
+            attention_reduce.to_sides(k + 1)
+            feed_reduce.to_planes(k + 1)
+
+        feed_reduce.to_corner(k)
+
+        @pl.when(step >= 2)
+        def _():
+            attention_reduce.to_corner(k + 2)
+
+        @pl.when(step >= 3)
+        def _():
+            attention_reduce.to_planes(k + 3)
+
         return carry
 
-    lax.fori_loop(0, models, finish, 0)
+    lax.fori_loop(0, models, back, 0)
     normed_grad = acc[...]
-    for i in (0, 1):
-        back[i] = reduce_core(chunks[i])
-    for i in (2, 3):
-        arrive(back[i])
-        back[i] = reduce_z(chunks[i])
     hat = scaled[...]
     row_grads[...] = (residual[...] + norm_back(normed_grad, hat, rstd[:, 0:1], pre_gain)).astype(bf16)
     grads_out = rows_home(row_grads, out_grads)
+    attention_reduce.to_sides(0)
+    attention_reduce.to_corner(1)
     norm_sums = [jnp.sum(normed_grad * hat, axis=0, keepdims=True), jnp.sum(normed_grad, axis=0, keepdims=True)] + norm_sums
     norm_got[0] = jnp.concatenate(norm_sums + [jnp.zeros((4, width), f32)], axis=0)
-    norm_peers = [[c_peer], [y_peer], [x_peer], [device(ax, ay, ac, (az + step) % models) for step in range(1, models)]]
-
-    def norm_send(stage):
-        first = 1 + 2 * stage
-        return [send(norm_got.at[2 * stage], norm_got.at[first + i], to) for i, to in enumerate(norm_peers[stage])]
-
-    def norm_sum(stage):
-        total = norm_got[2 * stage]
-        for i in range(len(norm_peers[stage])):
-            total = total + norm_got[1 + 2 * stage + i]
-        return total
-
-    small = norm_send(0)
-    stages = [reduce_first, reduce_second, reduce_z]
-    for step, stage in enumerate(stages):
-        for i in (0, 1):
-            arrive(back[i])
-            back[i] = stage(chunks[i])
-        arrive(small)
-        norm_got[2 * step + 2] = norm_sum(step)
-        small = norm_send(step + 1)
-    for i in (2, 3, 0, 1):
-        arrive(back[i])
-        reduce_end(chunks[i])
+    small = [send(marks.take(1), norm_got.at[0], norm_got.at[step], at_spot((spot + step) % spots)) for step in range(1, spots)]
+    attention_reduce.to_planes(2)
+    feed_reduce.to_planes(0)
     arrive(small)
-    norm_grads[...] = norm_sum(3)
+    norm_total = norm_got[0]
+    for step in range(1, spots):
+        norm_total = norm_total + norm_got[step]
+    norm_got[spots] = norm_total
+    small = [send(marks.take(1), norm_got.at[spots], norm_got.at[spots + k], z_peer(k)) for k in range(1, models)]
+    attention_reduce.to_corner(0)
+    attention_reduce.to_planes(1)
+    feed_reduce.end()
+    attention_reduce.to_planes(0)
+    attention_reduce.end()
+    arrive(small)
+    for k in range(1, models):
+        norm_total = norm_total + norm_got[spots + k]
+    norm_grads[...] = norm_total
     arrive(rows_out)
     arrive(grads_out)
-    for c, _ in sent:
+    assert marks.used <= net_count
+    for c in sent:
         c.wait_send()
-    rims_done()
-    back_done()
+
+    def drain(k, carry):
+        pair_rims(k).done()
+        grad_rims(k).done()
+        feed_reduce.done(k)
+        attention_reduce.done(k)
+        return carry
+
+    lax.fori_loop(0, models, drain, 0)
+    query_rims().done()
+    total_rims().done()
+
+
+def finish_outputs(dims, rows_ref, grads_ref, weights_ref, norms_ref,
+                   out_rows, out_grads, query, key, value, merge, up, down, *norm_outs):
+    part, width, pair, hidden = dims
+    out_rows[...] = rows_ref[...].reshape(out_rows.shape)
+    out_grads[...] = grads_ref[...].reshape(out_grads.shape)
+    strip = query.shape[0]
+    query[...] = weights_ref[:, 0:pair]
+    key[...] = weights_ref[:, pair:2 * pair]
+    value[...] = weights_ref[:, 2 * pair:3 * pair]
+    up[...] = weights_ref[:, 4 * pair:4 * pair + hidden]
+    padding = lambda block: jnp.concatenate([block, jnp.zeros((128 - strip, block.shape[1]), block.dtype)], axis=0)
+    merge[...] = padding(weights_ref[:, 3 * pair:4 * pair]).T[:, :strip]
+    down[...] = padding(weights_ref[:, 4 * pair + hidden:4 * pair + 2 * hidden]).T[:, :strip]
+    owner = lax.axis_index("dp") * 4 + lax.axis_index("seq")
+    strips = width // strip
+    mine = norms_ref[:, 0:strip] * (owner == 0).astype(jnp.float32)
+    for i in range(1, strips):
+        mine = jnp.where(owner == i, norms_ref[:, i * strip:(i + 1) * strip], mine)
+    for i, out in enumerate(norm_outs):
+        out[...] = mine[i].reshape(out.shape)
 
 
 def fast_body(plan, incoming_embeddings, output_sensitivity, sequence_extents, asking_projector, lookup_projector,
@@ -1197,18 +1338,12 @@
     seqs, _, part, width = incoming_embeddings.shape
     strip, pair = asking_projector.shape
     hidden = feedforward_expand.shape[1]
-    owner = lax.axis_index("dp") * lax.axis_size("seq") + lax.axis_index("seq")
-    own_weights = jnp.concatenate(
-        [asking_projector * jnp.asarray(HD ** -0.5, bf16), lookup_projector, content_projector,
-         attention_combiner.T, feedforward_expand, feedforward_contract.T], axis=1)
-    columns = own_weights.shape[1]
-    norm_parts = jnp.stack([attention_norm_scale, attention_norm_bias, feedforward_norm_scale, feedforward_norm_bias])
-    own_norms = lax.dynamic_update_slice(
-        jnp.zeros((8, width), f32), norm_parts.astype(f32), (0, owner * strip))
+    columns = 4 * pair + 2 * hidden
+    norm_parts = jnp.stack([attention_norm_scale, attention_norm_bias, feedforward_norm_scale, feedforward_norm_bias] * 2)
     share = part // models
     spots, rows = plan.spots, plan.rows
     deep = (2, 2, 2, strip, columns)
-    net_count = 128
+    net_count = 400
     vmem = pltpu.VMEM
     scratch = [
         vmem((models,) + deep, bf16), vmem((spots, 8, width), f32), vmem((part, width), bf16), vmem((part, width), bf16),
@@ -1218,8 +1353,9 @@
         vmem((part, width), bf16), vmem((part, width), f32), vmem((part, 128), f32),
         vmem((models, rows, pair), bf16), vmem((rows, 128), bf16), vmem((part, width), f32), vmem((part, width), f32),
         vmem((part, width), f32), vmem((part, 128), f32), vmem((part, width), bf16), vmem((part, width), bf16),
+        vmem((models, part, hidden), bf16), vmem((models, part, hidden), f32),
         vmem((models,) + deep, bf16), vmem((models, 2, 2, strip, columns), bf16), vmem((models, 2, strip, columns), bf16),
-        vmem((models, strip, columns), bf16), vmem((models - 1, strip, columns), bf16), vmem((10, 8, width), f32),
+        vmem((models, strip, columns), bf16), vmem((models, strip, columns), bf16), vmem((spots + models, 8, width), f32),
         pltpu.SemaphoreType.DMA((2,)), pltpu.SemaphoreType.DMA((net_count,)), pltpu.SemaphoreType.DMA((net_count,)),
     ]
     any_space, in_vmem = pl.BlockSpec(memory_space=pl.ANY), pl.BlockSpec(memory_space=pltpu.VMEM)
@@ -1227,18 +1363,24 @@
         functools.partial(whole_layer, plan, (part, width, pair, hidden), net_count),
         out_shape=(jax.ShapeDtypeStruct((seqs, share, width), bf16), jax.ShapeDtypeStruct((seqs, share, width), bf16),
                    jax.ShapeDtypeStruct((strip, columns), f32), jax.ShapeDtypeStruct((8, width), f32)),
-        in_specs=[pl.BlockSpec(memory_space=pltpu.SMEM), in_vmem, in_vmem, any_space, any_space],
+        in_specs=[pl.BlockSpec(memory_space=pltpu.SMEM)] + [in_vmem] * 7 + [any_space] * 2,
         out_specs=(in_vmem,) * 4,
         scratch_shapes=scratch,
         compiler_params=pltpu.CompilerParams(collective_id=0, has_side_effects=True, vmem_limit_bytes=60 * 2 ** 20),
         name="layer",
-    )(sequence_extents, own_weights, own_norms, incoming_embeddings, output_sensitivity)
-    ends = [0, pair, 2 * pair, 3 * pair, 4 * pair, 4 * pair + hidden, columns]
-    query_grad, key_grad, value_grad, merge_t, up_grad, down_t = (
-        weight_grads[:, low:high] for low, high in zip(ends, ends[1:]))
-    mine = lax.dynamic_slice(norm_grads, (0, owner * strip), (4, strip))
-    return (out_rows[:, None], out_grads[:, None], query_grad, key_grad, value_grad, merge_t.T, up_grad, down_t.T,
-            mine[0], mine[1], mine[2], mine[3])
+    )(sequence_extents, asking_projector, lookup_projector, content_projector, attention_combiner, feedforward_expand,
+      feedforward_contract, norm_parts, incoming_embeddings, output_sensitivity)
+    flat = lambda *shape: jax.ShapeDtypeStruct(shape, f32)
+    rows_type = jax.ShapeDtypeStruct((seqs, 1, share, width), bf16)
+    finished = pl.pallas_call(
+        functools.partial(finish_outputs, (part, width, pair, hidden)),
+        out_shape=(rows_type, rows_type, flat(strip, pair), flat(strip, pair), flat(strip, pair), flat(pair, strip),
+                   flat(strip, hidden), flat(hidden, strip)) + (flat(1, strip),) * 4,
+        in_specs=[in_vmem] * 4,
+        out_specs=(in_vmem,) * 12,
+        name="outputs",
+    )(out_rows, out_grads, weight_grads, norm_grads)
+    return finished[:8] + tuple(row.reshape(strip) for row in finished[8:])
 
 
 def solution(mesh):

time: 153 us -> 135 us (0.88)
  Pallas kernels: 138 us -> 127 us
  local copies, waits for them, and re-layouts: 12.1 us -> 7.66 us
    pallas_call x1, Pallas kernels: 138 us -> 124 us  [fast_body(): pl.pallas_call(functools.partial(whole_layer, plan, (part, width, pair, h...]
    transpose x2 -> x0, local copies, waits for them, and re-layouts: 3.14 us -> none  [fast_body(): return (out_rows[:, None], out_grads[:, None], query_grad, key_grad, valu...]
    pallas_call x0 -> x1, Pallas kernels: none -> 2.95 us  [fast_body(): pl.pallas_call(functools.partial(finish_outputs, (part, width, pair, hidd...]
    unnamed x12 -> x4, local copies, waits for them, and re-layouts: 6.37 us -> 6.29 us
where the time goes in v2:
time: 135 us
  Pallas kernels  127 us (94%)
  local copies, waits for them, and re-layouts  7.66 us (6%)
    pallas_call x1, Pallas kernels, fast_body(): pl.pallas_call(functools.partial(whole_layer, plan, (part, width, pair, h...  124 us
    unnamed x4, local copies, waits for them, and re-layouts  6.29 us
    pallas_call x1, Pallas kernels, fast_body(): pl.pallas_call(functools.partial(finish_outputs, (part, width, pair, hidd...  2.95 us

profile of v2, /device:TPU:0, one launch (start us, length us, event | category | flops | bytes accessed | tf_op | source)
XLA Modules:
  0.0 134.9 jit_solution(8655907230288207390)
XLA Ops:
  0.6 1.4 %stack.23.refs_7_ = bf16[8,64]{1,0:T(8,128)(2,1)} concatenate(bf16[1,64]{1,0:T(2,128)(2,1)} %bitcast.8, bf16[1,64]{1,0:T(2,128)(2,1)} %bitcast.10, bf16[1,64]{1,0:T(2,128)(2,1)} %bitcast.12, bf16[1,64]{1,0:T(2,128)(2,1)} %bitcast.14, bf16[1,64]{1,0:T(2,128)(2,1)} %bitcast.9, bf16[1,64]{1,0:T(2,128)(2,1)} %bitcast.11, bf16[1,64]{1,0:T(2,128)(2,1)} %bitcast.13, bf16[1,64]{1,0:T(2,128)(2,1)} %bitcast.15), dimensions={0} | concatenate | bytes 2048 | tf_op jit(solution)/shard_map/stack | solution.py:1342
  2.0 1.4 %copy.25.refs_4_ = bf16[128,64]{1,0:T(8,128)(2,1)} copy(bf16[128,64]{0,1:T(8,128)(2,1)} %param.19) | data formatting | bytes 32768 | tf_op args[6]
  3.4 1.6 %copy.26.refs_6_ = bf16[512,64]{1,0:T(8,128)(2,1)} copy(bf16[512,64]{0,1:T(8,128)(2,1)} %param.21) | data formatting | bytes 131072 | tf_op args[8]
  5.0 123.6 %layer.1 = (bf16[4,128,512]{2,1,0:T(8,128)(2,1)}, bf16[4,128,512]{2,1,0:T(8,128)(2,1)}, f32[64,1536]{1,0:T(8,128)}, f32[8,512]{1,0:T(8,128)}) custom-call(s32[4]{0:T(128)} %refs_0_.1, bf16[64,128]{1,0:T(8,128)(2,1)} %refs_1_.1, bf16[64,128]{1,0:T(8,128)(2,1)} %refs_2_.1, bf16[64,128]{1,0:T(8,128)(2,1)} %refs_3_.1, bf16[128,64]{1,0:T(8,128)(2,1)} %copy.25.refs_4_, ...), custom_call_target="tpu_custom_call" | custom-call | tf_op jit(solution)/shard_map/layer/pallas_call | solution.py:1362
  128.7 2.9 %outputs.1 = (bf16[4,1,128,512]{3,2,1,0:T(8,128)(2,1)}, bf16[4,1,128,512]{3,2,1,0:T(8,128)(2,1)}, f32[64,128]{1,0:T(8,128)}, f32[64,128]{1,0:T(8,128)}, f32[64,1...) custom-call(bf16[4,128,512]{2,1,0:T(8,128)(2,1)} %get-tuple-element., ...), custom_call_target="tpu_custom_call" | custom-call | tf_op jit(solution)/shard_map/outputs/pallas_call | solution.py:1375
  131.6 1.5 %copy.27 = f32[128,64]{0,1:T(8,128)} copy(f32[128,64]{1,0:T(8,128)} %get-tuple-element.49) | data formatting | bytes 65536
  133.2 1.7 %copy.28 = f32[512,64]{0,1:T(8,128)} copy(f32[512,64]{1,0:T(8,128)} %get-tuple-element.51) | data formatting | bytes 262144

commit v3 on v2

--- a/solution.py
+++ b/solution.py
@@ -671,13 +671,6 @@
     return nn(rows, jnp.where(target == source + place * width, 1.0, 0.0).astype(rows.dtype))
 
 
-def flipped(rows):
-    size = rows.shape[1]
-    row = lax.broadcasted_iota(jnp.int32, (size, size), 0)
-    col = lax.broadcasted_iota(jnp.int32, (size, size), 1)
-    return nt(jnp.where(row == col, 1.0, 0.0).astype(rows.dtype), rows).astype(rows.dtype)
-
-
 def flip_bits(value, k):
     low, high, k_low, k_high = value % 2, value // 2, k % 2, k // 2
     return (high + k_high - 2 * high * k_high) * 2 + low + k_low - 2 * low * k_low
@@ -693,7 +686,7 @@
 
 
 def whole_layer(plan, dims, net_count, *refs):
-    (extents, w_query, w_key, w_value, w_merge, w_expand, w_contract, norm_parts, tokens_in, cotangent_in,
+    (extents, w_query, w_key, w_value, w_merge, w_expand, w_contract, norm_0, norm_1, norm_2, norm_3, tokens_in, cotangent_in,
      out_rows, out_grads, weight_grads, norm_grads,
      weights, norms, tokens, cotangent, ext, logs, pool, unpool, inverse, work,
      attended, ratio, recip, normed, scaled, rstd, grad_ext, total_ext, residual, acc, acc2, totals, result, row_grads,
@@ -735,11 +728,13 @@
     weights[own + (slice(None), slice(0, pair))] = w_query[...] * jnp.asarray(HD ** -0.5, bf16)
     weights[own + (slice(None), slice(pair, 2 * pair))] = w_key[...]
     weights[own + (slice(None), slice(2 * pair, qkv))] = w_value[...]
-    weights[own + (slice(None), slice(qkv, qkv + pair))] = flipped(w_merge[...])
+    weights[own + (slice(None), slice(qkv, qkv + pair))] = w_merge[...]
     weights[own + (slice(None), slice(4 * pair, 4 * pair + hidden))] = w_expand[...]
-    weights[own + (slice(None), slice(4 * pair + hidden, columns))] = flipped(w_contract[...])
+    weights[own + (slice(None), slice(4 * pair + hidden, columns))] = w_contract[...]
     owner = ax * 4 + sq
-    norms[spot] = spread_columns(norm_parts[...], owner, width // strip)
+    norms[spot] = jnp.concatenate(
+        [spread_columns(row[...], owner, width // strip) for row in (norm_0, norm_1, norm_2, norm_3)]
+        + [jnp.zeros((4, width), f32)], axis=0)
     pl.semaphore_wait(barrier, spots - 1 + models - 1)
 
     marks = Marks()
@@ -749,17 +744,27 @@
             src_ref=src, dst_ref=dst, send_sem=send_sem.at[i], recv_sem=recv_sem.at[i],
             device_id=to, device_id_type=MESH)
 
+    class Group:
+        def __init__(self, i, pairs, whole):
+            self.i, self.pairs, self.whole = i, pairs, whole
+
+        def start(self):
+            for src, dst, to in self.pairs:
+                copy(self.i, src, dst, to).start()
+            return self
+
+        def arrive(self):
+            copy(self.i, self.whole, self.whole, self.pairs[0][2]).wait_recv()
+
+        def leave(self):
+            copy(self.i, self.whole, self.whole, self.pairs[0][2]).wait_send()
+
     sent = []
 
-    def send(i, src, dst, to):
-        c = copy(i, src, dst, to)
-        c.start()
-        sent.append(c)
-        return c
-
-    def arrive(copies):
-        for c in copies:
-            c.wait_recv()
+    def send(pairs, whole):
+        group = Group(marks.take(1), pairs, whole).start()
+        sent.append(group)
+        return group
 
     class Gather:
         def __init__(self, col, count, through_y):
@@ -772,27 +777,28 @@
         def to_planes(self):
             here = self.block(0, ax, ay)
             for k in range(1, models):
-                self.flight["z", k] = [send(marks.take(1), here, here, z_peer(k))]
+                self.flight["z", k] = send([(here, here, z_peer(k))], here)
 
         def to_sides(self, k):
             if k:
-                arrive(self.flight["z", k])
+                self.flight["z", k].arrive()
             here = self.block(k, ax, ay)
-            self.flight["side", k] = [send(marks.take(1), here, here, x_peer), send(marks.take(1), here, here, y_peer)]
+            self.flight["side", k] = send([(here, here, x_peer), (here, here, y_peer)],
+                                          weights.at[plane(k), :, ay, ac, :, self.cols])
 
         def to_corner(self, k):
-            arrive(self.flight["side", k])
+            self.flight["side", k].arrive()
             first = self.block(k, 1 - ax, ay, pl.ds(0, self.rows))
             rest = self.block(k, ax, 1 - ay, pl.ds(self.rows, strip - self.rows))
-            self.flight["corner", k] = [send(marks.take(1), first, first, y_peer), send(marks.take(1), rest, rest, x_peer)]
+            self.flight["corner", k] = send([(first, first, y_peer), (rest, rest, x_peer)], self.block(k, ax, ay))
 
         def to_core(self, k):
-            arrive(self.flight["corner", k])
+            self.flight["corner", k].arrive()
             here = weights.at[plane(k), :, :, ac, :, self.cols]
-            self.flight["core", k] = [send(marks.take(1), here, here, c_peer)]
+            self.flight["core", k] = send([(here, here, c_peer)], here)
 
         def here(self, k):
-            arrive(self.flight["core", k])
+            self.flight["core", k].arrive()
 
     first_gather = Gather(0, qkv, 32)
     merge_gather = Gather(qkv, pair + hidden, 48)
@@ -800,8 +806,8 @@
 
     first_gather.to_planes()
     first_gather.to_sides(0)
-    norm_copies = [send(marks.take(1), norms.at[spot], norms.at[spot], at_spot((spot + step) % spots))
-                   for step in range(1, spots)]
+    norm_copies = send([(norms.at[spot], norms.at[spot], at_spot((spot + step) % spots)) for step in range(1, spots)],
+                       norms.at[pl.ds(0, spots - 1)])
 
     low, size = pool_bounds(plan, (part, 128), 0)
     for block in range(part // 128):
@@ -838,7 +844,7 @@
     first_gather.to_corner(3)
     merge_gather.to_sides(0)
     first_gather.to_core(1)
-    arrive(norm_copies)
+    norm_copies.arrive()
     gains = norms[0]
     for i in range(1, spots):
         gains = gains + norms[i]
@@ -872,50 +878,61 @@
 
     slot_row = pl.multiple_of(spot * NR, NR)
     own_slot_rows = pl.ds(pl.multiple_of(plan.upper + slot_row, NR), NR)
-    per_rim = plan.levels * 2 + spots - 1
-
     class Rims:
-        def __init__(self, view, base):
+        def __init__(self, view, i):
+            self.view, self.i, self.to = view, i, at_spot((spot + 1) % spots)
+
+        def start(self):
+            view, i = self.view, self.i
             right, left = at_spot((spot + 1) % spots), at_spot((spot + spots - 1) % spots)
-            self.to_right, self.to_left, self.to_all = [], [], []
-            for lv in range(plan.levels):
-                start, rows = plan.at[lv], plan.own[lv]
-                self.to_right.append(copy(base + 2 * lv, view(pl.ds(start + rows, NR)), view(pl.ds(start, NR)), right))
-                self.to_left.append(copy(base + 2 * lv + 1, view(pl.ds(start + NR, NR)), view(pl.ds(start + NR + rows, NR)), left))
+
+            @pl.when(jnp.logical_not(is_last))
+            def _():
+                for start, rows in zip(plan.at, plan.own):
+                    copy(i, view(pl.ds(start + rows, NR)), view(pl.ds(start, NR)), right).start()
+
+            @pl.when(jnp.logical_not(is_first))
+            def _():
+                for start, rows in zip(plan.at, plan.own):
+                    copy(i, view(pl.ds(start + NR, NR)), view(pl.ds(start + NR + rows, NR)), left).start()
+
             block = view(own_slot_rows)
             for step in range(1, spots):
-                self.to_all.append(copy(base + 2 * plan.levels + step - 1, block, block, at_spot((spot + step) % spots)))
-
-        def each(self, verb, not_first, not_last):
-            @pl.when(jnp.logical_not(is_last))
+                copy(i, block, block, at_spot((spot + step) % spots)).start()
+
+        def whole(self, sides):
+            rows = self.view(pl.ds(0, (sides * plan.levels + spots - 1) * NR))
+            return copy(self.i, rows, rows, self.to)
+
+        def wait(self):
+            at_end = is_first | is_last
+
+            @pl.when(at_end)
             def _():
-                for c in not_last:
-                    getattr(c, verb)()
-
-            @pl.when(jnp.logical_not(is_first))
+                self.whole(1).wait_recv()
+
+            @pl.when(jnp.logical_not(at_end))
             def _():
-                for c in not_first:
-                    getattr(c, verb)()
-
-            for c in self.to_all:
-                getattr(c, verb)()
-
-        def start(self):
-            self.each("start", self.to_left, self.to_right)
-
-        def wait(self):
-            self.each("wait_recv", self.to_right, self.to_left)
+                self.whole(2).wait_recv()
 
         def done(self):
-            self.each("wait_send", self.to_left, self.to_right)
-
-    pair_base = marks.take(models * per_rim)
-    query_base = marks.take(per_rim)
-    grad_base = marks.take(models * per_rim)
-    total_base = marks.take(per_rim)
-    pair_rims = lambda k: Rims(lambda rows: ext.at[plane(k), rows, pl.ds(pair, 2 * pair)], pair_base + k * per_rim)
+            at_end = is_first | is_last
+
+            @pl.when(at_end)
+            def _():
+                self.whole(1).wait_send()
+
+            @pl.when(jnp.logical_not(at_end))
+            def _():
+                self.whole(2).wait_send()
+
+    pair_base = marks.take(models)
+    query_base = marks.take(1)
+    grad_base = marks.take(models)
+    total_base = marks.take(1)
+    pair_rims = lambda k: Rims(lambda rows: ext.at[plane(k), rows, pl.ds(pair, 2 * pair)], pair_base + k)
     query_rims = lambda: Rims(lambda rows: ext.at[:, rows, pl.ds(0, pair)], query_base)
-    grad_rims = lambda k: Rims(lambda rows: grad_ext.at[plane(k), rows, :], grad_base + k * per_rim)
+    grad_rims = lambda k: Rims(lambda rows: grad_ext.at[plane(k), rows, :], grad_base + k)
     total_rims = lambda: Rims(lambda rows: total_ext.at[rows, :], total_base)
 
     for k in range(models):
@@ -1051,78 +1068,75 @@
     class Reduce:
         def __init__(self, col, count):
             self.cols = pl.ds(col, count)
-            self.core = marks.take(models)
-            self.side = marks.take(2 * models)
-            self.corner = marks.take(2 * models)
-            self.z = marks.take(models)
-
-        def core_copy(self, k):
+            self.first = marks.take(4 * models)
+
+        def core(self, k):
             m = plane(k)
-            return copy(self.core + k, grads.at[m, :, :, 1 - ac, :, self.cols], got1.at[m, :, :, :, self.cols], c_peer)
-
-        def side_copies(self, k):
+            landing = got1.at[m, :, :, :, self.cols]
+            return Group(self.first + k, [(grads.at[m, :, :, 1 - ac, :, self.cols], landing, c_peer)], landing)
+
+        def side(self, k):
             m = plane(k)
-            return [copy(self.side + 2 * k, got1.at[m, 1 - ax, :, pl.ds(0, 32), self.cols],
-                         got2.at[m, :, pl.ds(0, 32), self.cols], x_peer),
-                    copy(self.side + 2 * k + 1, got1.at[m, :, 1 - ay, pl.ds(32, 32), self.cols],
-                         got2.at[m, :, pl.ds(32, 32), self.cols], y_peer)]
-
-        def corner_copies(self, k):
+            top, bottom = pl.ds(0, 32), pl.ds(32, 32)
+            return Group(self.first + models + k,
+                         [(got1.at[m, 1 - ax, :, top, self.cols], got2.at[m, :, top, self.cols], x_peer),
+                          (got1.at[m, :, 1 - ay, bottom, self.cols], got2.at[m, :, bottom, self.cols], y_peer)],
+                         got2.at[m, :, :, self.cols])
+
+        def corner(self, k):
             m = plane(k)
-            return [copy(self.corner + 2 * k, got2.at[m, 1 - ay, pl.ds(0, 32), self.cols],
-                         got3.at[m, pl.ds(0, 32), self.cols], y_peer),
-                    copy(self.corner + 2 * k + 1, got2.at[m, 1 - ax, pl.ds(32, 32), self.cols],
-                         got3.at[m, pl.ds(32, 32), self.cols], x_peer)]
-
-        def z_copy(self, k):
-            m = plane(k)
-            return copy(self.z + k, got3.at[m, :, self.cols], got4.at[k, :, self.cols], z_peer(k))
+            top, bottom = pl.ds(0, 32), pl.ds(32, 32)
+            return Group(self.first + 2 * models + k,
+                         [(got2.at[m, 1 - ay, top, self.cols], got3.at[m, top, self.cols], y_peer),
+                          (got2.at[m, 1 - ax, bottom, self.cols], got3.at[m, bottom, self.cols], x_peer)],
+                         got3.at[m, :, self.cols])
+
+        def home(self, k):
+            block = got3.at[plane(k), :, self.cols]
+            return Group(self.first + 3 * models + k, [(block, got4.at[k, :, self.cols], z_peer(k))], block)
 
         def start(self, k):
-            self.core_copy(k).start()
+            self.core(k).start()
 
         def to_sides(self, k):
             m = plane(k)
-            self.core_copy(k).wait_recv()
+            self.core(k).arrive()
             got1[m, :, :, :, self.cols] = got1[m, :, :, :, self.cols] + grads[m, :, :, ac, :, self.cols]
-            for c in self.side_copies(k):
-                c.start()
+            self.side(k).start()
 
         def to_corner(self, k):
             m = plane(k)
-            arrive(self.side_copies(k))
+            self.side(k).arrive()
             top, bottom = pl.ds(0, 32), pl.ds(32, 32)
             got2[m, :, top, self.cols] = got2[m, :, top, self.cols] + got1[m, ax, :, top, self.cols]
             got2[m, :, bottom, self.cols] = got2[m, :, bottom, self.cols] + got1[m, :, ay, bottom, self.cols]
-            for c in self.corner_copies(k):
-                c.start()
+            self.corner(k).start()
 
         def to_planes(self, k):
             m = plane(k)
-            arrive(self.corner_copies(k))
+            self.corner(k).arrive()
             top, bottom = pl.ds(0, 32), pl.ds(32, 32)
             got3[m, top, self.cols] = got3[m, top, self.cols] + got2[m, ay, top, self.cols]
             got3[m, bottom, self.cols] = got3[m, bottom, self.cols] + got2[m, ax, bottom, self.cols]
 
             @pl.when(k > 0)
             def _():
-                self.z_copy(k).start()
+                self.home(k).start()
 
         def end(self):
             total = got3[az, :, self.cols].astype(f32)
             for k in range(1, models):
-                self.z_copy(k).wait_recv()
+                self.home(k).arrive()
                 total = total + got4[k, :, self.cols].astype(f32)
             weight_grads[:, self.cols] = total
 
         def done(self, k):
-            self.core_copy(k).wait_send()
-            for c in self.side_copies(k) + self.corner_copies(k):
-                c.wait_send()
+            for group in (self.core(k), self.side(k), self.corner(k)):
+                group.leave()
 
             @pl.when(k > 0)
             def _():
-                self.z_copy(k).wait_send()
+                self.home(k).leave()
 
     feed_reduce = Reduce(4 * pair, 2 * hidden)
     attention_reduce = Reduce(0, 4 * pair)
@@ -1148,8 +1162,8 @@
     def rows_home(source, target):
         share = part // models
         target[az] = source[pl.ds(pl.multiple_of(az * share, share), share), :]
-        return [send(marks.take(1), source.at[pl.ds(pl.multiple_of(plane(k) * share, share), share), :],
-                     target.at[az], z_peer(k)) for k in range(1, models)]
+        return send([(source.at[pl.ds(pl.multiple_of(plane(k) * share, share), share), :], target.at[az], z_peer(k))
+                     for k in range(1, models)], target.at[pl.ds(0, models - 1)])
 
     def norm_back(grad, hat, scale_row, gain):
         scaled_grad = grad * gain
@@ -1272,29 +1286,31 @@
     attention_reduce.to_corner(1)
     norm_sums = [jnp.sum(normed_grad * hat, axis=0, keepdims=True), jnp.sum(normed_grad, axis=0, keepdims=True)] + norm_sums
     norm_got[0] = jnp.concatenate(norm_sums + [jnp.zeros((4, width), f32)], axis=0)
-    small = [send(marks.take(1), norm_got.at[0], norm_got.at[step], at_spot((spot + step) % spots)) for step in range(1, spots)]
+    small = send([(norm_got.at[0], norm_got.at[step], at_spot((spot + step) % spots)) for step in range(1, spots)],
+                 norm_got.at[pl.ds(0, spots - 1)])
     attention_reduce.to_planes(2)
     feed_reduce.to_planes(0)
-    arrive(small)
+    small.arrive()
     norm_total = norm_got[0]
     for step in range(1, spots):
         norm_total = norm_total + norm_got[step]
     norm_got[spots] = norm_total
-    small = [send(marks.take(1), norm_got.at[spots], norm_got.at[spots + k], z_peer(k)) for k in range(1, models)]
+    small = send([(norm_got.at[spots], norm_got.at[spots + k], z_peer(k)) for k in range(1, models)],
+                 norm_got.at[pl.ds(0, models - 1)])
     attention_reduce.to_corner(0)
     attention_reduce.to_planes(1)
     feed_reduce.end()
     attention_reduce.to_planes(0)
     attention_reduce.end()
-    arrive(small)
+    small.arrive()
     for k in range(1, models):
         norm_total = norm_total + norm_got[spots + k]
     norm_grads[...] = norm_total
-    arrive(rows_out)
-    arrive(grads_out)
-    assert marks.used <= net_count
-    for c in sent:
-        c.wait_send()
+    rows_out.arrive()
+    grads_out.arrive()
+    assert marks.used == net_count, marks.used
+    for group in sent:
+        group.leave()
 
     def drain(k, carry):
         pair_rims(k).done()
@@ -1318,9 +1334,8 @@
     key[...] = weights_ref[:, pair:2 * pair]
     value[...] = weights_ref[:, 2 * pair:3 * pair]
     up[...] = weights_ref[:, 4 * pair:4 * pair + hidden]
-    padding = lambda block: jnp.concatenate([block, jnp.zeros((128 - strip, block.shape[1]), block.dtype)], axis=0)
-    merge[...] = padding(weights_ref[:, 3 * pair:4 * pair]).T[:, :strip]
-    down[...] = padding(weights_ref[:, 4 * pair + hidden:4 * pair + 2 * hidden]).T[:, :strip]
+    merge[...] = weights_ref[:, 3 * pair:4 * pair]
+    down[...] = weights_ref[:, 4 * pair + hidden:4 * pair + 2 * hidden]
     owner = lax.axis_index("dp") * 4 + lax.axis_index("seq")
     strips = width // strip
     mine = norms_ref[:, 0:strip] * (owner == 0).astype(jnp.float32)
@@ -1339,11 +1354,12 @@
     strip, pair = asking_projector.shape
     hidden = feedforward_expand.shape[1]
     columns = 4 * pair + 2 * hidden
-    norm_parts = jnp.stack([attention_norm_scale, attention_norm_bias, feedforward_norm_scale, feedforward_norm_bias] * 2)
+    norm_parts = [row.reshape(1, strip) for row in (
+        attention_norm_scale, attention_norm_bias, feedforward_norm_scale, feedforward_norm_bias)]
     share = part // models
     spots, rows = plan.spots, plan.rows
     deep = (2, 2, 2, strip, columns)
-    net_count = 400
+    net_count = 92
     vmem = pltpu.VMEM
     scratch = [
         vmem((models,) + deep, bf16), vmem((spots, 8, width), f32), vmem((part, width), bf16), vmem((part, width), bf16),
@@ -1363,24 +1379,26 @@
         functools.partial(whole_layer, plan, (part, width, pair, hidden), net_count),
         out_shape=(jax.ShapeDtypeStruct((seqs, share, width), bf16), jax.ShapeDtypeStruct((seqs, share, width), bf16),
                    jax.ShapeDtypeStruct((strip, columns), f32), jax.ShapeDtypeStruct((8, width), f32)),
-        in_specs=[pl.BlockSpec(memory_space=pltpu.SMEM)] + [in_vmem] * 7 + [any_space] * 2,
+        in_specs=[pl.BlockSpec(memory_space=pltpu.SMEM)] + [in_vmem] * 10 + [any_space] * 2,
         out_specs=(in_vmem,) * 4,
         scratch_shapes=scratch,
         compiler_params=pltpu.CompilerParams(collective_id=0, has_side_effects=True, vmem_limit_bytes=60 * 2 ** 20),
         name="layer",
-    )(sequence_extents, asking_projector, lookup_projector, content_projector, attention_combiner, feedforward_expand,
-      feedforward_contract, norm_parts, incoming_embeddings, output_sensitivity)
+    )(sequence_extents, asking_projector, lookup_projector, content_projector, attention_combiner.T, feedforward_expand,
+      feedforward_contract.T, *norm_parts, incoming_embeddings, output_sensitivity)
     flat = lambda *shape: jax.ShapeDtypeStruct(shape, f32)
     rows_type = jax.ShapeDtypeStruct((seqs, 1, share, width), bf16)
     finished = pl.pallas_call(
         functools.partial(finish_outputs, (part, width, pair, hidden)),
-        out_shape=(rows_type, rows_type, flat(strip, pair), flat(strip, pair), flat(strip, pair), flat(pair, strip),
-                   flat(strip, hidden), flat(hidden, strip)) + (flat(1, strip),) * 4,
+        out_shape=(rows_type, rows_type, flat(strip, pair), flat(strip, pair), flat(strip, pair), flat(strip, pair),
+                   flat(strip, hidden), flat(strip, hidden)) + (flat(1, strip),) * 4,
         in_specs=[in_vmem] * 4,
         out_specs=(in_vmem,) * 12,
         name="outputs",
     )(out_rows, out_grads, weight_grads, norm_grads)
-    return finished[:8] + tuple(row.reshape(strip) for row in finished[8:])
+    rows_end, grads_end, query_grad, key_grad, value_grad, merge_t, up_grad, down_t = finished[:8]
+    return (rows_end, grads_end, query_grad, key_grad, value_grad, merge_t.T, up_grad, down_t.T,
+            *(row.reshape(strip) for row in finished[8:]))
 
 
 def solution(mesh):

time: 135 us -> 122 us (0.904)
  local copies, waits for them, and re-layouts: 7.66 us -> 0 us
  Pallas kernels: 127 us -> 121 us
    unnamed x4 -> x0, local copies, waits for them, and re-layouts: 6.29 us -> none
    pallas_call x1, Pallas kernels: 124 us -> 118 us  [fast_body(): pl.pallas_call(functools.partial(whole_layer, plan, (part, width, pair, h...]
    another operation x1 -> x0, local copies, waits for them, and re-layouts: 1.37 us -> none  [fast_body(): jnp.stack([attention_norm_scale, attention_norm_bias, feedforward_norm_sc...]
where the time goes in v3:
time: 122 us
  Pallas kernels  121 us (99%)
    pallas_call x1, Pallas kernels, fast_body(): pl.pallas_call(functools.partial(whole_layer, plan, (part, width, pair, h...  118 us
    pallas_call x1, Pallas kernels, fast_body(): pl.pallas_call(functools.partial(finish_outputs, (part, width, pair, hidd...  2.91 us

profile of v3, /device:TPU:0, one launch (start us, length us, event | category | flops | bytes accessed | tf_op | source)
XLA Modules:
  0.0 121.5 jit_solution(11102925557985000147)
XLA Ops:
  0.6 117.8 %layer.1 = (bf16[4,128,512]{2,1,0:T(8,128)(2,1)}, bf16[4,128,512]{2,1,0:T(8,128)(2,1)}, f32[64,1536]{1,0:T(8,128)}, f32[8,512]{1,0:T(8,128)}) custom-call(s32[4]{0:T(128)} %refs_0_.1, bf16[64,128]{1,0:T(8,128)(2,1)} %refs_1_.1, bf16[64,128]{1,0:T(8,128)(2,1)} %refs_2_.1, bf16[64,128]{1,0:T(8,128)(2,1)} %refs_3_.1, bf16[64,128]{1,0:T(8,128)(2,1)} %bitcast.13, ...), custom_call_target="tpu_custom_call" | custom-call | tf_op jit(solution)/shard_map/layer/pallas_call | solution.py:1378
  118.5 2.9 %outputs.1 = (bf16[4,1,128,512]{3,2,1,0:T(8,128)(2,1)}, bf16[4,1,128,512]{3,2,1,0:T(8,128)(2,1)}, f32[64,128]{1,0:T(8,128)}, f32[64,128]{1,0:T(8,128)}, f32[64,1...) custom-call(bf16[4,128,512]{2,1,0:T(8,128)(2,1)} %get-tuple-element., ...), custom_call_target="tpu_custom_call" | custom-call | tf_op jit(solution)/shard_map/outputs/pallas_call | solution.py:1391

commit v4 on v3

--- a/solution.py
+++ b/solution.py
@@ -539,6 +539,8 @@
 
 MESH = pl.DeviceIdType.MESH
 NEG = -1e30
+BACK_GROUP = 5
+GROUP = 5
 
 
 def nn(a, b):
@@ -690,7 +692,7 @@
      out_rows, out_grads, weight_grads, norm_grads,
      weights, norms, tokens, cotangent, ext, logs, pool, unpool, inverse, work,
      attended, ratio, recip, normed, scaled, rstd, grad_ext, total_ext, residual, acc, acc2, totals, result, row_grads,
-     active, slope, grads, got1, got2, got3, got4, norm_got,
+     grads, got1, got2, got3, got4, norm_got,
      load_sem, send_sem, recv_sem) = refs
     part, width, pair, hidden = dims
     f32, bf16 = jnp.float32, jnp.bfloat16
@@ -770,6 +772,7 @@
         def __init__(self, col, count, through_y):
             self.cols, self.rows = pl.ds(col, count), through_y
             self.flight = {}
+            self.first = marks.take(models)
 
         def block(self, k, x, y, rows=slice(None)):
             return weights.at[plane(k), x, y, ac, rows, self.cols]
@@ -794,15 +797,18 @@
 
         def to_core(self, k):
             self.flight["corner", k].arrive()
+            sent.append(self.last(k).start())
+
+        def last(self, k):
             here = weights.at[plane(k), :, :, ac, :, self.cols]
-            self.flight["core", k] = send([(here, here, c_peer)], here)
+            return Group(self.first + k, [(here, here, c_peer)], here)
 
         def here(self, k):
-            self.flight["core", k].arrive()
+            self.last(k).arrive()
 
     first_gather = Gather(0, qkv, 32)
-    merge_gather = Gather(qkv, pair + hidden, 48)
-    last_gather = Gather(4 * pair + hidden, hidden, 48)
+    merge_gather = Gather(qkv, pair, 48)
+    feed_gather = Gather(4 * pair, 2 * hidden, 48)
 
     first_gather.to_planes()
     first_gather.to_sides(0)
@@ -836,6 +842,7 @@
     first_gather.to_sides(2)
     first_gather.to_sides(3)
     merge_gather.to_planes()
+    feed_gather.to_planes()
     first_gather.to_core(0)
     first_gather.to_corner(1)
     for i, tile in enumerate(plan.tiles):
@@ -843,6 +850,7 @@
     first_gather.to_corner(2)
     first_gather.to_corner(3)
     merge_gather.to_sides(0)
+    feed_gather.to_sides(0)
     first_gather.to_core(1)
     norm_copies.arrive()
     gains = norms[0]
@@ -852,7 +860,6 @@
     normed[...] = (scaled[...] * pre_gain + pre_shift).astype(bf16)
     first_gather.to_core(2)
     first_gather.to_core(3)
-    last_gather.to_planes()
 
     is_first, is_last = spot == 0, spot == spots - 1
 
@@ -946,9 +953,6 @@
         ext[m, own_slot_rows, :] = means[plan.pool_upper:plan.pool_upper + NR]
         pair_rims(k).start()
 
-    for k in range(1, models):
-        merge_gather.to_sides(k)
-
     lane = lax.broadcasted_iota(jnp.int32, (1, pair), 1)
     left_head = lane < HD
 
@@ -972,42 +976,50 @@
         weight = jnp.exp(nt(queries, keys) + jnp.concatenate([mask, mask], axis=0))
         return queries, keys, values, weight
 
+    def attend_tiles(m, tiles):
+        pieces, weights_values = [], []
+        for tile in tiles:
+            first, _, window, _ = tile
+            index = plan.tiles.index(tile)
+            if first == plan.upper:
+                pieces.append([(first, NR)])
+                rows, mask = ext[m, own_slot_rows, 0:pair], logs[index, pl.ds(slot_row, NR)]
+            else:
+                pieces.append(plan.own_pieces(tile))
+                rows = stacked([ext[m, low:low + count, 0:pair] for low, count in pieces[-1]])
+                mask = stacked([logs[index, low - first:low - first + count] for low, count in pieces[-1]])
+            _, _, values, weight = tile_weights(m, rows, mask, window)
+            weights_values.append((weight.astype(bf16), values))
+        both = [nn(weight, values) for weight, values in weights_values]
+        sides = [(joined(product[:, :128]), joined(product[:, 128:])) for product in both]
+        for rows, (numer, tot) in zip(pieces, sides):
+            at = 0
+            for low, count in rows:
+                work[m, low:low + count, 0:pair] = numer[at:at + count]
+                work[m, low:low + count, pair:2 * pair] = tot[at:at + count]
+                at += count
+
     def attend(tiles, first_k, last_k, wait_rims):
         def body(k, carry):
             m = plane(k)
             if wait_rims:
                 pair_rims(k).wait()
-            for tile in tiles:
-                first, _, window, _ = tile
-                index = plan.tiles.index(tile)
-                if first == plan.upper:
-                    pieces = [(first, NR)]
-                    rows, mask = ext[m, own_slot_rows, 0:pair], logs[index, pl.ds(slot_row, NR)]
-                else:
-                    pieces = plan.own_pieces(tile)
-                    rows = stacked([ext[m, low:low + count, 0:pair] for low, count in pieces])
-                    mask = stacked([logs[index, low - first:low - first + count] for low, count in pieces])
-                _, _, values, weight = tile_weights(m, rows, mask, window)
-                both = nn(weight.astype(bf16), values)
-                numer, tot = joined(both[:, :128]), joined(both[:, 128:])
-                at = 0
-                for low, count in pieces:
-                    work[m, low:low + count, 0:pair] = numer[at:at + count]
-                    work[m, low:low + count, pair:2 * pair] = tot[at:at + count]
-                    at += count
+            for at in range(0, len(tiles), GROUP):
+                attend_tiles(m, tiles[at:at + GROUP])
             return carry
 
         lax.fori_loop(first_k, last_k, body, 0)
 
     attend(plan.inner, 0, models, False)
+    for k in range(1, models):
+        merge_gather.to_sides(k)
     attend(plan.outer, 0, 2, True)
+    feed_gather.to_corner(0)
+    feed_gather.to_sides(1)
+    attend(plan.outer, 2, models, True)
     for k in range(models):
         merge_gather.to_corner(k)
-    for k in range(models):
-        last_gather.to_sides(k)
-    attend(plan.outer, 2, models, True)
-    for k in range(models):
-        merge_gather.to_core(k)
+    feed_gather.to_sides(2)
 
     def coarse_rows(m, cols, slot_at):
         rows = [work[m, plan.at[lv] + NR:plan.at[lv] + NR + plan.own[lv], 0:cols] for lv in range(1, plan.levels)]
@@ -1028,8 +1040,11 @@
         return carry
 
     lax.fori_loop(0, models, normalise, 0)
+    feed_gather.to_core(0)
     for k in range(models):
-        last_gather.to_corner(k)
+        merge_gather.to_core(k)
+    feed_gather.to_corner(1)
+    feed_gather.to_sides(3)
 
     residual[...] = tokens[...].astype(f32)
     for k in range(models):
@@ -1053,17 +1068,8 @@
     acc2[...] = jnp.zeros(acc.shape, f32)
     block_shape = grads.shape[1:5] + (hidden,)
 
-    def feed_up(m, carry):
-        up = nn(mid, weight_cols(m, 4 * pair, hidden))
-        phi = 0.5 + 0.5 * lax.erf(up * (0.5 ** 0.5))
-        active[m] = (up * phi).astype(bf16)
-        slope[m] = phi + up * (jnp.exp(-0.5 * up * up) * 0.3989422804014327)
-        return carry
-
-    lax.fori_loop(0, models, feed_up, 0)
-    for k in range(models):
-        last_gather.to_core(k)
-    query_rims().start()
+    feed_gather.to_core(1)
+    feed_gather.to_corner(2)
 
     class Reduce:
         def __init__(self, col, count):
@@ -1093,7 +1099,7 @@
 
         def home(self, k):
             block = got3.at[plane(k), :, self.cols]
-            return Group(self.first + 3 * models + k, [(block, got4.at[k, :, self.cols], z_peer(k))], block)
+            return Group(self.first + 3 * models + k, [(block, got4.at[k, :, self.cols], z_peer(1 + 2 * (k // 3)))], block)
 
         def start(self, k):
             self.core(k).start()
@@ -1119,13 +1125,18 @@
             got3[m, top, self.cols] = got3[m, top, self.cols] + got2[m, ay, top, self.cols]
             got3[m, bottom, self.cols] = got3[m, bottom, self.cols] + got2[m, ax, bottom, self.cols]
 
+            @pl.when(k == 3)
+            def _():
+                self.home(2).arrive()
+                got3[m, :, self.cols] = got3[m, :, self.cols] + got4[2, :, self.cols]
+
             @pl.when(k > 0)
             def _():
                 self.home(k).start()
 
         def end(self):
             total = got3[az, :, self.cols].astype(f32)
-            for k in range(1, models):
+            for k in (1, 3):
                 self.home(k).arrive()
                 total = total + got4[k, :, self.cols].astype(f32)
             weight_grads[:, self.cols] = total
@@ -1140,22 +1151,34 @@
 
     feed_reduce = Reduce(4 * pair, 2 * hidden)
     attention_reduce = Reduce(0, 4 * pair)
-    for k in range(models):
-        last_gather.here(k)
-
-    def feed_down(step, carry):
-        k = models - 1 - step
+
+    def feed(k, carry):
         m = plane(k)
-        contract_t = weight_cols(m, 4 * pair + hidden, hidden)
-        acc[...] += nt(active[m], contract_t)
-        hidden_grad = (nn(out_grad, contract_t) * slope[m]).astype(bf16)
+        feed_gather.here(k)
+        expand, contract_t = weight_cols(m, 4 * pair, hidden), weight_cols(m, 4 * pair + hidden, hidden)
+        up = nn(mid, expand)
+        act_grad = nn(out_grad, contract_t)
+        phi = 0.5 + 0.5 * lax.erf(up * (0.5 ** 0.5))
+        act = (up * phi).astype(bf16)
+        slope = phi + up * (jnp.exp(-0.5 * up * up) * 0.3989422804014327)
+        hidden_grad = (act_grad * slope).astype(bf16)
         grads[m, :, :, :, :, 4 * pair:4 * pair + hidden] = nn(mid_t, hidden_grad).astype(bf16).reshape(block_shape)
-        grads[m, :, :, :, :, 4 * pair + hidden:columns] = nn(out_grad_t, active[m]).astype(bf16).reshape(block_shape)
+        grads[m, :, :, :, :, 4 * pair + hidden:columns] = nn(out_grad_t, act).astype(bf16).reshape(block_shape)
         feed_reduce.start(k)
-        acc2[...] += nt(hidden_grad, weight_cols(m, 4 * pair, hidden))
+        acc[...] += nt(act, contract_t)
+        acc2[...] += nt(hidden_grad, expand)
         return carry
 
-    lax.fori_loop(0, models, feed_down, 0)
+    lax.fori_loop(0, 1, feed, 0)
+    feed_gather.to_core(2)
+    feed_gather.to_corner(3)
+    query_rims().start()
+    lax.fori_loop(1, 2, feed, 0)
+    feed_gather.to_core(3)
+    feed_reduce.to_sides(0)
+    lax.fori_loop(2, 3, feed, 0)
+    feed_reduce.to_sides(1)
+    lax.fori_loop(3, 4, feed, 0)
     result[...] = jnp.where(valid, after + acc[...], 0.0).astype(bf16)
     mid_grad = acc2[...]
 
@@ -1211,11 +1234,9 @@
     total_rims().start()
     rows_out = rows_home(result, out_rows)
 
-    def advance(step, carry):
-        feed_reduce.to_sides(models - 1 - step)
-        return carry
-
-    lax.fori_loop(0, models, advance, 0)
+    feed_reduce.to_corner(0)
+    feed_reduce.to_sides(2)
+    feed_reduce.to_sides(3)
 
     head_of_lane = lax.broadcasted_iota(jnp.int32, (1, 128), 1) // 2
 
@@ -1228,31 +1249,48 @@
     acc[...] = jnp.zeros(acc.shape, f32)
     qkv_shape = grads.shape[1:5] + (qkv,)
     query_scale = jnp.where(lax.broadcasted_iota(jnp.int32, (1, qkv), 1) < pair, HD ** -0.5, 1.0)
+    def back_tiles(m, tiles):
+        rows_at = [slice(first, first + count) for first, count, _, _ in tiles]
+        key_rows = [slice(window, window + 128) for _, _, window, _ in tiles]
+        masks = [logs[plan.tiles.index(tile), 0:tile[1]] for tile in tiles]
+        made = [tile_weights(m, ext[m, rows, 0:pair], mask, tile[2]) for tile, rows, mask in zip(tiles, rows_at, masks)]
+        numers = [both_heads(grad_ext[m, rows, :]) for rows in rows_at]
+        slopes = []
+        for rows, numer, (_, _, values, _) in zip(rows_at, numers, made):
+            tot = total_ext[rows, :]
+            zero = jnp.zeros_like(tot)
+            tots = jnp.concatenate([jnp.where(head_of_lane == 2 * m, tot, zero),
+                                    jnp.where(head_of_lane == 2 * m + 1, tot, zero)], axis=0)
+            slopes.append(nt(jnp.concatenate([numer, tots], axis=1), values))
+        score_grads = [(weight * by).astype(bf16) for (_, _, _, weight), by in zip(made, slopes)]
+        query_sides = [joined(nn(grad, keys)) for grad, (_, keys, _, _) in zip(score_grads, made)]
+        key_sides = [tn(grad, queries) for grad, (queries, _, _, _) in zip(score_grads, made)]
+        value_sides = [tn(weight.astype(bf16), numer) for (_, _, _, weight), numer in zip(made, numers)]
+        for rows, side in zip(rows_at, query_sides):
+            work[m, rows, 0:pair] = side
+        for rows, key_side, value_side in zip(key_rows, key_sides, value_sides):
+            work[m, rows, pair:2 * pair] += key_side
+            work[m, rows, 2 * pair:3 * pair] += value_side
+
+    def back_inner(m, carry):
+        back_tiles(m, plan.inner)
+        return carry
+
+    lax.fori_loop(0, models, back_inner, 0)
+    feed_reduce.to_corner(1)
     total_rims().wait()
     query_rims().wait()
 
-    def back_tile(m, tile):
-        first, count, window, _ = tile
-        rows_at = slice(first, first + count)
-        mask = logs[plan.tiles.index(tile), 0:count]
-        queries, keys, values, weight = tile_weights(m, ext[m, rows_at, 0:pair], mask, window)
-        numer = both_heads(grad_ext[m, rows_at, :])
-        tot = total_ext[rows_at, :]
-        zero = jnp.zeros_like(tot)
-        tots = jnp.concatenate([jnp.where(head_of_lane == 2 * m, tot, zero),
-                                jnp.where(head_of_lane == 2 * m + 1, tot, zero)], axis=0)
-        score_grad = (weight * nt(jnp.concatenate([numer, tots], axis=1), values)).astype(bf16)
-        work[m, rows_at, 0:pair] = joined(nn(score_grad, keys))
-        key_rows = slice(window, window + 128)
-        work[m, key_rows, pair:2 * pair] += tn(score_grad, queries)
-        work[m, key_rows, 2 * pair:3 * pair] += tn(weight.astype(bf16), numer)
+    def turn(step):
+        late = step // 2
+        return (2 + step) * (1 - late) + (3 - step) * late
 
     def back(step, carry):
-        k = models - 1 - step
+        k = turn(step)
         m = plane(k)
         grad_rims(k).wait()
-        for tile in plan.tiles:
-            back_tile(m, tile)
+        for at in range(0, len(plan.outer), BACK_GROUP):
+            back_tiles(m, plan.outer[at:at + BACK_GROUP])
         coarse = coarse_rows(m, qkv, own_slot_rows)
         spread = spread_out(coarse * jnp.concatenate([inverse[...]] * 3, axis=1))
         rows = (work[m, NR:NR + part, :] + jnp.where(valid, spread, 0.0)).astype(bf16)
@@ -1260,20 +1298,35 @@
         attention_reduce.start(k)
         acc[...] += nt(rows, weight_cols(m, 0, qkv))
 
+        @pl.when(step == 0)
+        def _():
+            feed_reduce.to_corner(2)
+            feed_reduce.to_planes(0)
+
+        @pl.when(step == 1)
+        def _():
+            feed_reduce.to_corner(3)
+            feed_reduce.to_planes(1)
+
+        @pl.when(step == 2)
+        def _():
+            feed_reduce.to_planes(2)
+
+        @pl.when(step == 3)
+        def _():
+            feed_reduce.to_planes(3)
+
         @pl.when(step >= 1)
         def _():
-            attention_reduce.to_sides(k + 1)
-            feed_reduce.to_planes(k + 1)
-
-        feed_reduce.to_corner(k)
+            attention_reduce.to_sides(turn(step - 1))
 
         @pl.when(step >= 2)
         def _():
-            attention_reduce.to_corner(k + 2)
+            attention_reduce.to_corner(turn(step - 2))
 
         @pl.when(step >= 3)
         def _():
-            attention_reduce.to_planes(k + 3)
+            attention_reduce.to_planes(turn(step - 3))
 
         return carry
 
@@ -1284,12 +1337,15 @@
     grads_out = rows_home(row_grads, out_grads)
     attention_reduce.to_sides(0)
     attention_reduce.to_corner(1)
+    attention_reduce.to_planes(3)
     norm_sums = [jnp.sum(normed_grad * hat, axis=0, keepdims=True), jnp.sum(normed_grad, axis=0, keepdims=True)] + norm_sums
     norm_got[0] = jnp.concatenate(norm_sums + [jnp.zeros((4, width), f32)], axis=0)
     small = send([(norm_got.at[0], norm_got.at[step], at_spot((spot + step) % spots)) for step in range(1, spots)],
                  norm_got.at[pl.ds(0, spots - 1)])
-    attention_reduce.to_planes(2)
-    feed_reduce.to_planes(0)
+    attention_reduce.to_corner(0)
+    attention_reduce.to_planes(1)
+    feed_reduce.end()
+    attention_reduce.to_planes(0)
     small.arrive()
     norm_total = norm_got[0]
     for step in range(1, spots):
@@ -1297,10 +1353,6 @@
     norm_got[spots] = norm_total
     small = send([(norm_got.at[spots], norm_got.at[spots + k], z_peer(k)) for k in range(1, models)],
                  norm_got.at[pl.ds(0, models - 1)])
-    attention_reduce.to_corner(0)
-    attention_reduce.to_planes(1)
-    feed_reduce.end()
-    attention_reduce.to_planes(0)
     attention_reduce.end()
     small.arrive()
     for k in range(1, models):
@@ -1369,7 +1421,6 @@
         vmem((part, width), bf16), vmem((part, width), f32), vmem((part, 128), f32),
         vmem((models, rows, pair), bf16), vmem((rows, 128), bf16), vmem((part, width), f32), vmem((part, width), f32),
         vmem((part, width), f32), vmem((part, 128), f32), vmem((part, width), bf16), vmem((part, width), bf16),
-        vmem((models, part, hidden), bf16), vmem((models, part, hidden), f32),
         vmem((models,) + deep, bf16), vmem((models, 2, 2, strip, columns), bf16), vmem((models, 2, strip, columns), bf16),
         vmem((models, strip, columns), bf16), vmem((models, strip, columns), bf16), vmem((spots + models, 8, width), f32),
         pltpu.SemaphoreType.DMA((2,)), pltpu.SemaphoreType.DMA((net_count,)), pltpu.SemaphoreType.DMA((net_count,)),

time: 122 us -> 112 us (0.918)
  Pallas kernels: 121 us -> 111 us
    pallas_call x1, Pallas kernels: 118 us -> 108 us  [fast_body(): pl.pallas_call(functools.partial(whole_layer, plan, (part, width, pair, h...]
where the time goes in v4:
time: 112 us
  Pallas kernels  111 us (99%)
    pallas_call x1, Pallas kernels, fast_body(): pl.pallas_call(functools.partial(whole_layer, plan, (part, width, pair, h...  108 us
    pallas_call x1, Pallas kernels, fast_body(): pl.pallas_call(functools.partial(finish_outputs, (part, width, pair, hidd...  2.91 us

profile of v4, /device:TPU:0, one launch (start us, length us, event | category | flops | bytes accessed | tf_op | source)
XLA Modules:
  0.0 112.2 jit_solution(7430422316350077487)
XLA Ops:
  0.6 108.5 %layer.1 = (bf16[4,128,512]{2,1,0:T(8,128)(2,1)}, bf16[4,128,512]{2,1,0:T(8,128)(2,1)}, f32[64,1536]{1,0:T(8,128)}, f32[8,512]{1,0:T(8,128)}) custom-call(s32[4]{0:T(128)} %refs_0_.1, bf16[64,128]{1,0:T(8,128)(2,1)} %refs_1_.1, bf16[64,128]{1,0:T(8,128)(2,1)} %refs_2_.1, bf16[64,128]{1,0:T(8,128)(2,1)} %refs_3_.1, bf16[64,128]{1,0:T(8,128)(2,1)} %bitcast.13, ...), custom_call_target="tpu_custom_call" | custom-call | tf_op jit(solution)/shard_map/layer/pallas_call | solution.py:1429
  109.1 2.9 %outputs.1 = (bf16[4,1,128,512]{3,2,1,0:T(8,128)(2,1)}, bf16[4,1,128,512]{3,2,1,0:T(8,128)(2,1)}, f32[64,128]{1,0:T(8,128)}, f32[64,128]{1,0:T(8,128)}, f32[64,1...) custom-call(bf16[4,128,512]{2,1,0:T(8,128)(2,1)} %get-tuple-element., ...), custom_call_target="tpu_custom_call" | custom-call | tf_op jit(solution)/shard_map/outputs/pallas_call | solution.py:1442

commit v5 on v4

--- a/solution.py
+++ b/solution.py
@@ -540,6 +540,10 @@
 MESH = pl.DeviceIdType.MESH
 NEG = -1e30
 BACK_GROUP = 5
+FIRST = 32
+THROUGH_Y = 32
+TOP = 16
+TOP_LAST = 32
 GROUP = 5
 
 
@@ -715,6 +719,7 @@
         return flip_bits(az, k)
 
     x_peer, y_peer, c_peer = device(1 - ax, ay, ac, az), device(ax, 1 - ay, ac, az), device(ax, ay, 1 - ac, az)
+    xy_peer = device(1 - ax, 1 - ay, ac, az)
     z_peer = lambda k: device(ax, ay, ac, plane(k))
 
     barrier = pltpu.get_barrier_semaphore()
@@ -762,6 +767,7 @@
             copy(self.i, self.whole, self.whole, self.pairs[0][2]).wait_send()
 
     sent = []
+    kept = []
 
     def send(pairs, whole):
         group = Group(marks.take(1), pairs, whole).start()
@@ -786,14 +792,25 @@
             if k:
                 self.flight["z", k].arrive()
             here = self.block(k, ax, ay)
+            if self.rows == 0:
+                self.flight["corner", k] = send([(here, here, x_peer), (here, here, y_peer), (here, here, xy_peer)],
+                                                weights.at[pl.ds(0, 3), ax, ay, ac, :, self.cols])
+                return
             self.flight["side", k] = send([(here, here, x_peer), (here, here, y_peer)],
                                           weights.at[plane(k), :, ay, ac, :, self.cols])
 
         def to_corner(self, k):
+            if self.rows == 0:
+                return
             self.flight["side", k].arrive()
-            first = self.block(k, 1 - ax, ay, pl.ds(0, self.rows))
-            rest = self.block(k, ax, 1 - ay, pl.ds(self.rows, strip - self.rows))
-            self.flight["corner", k] = send([(first, first, y_peer), (rest, rest, x_peer)], self.block(k, ax, ay))
+            pairs = []
+            if self.rows > 0:
+                first = self.block(k, 1 - ax, ay, pl.ds(0, self.rows))
+                pairs.append((first, first, y_peer))
+            if self.rows < strip:
+                rest = self.block(k, ax, 1 - ay, pl.ds(self.rows, strip - self.rows))
+                pairs.append((rest, rest, x_peer))
+            self.flight["corner", k] = send(pairs, self.block(k, ax, ay))
 
         def to_core(self, k):
             self.flight["corner", k].arrive()
@@ -806,14 +823,18 @@
         def here(self, k):
             self.last(k).arrive()
 
-    first_gather = Gather(0, qkv, 32)
+    first_gather = Gather(0, qkv, FIRST)
     merge_gather = Gather(qkv, pair, 48)
-    feed_gather = Gather(4 * pair, 2 * hidden, 48)
+    feed_gather = Gather(4 * pair, 2 * hidden, THROUGH_Y)
 
     first_gather.to_planes()
     first_gather.to_sides(0)
     norm_copies = send([(norms.at[spot], norms.at[spot], at_spot((spot + step) % spots)) for step in range(1, spots)],
                        norms.at[pl.ds(0, spots - 1)])
+    merge_gather.to_planes()
+    feed_gather.to_planes()
+    merge_gather.to_sides(0)
+    feed_gather.to_sides(0)
 
     low, size = pool_bounds(plan, (part, 128), 0)
     for block in range(part // 128):
@@ -841,16 +862,13 @@
     rstd[...] = jnp.broadcast_to(scale, (part, 128))
     first_gather.to_sides(2)
     first_gather.to_sides(3)
-    merge_gather.to_planes()
-    feed_gather.to_planes()
     first_gather.to_core(0)
     first_gather.to_corner(1)
     for i, tile in enumerate(plan.tiles):
         logs[i, 0:tile[1]] = log_counts(plan, tile, spot, length)
     first_gather.to_corner(2)
     first_gather.to_corner(3)
-    merge_gather.to_sides(0)
-    feed_gather.to_sides(0)
+    feed_gather.to_corner(0)
     first_gather.to_core(1)
     norm_copies.arrive()
     gains = norms[0]
@@ -858,8 +876,6 @@
         gains = gains + norms[i]
     pre_gain, pre_shift, mid_gain, mid_shift = (gains[i:i + 1] for i in range(4))
     normed[...] = (scaled[...] * pre_gain + pre_shift).astype(bf16)
-    first_gather.to_core(2)
-    first_gather.to_core(3)
 
     is_first, is_last = spot == 0, spot == spots - 1
 
@@ -943,6 +959,8 @@
     total_rims = lambda: Rims(lambda rows: total_ext.at[rows, :], total_base)
 
     for k in range(models):
+        if k >= 1 and k + 1 < models:
+            first_gather.to_core(k + 1)
         first_gather.here(k)
         m = plane(k)
         rows = nn(normed[...], weight_cols(m, 0, qkv)).astype(bf16)
@@ -1014,7 +1032,6 @@
     for k in range(1, models):
         merge_gather.to_sides(k)
     attend(plan.outer, 0, 2, True)
-    feed_gather.to_corner(0)
     feed_gather.to_sides(1)
     attend(plan.outer, 2, models, True)
     for k in range(models):
@@ -1072,8 +1089,9 @@
     feed_gather.to_corner(2)
 
     class Reduce:
-        def __init__(self, col, count):
+        def __init__(self, col, count, top):
             self.cols = pl.ds(col, count)
+            self.top, self.bottom = pl.ds(0, top), pl.ds(top, strip - top)
             self.first = marks.take(4 * models)
 
         def core(self, k):
@@ -1083,7 +1101,7 @@
 
         def side(self, k):
             m = plane(k)
-            top, bottom = pl.ds(0, 32), pl.ds(32, 32)
+            top, bottom = self.top, self.bottom
             return Group(self.first + models + k,
                          [(got1.at[m, 1 - ax, :, top, self.cols], got2.at[m, :, top, self.cols], x_peer),
                           (got1.at[m, :, 1 - ay, bottom, self.cols], got2.at[m, :, bottom, self.cols], y_peer)],
@@ -1091,7 +1109,7 @@
 
         def corner(self, k):
             m = plane(k)
-            top, bottom = pl.ds(0, 32), pl.ds(32, 32)
+            top, bottom = self.top, self.bottom
             return Group(self.first + 2 * models + k,
                          [(got2.at[m, 1 - ay, top, self.cols], got3.at[m, top, self.cols], y_peer),
                           (got2.at[m, 1 - ax, bottom, self.cols], got3.at[m, bottom, self.cols], x_peer)],
@@ -1113,7 +1131,7 @@
         def to_corner(self, k):
             m = plane(k)
             self.side(k).arrive()
-            top, bottom = pl.ds(0, 32), pl.ds(32, 32)
+            top, bottom = self.top, self.bottom
             got2[m, :, top, self.cols] = got2[m, :, top, self.cols] + got1[m, ax, :, top, self.cols]
             got2[m, :, bottom, self.cols] = got2[m, :, bottom, self.cols] + got1[m, :, ay, bottom, self.cols]
             self.corner(k).start()
@@ -1121,7 +1139,7 @@
         def to_planes(self, k):
             m = plane(k)
             self.corner(k).arrive()
-            top, bottom = pl.ds(0, 32), pl.ds(32, 32)
+            top, bottom = self.top, self.bottom
             got3[m, top, self.cols] = got3[m, top, self.cols] + got2[m, ay, top, self.cols]
             got3[m, bottom, self.cols] = got3[m, bottom, self.cols] + got2[m, ax, bottom, self.cols]
 
@@ -1149,8 +1167,8 @@
             def _():
                 self.home(k).leave()
 
-    feed_reduce = Reduce(4 * pair, 2 * hidden)
-    attention_reduce = Reduce(0, 4 * pair)
+    feed_reduce = Reduce(4 * pair, 2 * hidden, TOP)
+    attention_reduce = Reduce(0, 4 * pair, TOP_LAST)
 
     def feed(k, carry):
         m = plane(k)
@@ -1182,9 +1200,12 @@
     result[...] = jnp.where(valid, after + acc[...], 0.0).astype(bf16)
     mid_grad = acc2[...]
 
-    def rows_home(source, target):
+    def rows_home(source, target, i):
         share = part // models
-        target[az] = source[pl.ds(pl.multiple_of(az * share, share), share), :]
+        mine = pltpu.make_async_copy(
+            source.at[pl.ds(pl.multiple_of(az * share, share), share), :], target.at[az], load_sem.at[i])
+        mine.start()
+        kept.append(mine)
         return send([(source.at[pl.ds(pl.multiple_of(plane(k) * share, share), share), :], target.at[az], z_peer(k))
                      for k in range(1, models)], target.at[pl.ds(0, models - 1)])
 
@@ -1232,7 +1253,7 @@
         total_ext[plan.at[lv] + NR:plan.at[lv] + NR + plan.own[lv], :] = sums[plan.pool_at[lv]:plan.pool_at[lv] + plan.own[lv]]
     total_ext[own_slot_rows, :] = sums[plan.pool_upper:plan.pool_upper + NR]
     total_rims().start()
-    rows_out = rows_home(result, out_rows)
+    rows_out = rows_home(result, out_rows, 2)
 
     feed_reduce.to_corner(0)
     feed_reduce.to_sides(2)
@@ -1333,36 +1354,37 @@
     lax.fori_loop(0, models, back, 0)
     normed_grad = acc[...]
     hat = scaled[...]
+    norm_sums = [jnp.sum(normed_grad * hat, axis=0, keepdims=True), jnp.sum(normed_grad, axis=0, keepdims=True)] + norm_sums
+    norm_got[0] = jnp.concatenate(norm_sums + [jnp.zeros((4, width), f32)], axis=0)
+    small = send([(norm_got.at[0], norm_got.at[k], z_peer(k)) for k in range(1, models)], norm_got.at[pl.ds(0, models - 1)])
     row_grads[...] = (residual[...] + norm_back(normed_grad, hat, rstd[:, 0:1], pre_gain)).astype(bf16)
-    grads_out = rows_home(row_grads, out_grads)
+    grads_out = rows_home(row_grads, out_grads, 3)
     attention_reduce.to_sides(0)
     attention_reduce.to_corner(1)
     attention_reduce.to_planes(3)
-    norm_sums = [jnp.sum(normed_grad * hat, axis=0, keepdims=True), jnp.sum(normed_grad, axis=0, keepdims=True)] + norm_sums
-    norm_got[0] = jnp.concatenate(norm_sums + [jnp.zeros((4, width), f32)], axis=0)
-    small = send([(norm_got.at[0], norm_got.at[step], at_spot((spot + step) % spots)) for step in range(1, spots)],
+    small.arrive()
+    norm_total = norm_got[0]
+    for k in range(1, models):
+        norm_total = norm_total + norm_got[k]
+    norm_got[models] = norm_total
+    small = send([(norm_got.at[models], norm_got.at[models + step], at_spot((spot + step) % spots)) for step in range(1, spots)],
                  norm_got.at[pl.ds(0, spots - 1)])
     attention_reduce.to_corner(0)
     attention_reduce.to_planes(1)
     feed_reduce.end()
     attention_reduce.to_planes(0)
     small.arrive()
-    norm_total = norm_got[0]
     for step in range(1, spots):
-        norm_total = norm_total + norm_got[step]
-    norm_got[spots] = norm_total
-    small = send([(norm_got.at[spots], norm_got.at[spots + k], z_peer(k)) for k in range(1, models)],
-                 norm_got.at[pl.ds(0, models - 1)])
+        norm_total = norm_total + norm_got[models + step]
+    norm_grads[...] = norm_total
     attention_reduce.end()
-    small.arrive()
-    for k in range(1, models):
-        norm_total = norm_total + norm_got[spots + k]
-    norm_grads[...] = norm_total
     rows_out.arrive()
     grads_out.arrive()
-    assert marks.used == net_count, marks.used
+    assert marks.used <= net_count, marks.used
     for group in sent:
         group.leave()
+    for c in kept:
+        c.wait()
 
     def drain(k, carry):
         pair_rims(k).done()
@@ -1377,10 +1399,13 @@
 
 
 def finish_outputs(dims, rows_ref, grads_ref, weights_ref, norms_ref,
-                   out_rows, out_grads, query, key, value, merge, up, down, *norm_outs):
+                   out_rows, out_grads, query, key, value, merge, up, down, *rest):
+    norm_outs, sem = rest[:4], rest[4]
     part, width, pair, hidden = dims
-    out_rows[...] = rows_ref[...].reshape(out_rows.shape)
-    out_grads[...] = grads_ref[...].reshape(out_grads.shape)
+    copies = [pltpu.make_async_copy(rows_ref, out_rows.at[:, 0], sem.at[0]),
+              pltpu.make_async_copy(grads_ref, out_grads.at[:, 0], sem.at[1])]
+    for c in copies:
+        c.start()
     strip = query.shape[0]
     query[...] = weights_ref[:, 0:pair]
     key[...] = weights_ref[:, pair:2 * pair]
@@ -1395,6 +1420,8 @@
         mine = jnp.where(owner == i, norms_ref[:, i * strip:(i + 1) * strip], mine)
     for i, out in enumerate(norm_outs):
         out[...] = mine[i].reshape(out.shape)
+    for c in copies:
+        c.wait()
 
 
 def fast_body(plan, incoming_embeddings, output_sensitivity, sequence_extents, asking_projector, lookup_projector,
@@ -1423,7 +1450,7 @@
         vmem((part, width), f32), vmem((part, 128), f32), vmem((part, width), bf16), vmem((part, width), bf16),
         vmem((models,) + deep, bf16), vmem((models, 2, 2, strip, columns), bf16), vmem((models, 2, strip, columns), bf16),
         vmem((models, strip, columns), bf16), vmem((models, strip, columns), bf16), vmem((spots + models, 8, width), f32),
-        pltpu.SemaphoreType.DMA((2,)), pltpu.SemaphoreType.DMA((net_count,)), pltpu.SemaphoreType.DMA((net_count,)),
+        pltpu.SemaphoreType.DMA((4,)), pltpu.SemaphoreType.DMA((net_count,)), pltpu.SemaphoreType.DMA((net_count,)),
     ]
     any_space, in_vmem = pl.BlockSpec(memory_space=pl.ANY), pl.BlockSpec(memory_space=pltpu.VMEM)
     out_rows, out_grads, weight_grads, norm_grads = pl.pallas_call(
@@ -1431,7 +1458,7 @@
         out_shape=(jax.ShapeDtypeStruct((seqs, share, width), bf16), jax.ShapeDtypeStruct((seqs, share, width), bf16),
                    jax.ShapeDtypeStruct((strip, columns), f32), jax.ShapeDtypeStruct((8, width), f32)),
         in_specs=[pl.BlockSpec(memory_space=pltpu.SMEM)] + [in_vmem] * 10 + [any_space] * 2,
-        out_specs=(in_vmem,) * 4,
+        out_specs=(any_space,) * 2 + (in_vmem,) * 2,
         scratch_shapes=scratch,
         compiler_params=pltpu.CompilerParams(collective_id=0, has_side_effects=True, vmem_limit_bytes=60 * 2 ** 20),
         name="layer",
@@ -1444,7 +1471,8 @@
         out_shape=(rows_type, rows_type, flat(strip, pair), flat(strip, pair), flat(strip, pair), flat(strip, pair),
                    flat(strip, hidden), flat(strip, hidden)) + (flat(1, strip),) * 4,
         in_specs=[in_vmem] * 4,
-        out_specs=(in_vmem,) * 12,
+        out_specs=(any_space,) * 2 + (in_vmem,) * 10,
+        scratch_shapes=[pltpu.SemaphoreType.DMA((2,))],
         name="outputs",
     )(out_rows, out_grads, weight_grads, norm_grads)
     rows_end, grads_end, query_grad, key_grad, value_grad, merge_t, up_grad, down_t = finished[:8]

time: 112 us -> 107 us (0.955); the launches traced: 112 us -> 105 us
  Pallas kernels: 111 us -> 104 us
    pallas_call x1, Pallas kernels: 108 us -> 101 us  [fast_body(): pl.pallas_call(functools.partial(whole_layer, plan, (part, width, pair, h...]
where the time goes in v5:
time: 107 us; the launch traced here: 105 us
  Pallas kernels  104 us (97%)
    pallas_call x1, Pallas kernels, fast_body(): pl.pallas_call(functools.partial(whole_layer, plan, (part, width, pair, h...  101 us
    pallas_call x1, Pallas kernels, fast_body(): pl.pallas_call(functools.partial(finish_outputs, (part, width, pair, hidd...  3.06 us

profile of v5, /device:TPU:0, one launch (start us, length us, event | category | flops | bytes accessed | tf_op | source)
XLA Modules:
  0.0 105.2 jit_solution(12967712516547862129)
XLA Ops:
  0.6 101.3 %layer.1 = (bf16[4,128,512]{2,1,0:T(8,128)(2,1)}, bf16[4,128,512]{2,1,0:T(8,128)(2,1)}, f32[64,1536]{1,0:T(8,128)}, f32[8,512]{1,0:T(8,128)}) custom-call(s32[4]{0:T(128)} %refs_0_.1, bf16[64,128]{1,0:T(8,128)(2,1)} %refs_1_.1, bf16[64,128]{1,0:T(8,128)(2,1)} %refs_2_.1, bf16[64,128]{1,0:T(8,128)(2,1)} %refs_3_.1, bf16[64,128]{1,0:T(8,128)(2,1)} %bitcast.13, ...), custom_call_target="tpu_custom_call" | custom-call | tf_op jit(solution)/shard_map/layer/pallas_call | solution.py:1456
  102.0 3.1 %outputs.1 = (bf16[4,1,128,512]{3,2,1,0:T(8,128)(2,1)}, bf16[4,1,128,512]{3,2,1,0:T(8,128)(2,1)}, f32[64,128]{1,0:T(8,128)}, f32[64,128]{1,0:T(8,128)}, f32[64,1...) custom-call(bf16[4,128,512]{2,1,0:T(8,128)(2,1)} %get-tuple-element., ...), custom_call_target="tpu_custom_call" | custom-call | tf_op jit(solution)/shard_map/outputs/pallas_call | solution.py:1469

commit v6 on v5

--- a/solution.py
+++ b/solution.py
@@ -824,7 +824,7 @@
             self.last(k).arrive()
 
     first_gather = Gather(0, qkv, FIRST)
-    merge_gather = Gather(qkv, pair, 48)
+    merge_gather = Gather(qkv, pair, 32)
     feed_gather = Gather(4 * pair, 2 * hidden, THROUGH_Y)
 
     first_gather.to_planes()
@@ -1063,6 +1063,11 @@
     feed_gather.to_corner(1)
     feed_gather.to_sides(3)
 
+    def clear(m, carry):
+        work[m, :, pair:qkv] = jnp.zeros((work.shape[1], 2 * pair), f32)
+        return carry
+
+    lax.fori_loop(0, models, clear, 0)
     residual[...] = tokens[...].astype(f32)
     for k in range(models):
         merge_gather.here(k)
@@ -1261,11 +1266,6 @@
 
     head_of_lane = lax.broadcasted_iota(jnp.int32, (1, 128), 1) // 2
 
-    def clear(m, carry):
-        work[m] = jnp.zeros(work.shape[1:], f32)
-        return carry
-
-    lax.fori_loop(0, models, clear, 0)
     normed_t = normed[...].T
     acc[...] = jnp.zeros(acc.shape, f32)
     qkv_shape = grads.shape[1:5] + (qkv,)
@@ -1321,19 +1321,16 @@
 
         @pl.when(step == 0)
         def _():
+            feed_reduce.to_planes(0)
             feed_reduce.to_corner(2)
-            feed_reduce.to_planes(0)
 
         @pl.when(step == 1)
         def _():
+            feed_reduce.to_planes(1)
             feed_reduce.to_corner(3)
-            feed_reduce.to_planes(1)
+            feed_reduce.to_planes(2)
 
         @pl.when(step == 2)
-        def _():
-            feed_reduce.to_planes(2)
-
-        @pl.when(step == 3)
         def _():
             feed_reduce.to_planes(3)
 

time: 107 us -> 106 us (level)
  no operation moved by 1% of the time
where the time goes in v6:
time: 106 us; the launch traced here: 105 us
  Pallas kernels  104 us (98%)
    pallas_call x1, Pallas kernels, fast_body(): pl.pallas_call(functools.partial(whole_layer, plan, (part, width, pair, h...  101 us
    pallas_call x1, Pallas kernels, fast_body(): pl.pallas_call(functools.partial(finish_outputs, (part, width, pair, hidd...  3.06 us

profile of v6, /device:TPU:0, one launch (start us, length us, event | category | flops | bytes accessed | tf_op | source)
XLA Modules:
  0.0 104.7 jit_solution(7268039481027629175)
XLA Ops:
  0.6 100.8 %layer.1 = (bf16[4,128,512]{2,1,0:T(8,128)(2,1)}, bf16[4,128,512]{2,1,0:T(8,128)(2,1)}, f32[64,1536]{1,0:T(8,128)}, f32[8,512]{1,0:T(8,128)}) custom-call(s32[4]{0:T(128)} %refs_0_.1, bf16[64,128]{1,0:T(8,128)(2,1)} %refs_1_.1, bf16[64,128]{1,0:T(8,128)(2,1)} %refs_2_.1, bf16[64,128]{1,0:T(8,128)(2,1)} %refs_3_.1, bf16[64,128]{1,0:T(8,128)(2,1)} %bitcast.13, ...), custom_call_target="tpu_custom_call" | custom-call | tf_op jit(solution)/shard_map/layer/pallas_call | solution.py:1453
  101.4 3.1 %outputs.1 = (bf16[4,1,128,512]{3,2,1,0:T(8,128)(2,1)}, bf16[4,1,128,512]{3,2,1,0:T(8,128)(2,1)}, f32[64,128]{1,0:T(8,128)}, f32[64,128]{1,0:T(8,128)}, f32[64,1...) custom-call(bf16[4,128,512]{2,1,0:T(8,128)(2,1)} %get-tuple-element., ...), custom_call_target="tpu_custom_call" | custom-call | tf_op jit(solution)/shard_map/outputs/pallas_call | solution.py:1466
